TPU v7x, 32 devices: a whole 2x2x4 slice. The times are simulated.
32 devices in a mesh: mem: 4 (over y, core), patch: 8 (over z, x).
Axes of the slice: x: 2, y: 2, z: 4, core: 2. Of those that a mesh axis runs over, the one named last changes fastest.
Arguments:
- mesh_latent: bfloat16 [4, 4096, 512], P('mem', 'patch'), may hold values from -6 to 6
- edge_latent: bfloat16 [8192, 512], P('patch'), may hold values from -6 to 6
- grid_edge_latent: bfloat16 [12288, 512], P('patch'), may hold values from -6 to 6
- edge_inner: bfloat16 [1536, 512], replicated, may hold values from -0.15625 to 0.15625
- edge_outer: bfloat16 [512, 512], replicated, may hold values from -0.25 to 0.25
- node_inner: bfloat16 [1024, 512], replicated, may hold values from -0.1875 to 0.1875
- node_outer: bfloat16 [512, 512], replicated, may hold values from -0.25 to 0.25
- grid_inner: bfloat16 [1024, 512], replicated, may hold values from -0.1875 to 0.1875
- grid_outer: bfloat16 [512, 512], replicated, may hold values from -0.25 to 0.25
- out_weight: bfloat16 [87, 512], replicated, may hold values from -0.25 to 0.25
- prior_state: float32 [87, 4096], P(None, 'patch'), may hold values from -6 to 6
- target: float32 [87, 4096], P(None, 'patch'), may hold values from -6 to 6
- channel_weight: float32 [87], replicated, may hold values from 0.2 to 2
- area_weight: float32 [4096], P('patch'), may hold values from 0.2 to 2
- send_rows: int32 [8, 2, 96], P('patch'), may hold values from 0 to 511
- edge_senders: int32 [8192], P('patch'), may hold values from 0 to 703, as said below
- edge_receivers: int32 [8192], P('patch'), may hold values from 0 to 511
- edge_count: int32 [8], P('patch'), may hold values from 256 to 1024, as said below
- grid_senders: int32 [12288], P('patch'), may hold values from 0 to 703, as said below
Outputs:
- crps_gradient: float32 [4, 87, 4096], P('mem', None, 'patch')
Inputs may be any that keep to these rules, and one draw needn't show every extreme that they name: `edge_senders`: values below 512 name a row of the band itself, values from 512 to 607 a row received from the previous band, larger values a row received from the next band; the first band names none of the second kind and the last band none of the third. `grid_senders`: as for edge_senders: own rows, rows from the previous band, rows from the next band; the first and last bands name only bands that exist. The live slots of a band are its first edge_count slots; some band has all 1024 slots live.
All inputs are finite; a program needn't handle non-finite values.
Results may differ from a plain program's by a relative error of at most 0.023.
Values may be sent and summed in bfloat16 or wider, within the bound.
No kernel may reach another device: no remote copies, remote signals or barrier semaphores. Data moves between devices by JAX's collectives and lax.ppermute only.
A program may use at most 64 MiB of HBM per device.

v0:
```python
import jax
import jax.numpy as jnp
from jax import lax
from jax.sharding import PartitionSpec as P

epsilon = 1e-05
smooth = 0.25


def shifted(block, axis, distance):
    devices = range(lax.axis_size(axis))
    route = [(i - distance, i) for i in devices if i - distance in devices]
    return lax.ppermute(block, axis, route)


def layer_norm(values):
    average = jnp.mean(values, -1, keepdims=True)
    centred = values - average
    spread = jnp.mean(centred * centred, -1, keepdims=True)
    return centred / jnp.sqrt(spread + epsilon)


def network(inputs, inner_weight, outer_weight):
    inner = jax.nn.silu(jnp.dot(inputs, inner_weight, preferred_element_type=jnp.float32)).astype(
        jnp.bfloat16
    )
    return layer_norm(jnp.dot(inner, outer_weight, preferred_element_type=jnp.float32))


def smooth_slope(values):
    return values / jnp.sqrt(values * values + smooth * smooth)


def selector(rows, length):
    return (rows[:, None] == jnp.arange(length, dtype=jnp.int32)[None, :]).astype(jnp.bfloat16)


def pick_rows(table, rows):
    return jnp.dot(
        selector(rows, table.shape[0]), table, preferred_element_type=jnp.float32
    ).astype(jnp.bfloat16)


def add_into(message, receivers, nodes):
    placing = (jnp.arange(nodes, dtype=jnp.int32)[:, None] == receivers[None, :]).astype(
        jnp.float32
    )
    return jnp.dot(
        placing, message, preferred_element_type=jnp.float32, precision=lax.Precision.HIGHEST
    )


def extend(latent, sends):
    lower = shifted(pick_rows(latent, sends[0]), "patch", 1)
    upper = shifted(pick_rows(latent, sends[1]), "patch", -1)
    return jnp.concatenate([latent, lower, upper], 0)


def per_device(
    mesh_latent,
    edge_latent,
    grid_edge_latent,
    edge_inner,
    edge_outer,
    node_inner,
    node_outer,
    grid_inner,
    grid_outer,
    out_weight,
    prior_state,
    target,
    channel_weight,
    area_weight,
    send_rows,
    edge_senders,
    edge_receivers,
    edge_count,
    grid_senders,
):
    latent = mesh_latent[0]
    sends = send_rows[0]
    live_count = edge_count[0]
    nodes = latent.shape[0]
    edges = edge_senders.shape[0]
    width = latent.shape[1]
    extended = extend(latent, sends)
    inputs = jnp.concatenate(
        [pick_rows(extended, edge_senders), pick_rows(latent, edge_receivers), edge_latent], 1
    )
    message = network(inputs, edge_inner, edge_outer)
    live_slots = jnp.arange(edges, dtype=jnp.int32) < live_count
    message = jnp.where(live_slots[:, None], message, 0.0)
    summed = add_into(message, edge_receivers, nodes)
    node_inputs = jnp.concatenate([latent, summed.astype(jnp.bfloat16)], 1)
    updated = (latent.astype(jnp.float32) + network(node_inputs, node_inner, node_outer)).astype(
        jnp.bfloat16
    )
    extended_new = extend(updated, sends)
    grid_inputs = jnp.concatenate([pick_rows(extended_new, grid_senders), grid_edge_latent], 1)
    grid_message = network(grid_inputs, grid_inner, grid_outer)
    grid_sum = grid_message.reshape(-1, 3, width).sum(1).astype(jnp.bfloat16)
    output = lax.dot_general(
        out_weight, grid_sum, (((1,), (1,)), ((), ())), preferred_element_type=jnp.float32
    )
    difference = prior_state + output - target
    everyone = lax.all_gather(
        difference[None].astype(jnp.bfloat16), "mem", axis=0, tiled=True
    ).astype(jnp.float32)
    pairwise = jnp.sum(smooth_slope(difference[None] - everyone), 0)
    result = smooth_slope(difference) - pairwise / (everyone.shape[0] - 1)
    gradient = result * channel_weight[:, None] * area_weight[None, :]
    return gradient[None]


def solution(mesh):
    in_specs = (
        P("mem", "patch", None),
        P("patch", None),
        P("patch", None),
        P(),
        P(),
        P(),
        P(),
        P(),
        P(),
        P(),
        P(None, "patch"),
        P(None, "patch"),
        P(),
        P("patch"),
        P("patch", None, None),
        P("patch"),
        P("patch"),
        P("patch"),
        P("patch"),
    )
    out_specs = P("mem", None, "patch")
    return jax.shard_map(
        per_device, mesh=mesh, in_specs=in_specs, out_specs=out_specs, check_vma=False
    )
```

profile of v0, /device:TPU:17, one launch (start us, length us, event | category | flops | bytes accessed | tf_op | source)
XLA Modules:
  0.0 80.5 jit_solution(3780969010829671242)
XLA Ops:
  0.0 0.8 %slice_bitcast_fusion.1 = (s32[96]{0:T(128)S(1)}, s32[96]{0:T(128)S(1)}) fusion(s32[1,2,96]{2,1,0:T(2,128)} %param.33), kind=kLoop, calls=%fused_computation.92 | loop fusion | bytes 1536 | tf_op jit(solution)/shard_map/eq | solution.py:35
  0.8 1.4 %convolution_convert_fusion.2 = bf16[96,512]{1,0:T(8,128)(2,1)S(1)} fusion(bf16[1,512,512]{2,1,0:T(8,128)(2,1)} %param.19, s32[96]{0:T(128)S(1)} %get-tuple-element.6), kind=kOutput, calls=%fused_computation.38 | convolution fusion | flops 50429952 | bytes 622976 | tf_op jit(solution)/shard_map/dot_general | solution.py:39
  2.2 3.0 %collective-permute-start.1 = (bf16[96,512]{1,0:T(8,128)(2,1)S(1)}, bf16[96,512]{1,0:T(8,128)(2,1)S(1)}, u32[]{:S(2)}, u32[]{:S(2)}) collective-permute-start(bf16[96,512]{1,0:T(8,128)(2,1)S(1)} %convolution_convert_fusion.2), channel_id=1, source_target_pairs={{1,0},{2,1},{3,2},{4,3},{5,4},{6,5},{7,6},{9,8},{10,9},{11,10},{12... | collective-permute-start | bytes 294920 | tf_op jit(solution)/shard_map/ppermute | solution.py:13
  5.2 1.3 %convolution_convert_fusion.3 = bf16[96,512]{1,0:T(8,128)(2,1)S(1)} fusion(bf16[1,512,512]{2,1,0:T(8,128)(2,1)} %param.19, s32[96]{0:T(128)S(1)} %get-tuple-element.5), kind=kOutput, calls=%fused_computation.39 | convolution fusion | flops 50429952 | bytes 622976 | tf_op jit(solution)/shard_map/dot_general | solution.py:39
  6.5 2.3 %collective-permute-start = (bf16[96,512]{1,0:T(8,128)(2,1)S(1)}, bf16[96,512]{1,0:T(8,128)(2,1)S(1)}, u32[]{:S(2)}, u32[]{:S(2)}) collective-permute-start(bf16[96,512]{1,0:T(8,128)(2,1)S(1)} %convolution_convert_fusion.3), channel_id=1, source_target_pairs={{0,1},{1,2},{2,3},{3,4},{4,5},{5,6},{6,7},{8,9},{9,10},{10,11},{11... | collective-permute-start | bytes 294920 | tf_op jit(solution)/shard_map/ppermute | solution.py:13
  8.8 1.3 %copy.31 = bf16[1,512,512]{1,2,0:T(8,128)(2,1)S(1)} copy(bf16[1,512,512]{2,1,0:T(8,128)(2,1)} %param.19) | data formatting | bytes 1048576 | tf_op args[0]
  10.7 2.3 %copy.34 = bf16[1024,512]{0,1:T(8,128)(2,1)} copy(bf16[1024,512]{1,0:T(8,128)(2,1)} %param.20) | data formatting | bytes 2097152 | tf_op args[1]
  13.0 1.9 %fusion.22 = bf16[1024,512]{0,1:T(8,128)(2,1)} fusion(s32[1024]{0:T(1024)S(1)} %copy-done.15, bf16[1,512,512]{2,1,0:T(8,128)(2,1)S(1)} %copy-done.2), kind=kOutput, calls=%fused_computation.29 | convolution fusion | flops 537919488 | bytes 1576960 | tf_op jit(solution)/shard_map/dot_general | solution.py:39
  15.2 2.1 %fusion.23 = bf16[1024,512]{0,1:T(8,128)(2,1)} fusion(s32[1024]{0:T(1024)S(1)} %copy-done.14, bf16[96,512]{0,1:T(8,128)(2,1)S(1)} %copy.33, bf16[96,512]{0,1:T(8,128)(2,1)S(1)} %copy.32, bf16[512,512]{0,1:T(8,128)(2,1)S(1)} %bitcast.37), kind=kOutput, calls=%fused_computation.30 | convolution fusion | flops 741605376 | bytes 1773568 | tf_op jit(solution)/shard_map/dot_general | solution.py:39
  17.3 5.8 %fusion.88 = (f32[1024]{0:T(1024)S(1)}, f32[1024,512]{0,1:T(8,128)}) fusion(bf16[512,512]{1,0:T(8,128)(2,1)S(1)} %copy-done.11, bf16[1536,512]{1,0:T(8,128)(2,1)S(1)} %copy-done, bf16[1024,512]{0,1:T(8,128)(2,1)} %copy.34, bf16[1024,512]{0,1:T(8,128)(2,1)} %fusion.22, bf16[1024,512]{0,1:T(8,128)(2,1)} %fusion.23), kind=kOutput, calls=%fused_computation.102 | convolution fusion | flops 2160065536 | bytes 7344128 | tf_op jit(solution)/shard_map/dot_general | solution.py:27
  23.2 2.0 %multiply_reduce_fusion.1 = f32[1024]{0:T(1024)S(1)} fusion(f32[1024,512]{0,1:T(8,128)} %get-tuple-element.8, f32[1024]{0:T(1024)S(1)} %broadcast_multiply_fusion.1), kind=kLoop, calls=%fused_computation.22 | loop fusion | flops 1571840 | bytes 2105344 | tf_op jit(solution)/shard_map/reduce_sum | solution.py:19
  25.2 0.2 copy-done.3
  25.4 3.0 %fusion.27 = bf16[512,512]{0,1:T(8,128)(2,1)} fusion(f32[1024,512]{0,1:T(8,128)S(1)} %copy-done.3, f32[1024]{0:T(1024)S(1)} %add_sqrt_fusion.1, f32[1024]{0:T(1024)S(1)} %broadcast_multiply_fusion.1, s32[1024]{0:T(1024)S(1)} %copy-done.15, pred[1024]{0:T(1024)(128)(4,1)S(1)} %iota_compare_fusion.22), kind=kOutput, calls=%fused_computation.32 | convolution fusion | flops 3223584768 | bytes 2634752 | tf_op jit(solution)/shard_map/dot_general | solution.py:48
  28.3 3.5 %fusion.91 = (f32[512]{0:T(512)S(1)}, f32[512,512]{1,0:T(8,128)}) fusion(bf16[512,512]{1,0:T(8,128)(2,1)S(1)} %copy-done.12, bf16[1024,512]{1,0:T(8,128)(2,1)} %param.24, bf16[512,512]{0,1:T(8,128)(2,1)} %fusion.27, bf16[512,512]{0,1:T(8,128)(2,1)S(1)} %bitcast.38), kind=kOutput, calls=%fused_computation.103 | convolution fusion | flops 808975872 | bytes 3672064 | tf_op jit(solution)/shard_map/dot_general | solution.py:27
  31.9 1.6 %copy.35 = f32[512,512]{0,1:T(8,128)S(1)} copy(f32[512,512]{1,0:T(8,128)} %get-tuple-element.10) | data formatting | bytes 2097152 | tf_op jit(solution)/shard_map/dot_general | solution.py:27
  33.6 1.2 %add_convert_fusion = bf16[512,512]{0,1:T(8,128)(2,1)S(1)} fusion(f32[512,512]{0,1:T(8,128)S(1)} %copy.35, f32[512]{0:T(512)S(1)} %add_sqrt_fusion.2, f32[512]{0:T(512)S(1)} %broadcast_multiply_fusion.2, bf16[1,512,512]{1,2,0:T(8,128)(2,1)} %copy-done.4), kind=kLoop, calls=%fused_computation.44 | loop fusion | flops 1310720 | bytes 2101248 | tf_op jit(solution)/shard_map/convert_element_type | solution.py:95
  34.9 0.3 convolution_convert_fusion.1
  35.2 4.2 %collective-permute-start.2 = (bf16[96,512]{1,0:T(8,128)(2,1)S(1)}, bf16[96,512]{1,0:T(8,128)(2,1)S(1)}, u32[]{:S(2)}, u32[]{:S(2)}) collective-permute-start(bf16[96,512]{1,0:T(8,128)(2,1)S(1)} %convolution_convert_fusion.1), channel_id=1, source_target_pairs={{0,1},{1,2},{2,3},{3,4},{4,5},{5,6},{6,7},{8,9},{9,10},{10,11},{11... | collective-permute-start | bytes 294920 | tf_op jit(solution)/shard_map/ppermute | solution.py:13
  39.3 0.3 convolution_convert_fusion
  39.6 2.3 %collective-permute-start.3 = (bf16[96,512]{1,0:T(8,128)(2,1)S(1)}, bf16[96,512]{1,0:T(8,128)(2,1)S(1)}, u32[]{:S(2)}, u32[]{:S(2)}) collective-permute-start(bf16[96,512]{1,0:T(8,128)(2,1)S(1)} %convolution_convert_fusion), channel_id=1, source_target_pairs={{1,0},{2,1},{3,2},{4,3},{5,4},{6,5},{7,6},{9,8},{10,9},{11,10},{12... | collective-permute-start | bytes 294920 | tf_op jit(solution)/shard_map/ppermute | solution.py:13
  42.0 2.6 %copy.38 = bf16[1536,512]{0,1:T(8,128)(2,1)} copy(bf16[1536,512]{1,0:T(8,128)(2,1)} %param.21) | data formatting | bytes 3145728 | tf_op args[2]
  44.7 0.3 collective-permute-done.3
  45.1 2.7 %fusion.12 = bf16[1536,512]{0,1:T(8,128)(2,1)} fusion(s32[1536]{0:T(1024)S(1)} %copy-done.13, bf16[96,512]{0,1:T(8,128)(2,1)S(1)} %copy.37, bf16[96,512]{0,1:T(8,128)(2,1)S(1)} %copy.36, bf16[512,512]{0,1:T(8,128)(2,1)S(1)} %add_convert_fusion), kind=kOutput, calls=%fused_computation.16 | convolution fusion | flops 1111326720 | bytes 2299904 | tf_op jit(solution)/shard_map/dot_general | solution.py:39
  47.9 6.6 %fusion.94 = (f32[1536]{0:T(1024)S(1)}, f32[1536,512]{1,0:T(8,128)}) fusion(bf16[512,512]{1,0:T(8,128)(2,1)} %param.27, bf16[1024,512]{1,0:T(8,128)(2,1)S(1)} %copy-done.10, bf16[1536,512]{0,1:T(8,128)(2,1)} %copy.38, bf16[1536,512]{0,1:T(8,128)(2,1)} %fusion.12), kind=kOutput, calls=%fused_computation.104 | convolution fusion | flops 2426927616 | bytes 7870464 | tf_op jit(solution)/shard_map/dot_general | solution.py:27
  54.5 2.6 %multiply_reduce_fusion = f32[1536]{0:T(1024)S(1)} fusion(f32[1536,512]{1,0:T(8,128)} %get-tuple-element.12, f32[1536]{0:T(1024)S(1)} %broadcast_multiply_fusion), kind=kLoop, calls=%fused_computation.12 | loop fusion | flops 2357760 | bytes 3158016 | tf_op jit(solution)/shard_map/reduce_sum | solution.py:19
  57.1 0.2 copy-done.1
  57.3 2.2 %subtract_divide_fusion = f32[1536,512]{1,0:T(8,128)} fusion(f32[1536,512]{1,0:T(8,128)S(1)} %copy-done.1, f32[1536]{0:T(1024)S(1)} %add_sqrt_fusion, f32[1536]{0:T(1024)S(1)} %broadcast_multiply_fusion), kind=kLoop, calls=%fused_computation.17 | loop fusion | flops 1572864 | bytes 6303744 | tf_op jit(solution)/shard_map/div | solution.py:20
  59.5 5.8 %reshape.57 = f32[512,3,512]{2,1,0:T(4,128)} reshape(f32[1536,512]{1,0:T(8,128)} %subtract_divide_fusion) | data formatting | bytes 6291456 | tf_op jit(solution)/shard_map/reshape | solution.py:101
  65.3 4.8 %reduce_sum.78 = bf16[512,512]{1,0:T(8,128)(2,1)S(1)} reduce(f32[512,3,512]{2,1,0:T(4,128)} %reshape.57, f32[]{:T(128)} %constant.12.clone.1), dimensions={1}, to_apply=%region_6.7 | reduce | flops 524288 | bytes 3670020 | tf_op jit(solution)/shard_map/reduce_sum | solution.py:101
  70.2 0.3 fusion.31
  70.5 8.8 %all-gather.1 = bf16[4,87,512]{2,1,0:T(8,128)(2,1)S(1)} all-gather(bf16[1,87,512]{2,1,0:T(8,128)(2,1)S(1)} %convert_bitcast_fusion), channel_id=2, replica_groups=mesh['mem'=4,'patch'=8] {'mem'}, dimensions={0}, use_global_device_ids=true | all-gather | bytes 445440 | tf_op jit(solution)/shard_map/all_gather | solution.py:106
  79.6 0.9 %copy.39 = f32[1,87,512]{2,0,1:T(1,128)} copy(f32[1,87,512]{2,1,0:T(8,128)S(1)} %multiply_bitcast_fusion) | data formatting | bytes 356352 | tf_op jit(solution)/shard_map/broadcast_in_dim | solution.py:112
  (48 shorter events, 1.0 us)
Async XLA Ops:
  0.0 17.3 %copy-start = (bf16[1536,512]{1,0:T(8,128)(2,1)S(1)}, bf16[1536,512]{1,0:T(8,128)(2,1)}, u32[]{:S(2)}) copy-start(bf16[1536,512]{1,0:T(8,128)(2,1)} %param.22) | copy-start | bytes 4718596
  0.8 12.2 %copy-start.2 = (bf16[1,512,512]{2,1,0:T(8,128)(2,1)S(1)}, bf16[1,512,512]{2,1,0:T(8,128)(2,1)}, u32[]{:S(2)}) copy-start(bf16[1,512,512]{2,1,0:T(8,128)(2,1)} %param.19) | copy-start | bytes 1572868
  0.8 12.2 %copy-start.15 = (s32[1024]{0:T(1024)S(1)}, s32[1024]{0:T(1024)}, u32[]{:S(2)}) copy-start(s32[1024]{0:T(1024)} %param.35) | copy-start | bytes 12292
  2.2 12.7 %collective-permute-start.1 = (bf16[96,512]{1,0:T(8,128)(2,1)S(1)}, bf16[96,512]{1,0:T(8,128)(2,1)S(1)}, u32[]{:S(2)}, u32[]{:S(2)}) collective-permute-start(bf16[96,512]{1,0:T(8,128)(2,1)S(1)} %convolution_convert_fusion.2), channel_id=1, source_target_pairs={{1,0},{2,1},{3,2},{4,3},{5,4},{6,5},{7,6},{9,8},{10,9},{11,10},{12... | collective-permute-start | bytes 294920 | tf_op jit(solution)/shard_map/ppermute | solution.py:13
  6.5 8.5 %collective-permute-start = (bf16[96,512]{1,0:T(8,128)(2,1)S(1)}, bf16[96,512]{1,0:T(8,128)(2,1)S(1)}, u32[]{:S(2)}, u32[]{:S(2)}) collective-permute-start(bf16[96,512]{1,0:T(8,128)(2,1)S(1)} %convolution_convert_fusion.3), channel_id=1, source_target_pairs={{0,1},{1,2},{2,3},{3,4},{4,5},{5,6},{6,7},{8,9},{9,10},{10,11},{11... | collective-permute-start | bytes 294920 | tf_op jit(solution)/shard_map/ppermute | solution.py:13
  10.0 18.3 %copy-start.4 = (bf16[1,512,512]{1,2,0:T(8,128)(2,1)}, bf16[1,512,512]{1,2,0:T(8,128)(2,1)S(1)}, u32[]{:S(2)}) copy-start(bf16[1,512,512]{1,2,0:T(8,128)(2,1)S(1)} %copy.31) | copy-start | bytes 1572868
  13.0 2.2 %copy-start.14 = (s32[1024]{0:T(1024)S(1)}, s32[1024]{0:T(1024)}, u32[]{:S(2)}) copy-start(s32[1024]{0:T(1024)} %param.34) | copy-start | bytes 12292
  15.2 2.1 %copy-start.11 = (bf16[512,512]{1,0:T(8,128)(2,1)S(1)}, bf16[512,512]{1,0:T(8,128)(2,1)}, u32[]{:S(2)}) copy-start(bf16[512,512]{1,0:T(8,128)(2,1)} %param.23) | copy-start | bytes 1572868
  23.2 2.2 %copy-start.3 = (f32[1024,512]{0,1:T(8,128)S(1)}, f32[1024,512]{0,1:T(8,128)}, u32[]{:S(2)}) copy-start(f32[1024,512]{0,1:T(8,128)} %get-tuple-element.8) | copy-start | bytes 6291460
  25.4 3.0 %copy-start.12 = (bf16[512,512]{1,0:T(8,128)(2,1)S(1)}, bf16[512,512]{1,0:T(8,128)(2,1)}, u32[]{:S(2)}) copy-start(bf16[512,512]{1,0:T(8,128)(2,1)} %param.25) | copy-start | bytes 1572868
  35.2 9.9 %copy-start.13 = (s32[1536]{0:T(1024)S(1)}, s32[1536]{0:T(1024)}, u32[]{:S(2)}) copy-start(s32[1536]{0:T(1024)} %param.37) | copy-start | bytes 18436
  35.2 9.4 %collective-permute-start.2 = (bf16[96,512]{1,0:T(8,128)(2,1)S(1)}, bf16[96,512]{1,0:T(8,128)(2,1)S(1)}, u32[]{:S(2)}, u32[]{:S(2)}) collective-permute-start(bf16[96,512]{1,0:T(8,128)(2,1)S(1)} %convolution_convert_fusion.1), channel_id=1, source_target_pairs={{0,1},{1,2},{2,3},{3,4},{4,5},{5,6},{6,7},{8,9},{9,10},{10,11},{11... | collective-permute-start | bytes 294920 | tf_op jit(solution)/shard_map/ppermute | solution.py:13
  39.6 5.4 %collective-permute-start.3 = (bf16[96,512]{1,0:T(8,128)(2,1)S(1)}, bf16[96,512]{1,0:T(8,128)(2,1)S(1)}, u32[]{:S(2)}, u32[]{:S(2)}) collective-permute-start(bf16[96,512]{1,0:T(8,128)(2,1)S(1)} %convolution_convert_fusion), channel_id=1, source_target_pairs={{1,0},{2,1},{3,2},{4,3},{5,4},{6,5},{7,6},{9,8},{10,9},{11,10},{12... | collective-permute-start | bytes 294920 | tf_op jit(solution)/shard_map/ppermute | solution.py:13
  45.1 2.8 %copy-start.10 = (bf16[1024,512]{1,0:T(8,128)(2,1)S(1)}, bf16[1024,512]{1,0:T(8,128)(2,1)}, u32[]{:S(2)}) copy-start(bf16[1024,512]{1,0:T(8,128)(2,1)} %param.26) | copy-start | bytes 3145732
  54.5 2.8 %copy-start.1 = (f32[1536,512]{1,0:T(8,128)S(1)}, f32[1536,512]{1,0:T(8,128)}, u32[]{:S(2)}) copy-start(f32[1536,512]{1,0:T(8,128)} %get-tuple-element.12) | copy-start | bytes 9437188
  65.3 4.8 %copy-start.5 = (f32[87,512]{1,0:T(8,128)S(1)}, f32[87,512]{1,0:T(8,128)}, u32[]{:S(2)}) copy-start(f32[87,512]{1,0:T(8,128)} %param.30) | copy-start | bytes 534532
  65.3 4.9 %copy-start.6 = (f32[87,512]{1,0:T(8,128)S(1)}, f32[87,512]{1,0:T(8,128)}, u32[]{:S(2)}) copy-start(f32[87,512]{1,0:T(8,128)} %param.29) | copy-start | bytes 534532
  65.3 4.9 %copy-start.7 = (bf16[87,512]{1,0:T(8,128)(2,1)S(1)}, bf16[87,512]{1,0:T(8,128)(2,1)}, u32[]{:S(2)}) copy-start(bf16[87,512]{1,0:T(8,128)(2,1)} %param.28) | copy-start | bytes 267268
  70.2 9.3 %copy-start.8 = (f32[512]{0:T(512)S(1)}, f32[512]{0:T(512)}, u32[]{:S(2)}) copy-start(f32[512]{0:T(512)} %param.32) | copy-start | bytes 6148
  70.2 9.3 %copy-start.9 = (f32[87]{0:T(128)S(1)}, f32[87]{0:T(128)}, u32[]{:S(2)}) copy-start(f32[87]{0:T(128)} %param.31) | copy-start | bytes 1048
where the time goes:
time: 82.1 us; the launch traced here: 80.5 us
  matrix products  29.3 us (36%)
  local copies, waits for them, and re-layouts  16.1 us (20%)
  other arithmetic  13.3 us (16%)
  starting transfers between devices  11.8 us (14%)
  blocking collectives  8.82 us (11%)
  between operations  0.9 us (1%)
    dot_general x3, matrix products, network(): jnp.dot(inner, outer_weight, preferred_element_type=jnp.float32)  16 us
    ppermute x4, starting transfers between devices, shifted(): return lax.ppermute(block, axis, route)  11.8 us
    dot_general x7, matrix products, pick_rows(): jnp.dot(selector(rows, table.shape[0]), table, preferred_element_type=jnp...  10 us
    all_gather x1, blocking collectives, per_device(): lax.all_gather(difference[None].astype(jnp.bfloat16), 'mem', axis=0, tile...  8.82 us
    unnamed x35, local copies, waits for them, and re-layouts  6.64 us
    reshape x1, local copies, waits for them, and re-layouts, per_device(): grid_sum = grid_message.reshape(-1, 3, width).sum(1).astype(jnp.bfloat16)  5.81 us
    reduce_sum x1, other arithmetic, per_device(): grid_sum = grid_message.reshape(-1, 3, width).sum(1).astype(jnp.bfloat16)  4.83 us
    reduce_sum x3, other arithmetic, layer_norm(): spread = jnp.mean(centred * centred, -1, keepdims=True)  4.75 us
  transfers between devices with their start and end apart: 4, of which 1 were waited for; matrix products, arithmetic and copies ran while one was open for 12% of the time, Pallas kernels for 0%

commit v1 on v0

v1 whole, which is shorter than its diff:
```python
import jax
import jax.numpy as jnp
from jax import lax
from jax.experimental import pallas as pl
from jax.experimental.pallas import tpu as pltpu
from jax.sharding import PartitionSpec as P

epsilon = 1e-05
smooth = 0.25
LANES = 128
VMEM = pltpu.VMEM
f32 = jnp.float32
bf16 = jnp.bfloat16


def dot(a, b):
    return jnp.dot(a, b, preferred_element_type=f32)


def silu(v):
    half = 0.5 * v
    return half + half * jnp.tanh(half)


def normalised(u):
    average = jnp.mean(u, -1, keepdims=True)
    centred = u - average
    spread = jnp.mean(centred * centred, -1, keepdims=True)
    return centred * lax.rsqrt(spread + epsilon)


def column(row):
    return jnp.transpose(jnp.broadcast_to(row, (8, row.shape[1])))[:, :1]


def columns(ref, first, count):
    parts = [
        column(ref[:, first + at : first + at + LANES]) for at in range(0, count, LANES)
    ]
    return parts[0] if len(parts) == 1 else jnp.concatenate(parts, 0)


def chosen(index, width):
    lanes = lax.broadcasted_iota(jnp.int32, (index.shape[0], width), 1)
    return jnp.where(index == lanes, 1.0, 0.0).astype(bf16)


def placed(index, height):
    rows = lax.broadcasted_iota(jnp.int32, (height, index.shape[1]), 0)
    return jnp.where(index == rows, 1.0, 0.0).astype(bf16)


def halo_slots(index, nodes, halo, odd):
    at = index - nodes
    turned = jnp.where(at < halo, at + halo, at - halo)
    return jnp.where(at < 0, -1, jnp.where(odd, at, turned))


def send_columns(sends_ref, odd):
    halo = sends_ref.shape[1]
    onward, back = sends_ref[0:1, :], sends_ref[1:2, :]
    pair = jnp.where(odd, back, onward)
    cross = jnp.where(odd, onward, back)
    return column(pair), column(cross), halo


def select_kernel(odd_ref, sends_ref, table_ref, pair_ref, cross_ref):
    odd = odd_ref[0] == 1
    pair, cross, _ = send_columns(sends_ref, odd)
    nodes = table_ref.shape[0]
    pair_ref[...] = dot(chosen(pair, nodes), table_ref[...]).astype(bf16)
    cross_ref[...] = dot(chosen(cross, nodes), table_ref[...]).astype(bf16)


def edge_own_kernel(block, senders_ref, receivers_ref, table_ref, edge_ref, inner_ref, pre_ref, sent_ref, got_ref):
    nodes, width = table_ref.shape
    sent_ref[...] = dot(table_ref[...], inner_ref[0:width, :]).astype(bf16)
    got_ref[...] = dot(table_ref[...], inner_ref[width : 2 * width, :]).astype(bf16)
    for at in range(0, edge_ref.shape[0], block):
        rows = slice(at, at + block)
        total = dot(edge_ref[rows, :], inner_ref[2 * width :, :])
        total += dot(chosen(columns(senders_ref, at, block), nodes), sent_ref[...])
        total += dot(chosen(columns(receivers_ref, at, block), nodes), got_ref[...])
        pre_ref[rows, :] = total


def node_kernel(
    block,
    odd_ref,
    count_ref,
    sends_ref,
    senders_ref,
    receivers_ref,
    pre_ref,
    pair_in_ref,
    cross_in_ref,
    table_ref,
    sender_weight_ref,
    outer_ref,
    node_inner_ref,
    node_outer_ref,
    updated_ref,
    pair_ref,
    cross_ref,
    halo_ref,
):
    odd = odd_ref[0] == 1
    nodes, width = table_ref.shape
    halo = pair_in_ref.shape[0]
    halo_ref[0:halo, :] = dot(pair_in_ref[...], sender_weight_ref[...]).astype(bf16)
    halo_ref[halo:, :] = dot(cross_in_ref[...], sender_weight_ref[...]).astype(bf16)
    summed = None
    for at in range(0, pre_ref.shape[0], block):
        rows = slice(at, at + block)
        slots = halo_slots(columns(senders_ref, at, block), nodes, halo, odd)
        total = pre_ref[rows, :] + dot(chosen(slots, 2 * halo), halo_ref[...])
        message = normalised(dot(silu(total).astype(bf16), outer_ref[...])).astype(bf16)
        position = at + lax.broadcasted_iota(jnp.int32, (1, block), 1)
        target = jnp.where(position < count_ref[0], receivers_ref[:, rows], -1)
        part = dot(placed(target, nodes), message)
        summed = part if summed is None else summed + part
    pre = dot(table_ref[...], node_inner_ref[0:width, :])
    pre += dot(summed.astype(bf16), node_inner_ref[width:, :])
    change = normalised(dot(silu(pre).astype(bf16), node_outer_ref[...]))
    updated_ref[...] = (table_ref[...].astype(f32) + change).astype(bf16)
    pair, cross, _ = send_columns(sends_ref, odd)
    pair_ref[...] = dot(chosen(pair, nodes), updated_ref[...]).astype(bf16)
    cross_ref[...] = dot(chosen(cross, nodes), updated_ref[...]).astype(bf16)


def grid_own_kernel(block, senders_ref, table_ref, edge_ref, inner_ref, pre_ref, sent_ref):
    nodes, width = table_ref.shape
    sent_ref[...] = dot(table_ref[...], inner_ref[0:width, :]).astype(bf16)
    for at in range(0, edge_ref.shape[0], block):
        rows = slice(at, at + block)
        total = dot(edge_ref[rows, :], inner_ref[width:, :])
        total += dot(chosen(columns(senders_ref, at, block), nodes), sent_ref[...])
        pre_ref[rows, :] = total


def grid_kernel(
    block,
    nodes,
    odd_ref,
    senders_ref,
    pre_ref,
    pair_in_ref,
    cross_in_ref,
    sender_weight_ref,
    outer_ref,
    out_weight_ref,
    prior_ref,
    target_ref,
    difference_ref,
    rounded_ref,
    halo_ref,
):
    odd = odd_ref[0] == 1
    halo = pair_in_ref.shape[0]
    halo_ref[0:halo, :] = dot(pair_in_ref[...], sender_weight_ref[...]).astype(bf16)
    halo_ref[halo:, :] = dot(cross_in_ref[...], sender_weight_ref[...]).astype(bf16)
    points = block // 3
    first = 3 * lax.broadcasted_iota(jnp.int32, (points, block), 0)
    lanes = lax.broadcasted_iota(jnp.int32, (points, block), 1)
    adding = jnp.where((lanes >= first) & (lanes < first + 3), 1.0, 0.0).astype(bf16)
    for at in range(0, pre_ref.shape[0], block):
        rows = slice(at, at + block)
        slots = halo_slots(columns(senders_ref, at, block), nodes, halo, odd)
        total = pre_ref[rows, :] + dot(chosen(slots, 2 * halo), halo_ref[...])
        message = normalised(dot(silu(total).astype(bf16), outer_ref[...])).astype(bf16)
        grid_sum = dot(adding, message).astype(bf16)
        output = lax.dot_general(
            out_weight_ref[...], grid_sum, (((1,), (1,)), ((), ())), preferred_element_type=f32
        )
        spots = slice(at // 3, at // 3 + points)
        difference = prior_ref[:, spots] + output - target_ref[:, spots]
        difference_ref[:, spots] = difference
        rounded_ref[:, spots] = difference.astype(bf16)


def smooth_slope(values):
    return values * lax.rsqrt(values * values + smooth * smooth)


def score_kernel(channel_ref, area_ref, difference_ref, everyone_ref, out_ref):
    difference = difference_ref[...]
    members = everyone_ref.shape[0]
    pairwise = smooth_slope(difference - everyone_ref[0].astype(f32))
    for n in range(1, members):
        pairwise += smooth_slope(difference - everyone_ref[n].astype(f32))
    result = smooth_slope(difference) - pairwise / (members - 1)
    weight = jnp.transpose(jnp.broadcast_to(channel_ref[...], (8, channel_ref.shape[1])))[:, :1]
    out_ref[:, 0, :] = result * weight * area_ref[...]


def spec():
    return pl.BlockSpec(memory_space=VMEM)


def scalar():
    return pl.BlockSpec(memory_space=pltpu.SMEM)


def shape(*dims, dtype=bf16):
    return jax.ShapeDtypeStruct(dims, dtype)


def call(kernel, name, scalars, operands, outs, scratch, flops):
    moved = sum(o.size * o.dtype.itemsize for o in (*operands, *outs))
    return pl.pallas_call(
        kernel,
        name=name,
        out_shape=outs,
        in_specs=[scalar()] * len(scalars) + [spec()] * len(operands),
        out_specs=tuple(spec() for _ in outs),
        scratch_shapes=scratch,
        cost_estimate=pl.CostEstimate(flops=flops, bytes_accessed=moved, transcendentals=0),
    )(*scalars, *operands)


def exchange(pair_rows, cross_rows):
    bands = lax.axis_size("patch")
    pair = [(i, i ^ 1) for i in range(bands) if i ^ 1 < bands]
    other = [((i + 1) ^ 1) - 1 for i in range(bands)]
    cross = [(i, j) for i, j in enumerate(other) if 0 <= j < bands]
    return lax.ppermute(pair_rows, "patch", pair), lax.ppermute(cross_rows, "patch", cross)


def per_device(
    mesh_latent,
    edge_latent,
    grid_edge_latent,
    edge_inner,
    edge_outer,
    node_inner,
    node_outer,
    grid_inner,
    grid_outer,
    out_weight,
    prior_state,
    target,
    channel_weight,
    area_weight,
    send_rows,
    edge_senders,
    edge_receivers,
    edge_count,
    grid_senders,
):
    latent = mesh_latent[0]
    sends = send_rows[0]
    halo = sends.shape[1]
    nodes, width = latent.shape
    edges = edge_senders.shape[0]
    grid_edges = grid_senders.shape[0]
    channels, points = prior_state.shape
    odd = (lax.axis_index("patch") % 2).astype(jnp.int32)[None]
    senders = edge_senders[None]
    receivers = edge_receivers[None]
    grid_rows = grid_senders[None]
    block = 256
    grid_block = 384

    pair, cross = call(
        select_kernel, "select", (odd,), (sends, latent), (shape(halo, width), shape(halo, width)), (), 10**8
    )
    pair_in, cross_in = exchange(pair, cross)
    (pre,) = call(
        lambda *refs: edge_own_kernel(block, *refs),
        "edge_own",
        (),
        (senders, receivers, latent, edge_latent, edge_inner),
        (shape(edges, width, dtype=f32),),
        (VMEM((nodes, width), bf16), VMEM((nodes, width), bf16)),
        2 * 10**9,
    )
    updated, pair, cross = call(
        lambda *refs: node_kernel(block, *refs),
        "node",
        (odd, edge_count),
        (
            sends,
            senders,
            receivers,
            pre,
            pair_in,
            cross_in,
            latent,
            edge_inner[:width],
            edge_outer,
            node_inner,
            node_outer,
        ),
        (shape(nodes, width), shape(halo, width), shape(halo, width)),
        (VMEM((2 * halo, width), bf16),),
        2 * 10**9,
    )
    pair_in, cross_in = exchange(pair, cross)
    (pre,) = call(
        lambda *refs: grid_own_kernel(grid_block, *refs),
        "grid_own",
        (),
        (grid_rows, updated, grid_edge_latent, grid_inner),
        (shape(grid_edges, width, dtype=f32),),
        (VMEM((nodes, width), bf16),),
        2 * 10**9,
    )
    difference, rounded = call(
        lambda *refs: grid_kernel(grid_block, nodes, *refs),
        "grid",
        (odd,),
        (
            grid_rows,
            pre,
            pair_in,
            cross_in,
            grid_inner[:width],
            grid_outer,
            out_weight,
            prior_state,
            target,
        ),
        (shape(channels, points, dtype=f32), shape(channels, points)),
        (VMEM((2 * halo, width), bf16),),
        2 * 10**9,
    )
    everyone = lax.all_gather(rounded[None], "mem", axis=0, tiled=True)
    (gradient,) = call(
        score_kernel,
        "score",
        (),
        (channel_weight[None], area_weight[None], difference, everyone),
        (shape(channels, 1, points, dtype=f32),),
        (),
        10**7,
    )
    return jnp.transpose(gradient, (1, 0, 2))


def solution(mesh):
    in_specs = (
        P("mem", "patch", None),
        P("patch", None),
        P("patch", None),
        P(),
        P(),
        P(),
        P(),
        P(),
        P(),
        P(),
        P(None, "patch"),
        P(None, "patch"),
        P(),
        P("patch"),
        P("patch", None, None),
        P("patch"),
        P("patch"),
        P("patch"),
        P("patch"),
    )
    out_specs = P("mem", None, "patch")
    return jax.shard_map(
        per_device, mesh=mesh, in_specs=in_specs, out_specs=out_specs, check_vma=False
    )
```

time: 82.1 us -> 57.5 us (0.70)
  the two profiles are of different devices: /device:TPU:17 before, /device:TPU:11 now
where the time goes in v1:
time: 57.5 us; the launch traced here: 57.1 us
  Pallas kernels  30.8 us (54%)
  blocking collectives  9.3 us (16%)
  starting transfers between devices  8.75 us (15%)
  local copies, waits for them, and re-layouts  7.61 us (13%)
  between operations  0.69 us (1%)
    pallas_call x6, Pallas kernels, call(): pl.pallas_call(kernel, name=name, out_shape=outs, in_specs=[scalar()] * l...  30.8 us
    all_gather x1, blocking collectives, per_device(): everyone = lax.all_gather(rounded[None], 'mem', axis=0, tiled=True)  9.3 us
    ppermute x2, starting transfers between devices, exchange(): lax.ppermute(cross_rows, 'patch', cross)  8.49 us
    unnamed x8, local copies, waits for them, and re-layouts  2.54 us
    slice x1, local copies, waits for them, and re-layouts, per_device(): edge_inner[:width]  1.88 us
    slice x1, local copies, waits for them, and re-layouts, per_device(): grid_inner[:width]  1.88 us
    broadcast_in_dim x1, local copies, waits for them, and re-layouts, per_device(): grid_rows = grid_senders[None]  1.3 us
  transfers between devices with their start and end apart: 4, of which 0 were waited for; matrix products, arithmetic and copies ran while one was open for 9% of the time, Pallas kernels for 20%

profile of v1, /device:TPU:11, one launch (start us, length us, event | category | flops | bytes accessed | tf_op | source)
XLA Modules:
  0.0 57.1 jit_solution(12775924119210564488)
XLA Ops:
  0.0 2.2 %select.3 = (bf16[96,512]{1,0:T(8,128)(2,1)}, bf16[96,512]{1,0:T(8,128)(2,1)}) custom-call(s32[1]{0:T(128)} %bitcast.2.odd_ref.refs_0_, s32[2,96]{1,0:T(2,128)} %bitcast.14, bf16[512,512]{1,0:T(8,128)(2,1)} %bitcast.9), custom_call_target="tpu_custom_call" | custom-call | flops 100000000 | bytes 721664 | tf_op jit(solution)/shard_map/select/pallas_call | solution.py:210
  2.2 0.3 collective-permute-start
  2.4 4.1 %collective-permute-start.1 = (bf16[96,512]{1,0:T(8,128)(2,1)}, bf16[96,512]{1,0:T(8,128)(2,1)S(1)}, u32[]{:S(2)}, u32[]{:S(2)}) collective-permute-start(bf16[96,512]{1,0:T(8,128)(2,1)} %get-tuple-element.13), channel_id=1, source_target_pairs={{1,2},{2,1},{3,4},{4,3},{5,6},{6,5},{9,10},{10,9},{11,12},{12,11},... | collective-permute-start | bytes 294920 | tf_op jit(solution)/shard_map/ppermute | solution.py:226
  6.6 1.9 %slice.6.refs_9_ = bf16[512,512]{1,0:T(8,128)(2,1)} slice(bf16[1536,512]{1,0:T(8,128)(2,1)} %refs_4_.1), slice={[0:512], [0:512]} | slice | bytes 1048576 | tf_op jit(solution)/shard_map/slice | solution.py:289
  9.1 1.3 %broadcast_in_dim.24.refs_0_.refs_1_ = s32[1,1536]{1,0:T(1,128)} reshape(s32[1536]{0:T(1024)} %param.37) | data formatting | bytes 12288 | tf_op jit(solution)/shard_map/broadcast_in_dim | solution.py:260
  10.4 1.9 %slice.7.refs_5_ = bf16[512,512]{1,0:T(8,128)(2,1)} slice(bf16[1024,512]{1,0:T(8,128)(2,1)} %refs_3_.3), slice={[0:512], [0:512]} | slice | bytes 1048576 | tf_op jit(solution)/shard_map/slice | solution.py:317
  12.3 5.6 %edge_own.1.refs_5_ = f32[1024,512]{1,0:T(8,128)} custom-call(s32[1,1024]{1,0:T(1,128)} %bitcast.17, s32[1,1024]{1,0:T(1,128)} %bitcast.19, bf16[512,512]{1,0:T(8,128)(2,1)} %bitcast.10, bf16[1024,512]{1,0:T(8,128)(2,1)} %refs_3_.2, bf16[1536,512]{1,0:T(8,128)(2,1)} %refs_4_.1), custom_call_target="tpu_custom_call" | custom-call | flops 2000000000 | bytes 5251072 | tf_op jit(solution)/shard_map/edge_own/pallas_call | solution.py:210
  17.9 0.0 collective-permute-done.refs_6_
  17.9 0.0 copy-start
  17.9 0.0 collective-permute-done.1.refs_7_
  17.9 0.6 %copy-done = bf16[96,512]{1,0:T(8,128)(2,1)} copy-done((bf16[96,512]{1,0:T(8,128)(2,1)}, bf16[96,512]{1,0:T(8,128)(2,1)S(1)}, u32[]{:S(2)}) %copy-start) | copy-done | bytes 98328
  18.6 0.0 copy-start.2
  18.6 0.6 %copy-done.2 = bf16[96,512]{1,0:T(8,128)(2,1)} copy-done((bf16[96,512]{1,0:T(8,128)(2,1)}, bf16[96,512]{1,0:T(8,128)(2,1)S(1)}, u32[]{:S(2)}) %copy-start.2) | copy-done | bytes 98328
  19.2 7.9 %node.1 = (bf16[512,512]{1,0:T(8,128)(2,1)}, bf16[96,512]{1,0:T(8,128)(2,1)}, bf16[96,512]{1,0:T(8,128)(2,1)}) custom-call(s32[1]{0:T(128)} %bitcast.2.odd_ref.refs_0_, s32[1]{0:T(128)S(6)} %copy.20.refs_1_, s32[2,96]{1,0:T(2,128)} %bitcast.15, s32[1,1024]{1,0:T(1,128)} %bitcast.18, s32[1,1024]{1,0:T(1,128)} %bitcast.20, f32[1024,512]{1,0:T(8,128)} %edge_own.1.refs_5_, ...), custom_call_target="tpu_custom_call" | custom-call | flops 2000000000 | bytes 6169344 | tf_op jit(solution)/shard_map/node/pallas_call | solution.py:210
  27.1 0.0 collective-permute-start.2
  27.1 4.4 %collective-permute-start.3 = (bf16[96,512]{1,0:T(8,128)(2,1)}, bf16[96,512]{1,0:T(8,128)(2,1)S(1)}, u32[]{:S(2)}, u32[]{:S(2)}) collective-permute-start(bf16[96,512]{1,0:T(8,128)(2,1)} %get-tuple-element.16), channel_id=1, source_target_pairs={{1,2},{2,1},{3,4},{4,3},{5,6},{6,5},{9,10},{10,9},{11,12},{12,11},... | collective-permute-start | bytes 294920 | tf_op jit(solution)/shard_map/ppermute | solution.py:226
  31.5 5.7 %grid_own.1.refs_2_ = f32[1536,512]{1,0:T(8,128)} custom-call(s32[1,1536]{1,0:T(1,128)} %broadcast_in_dim.24.refs_0_.refs_1_, bf16[512,512]{1,0:T(8,128)(2,1)} %get-tuple-element.14.refs_1_, bf16[1536,512]{1,0:T(8,128)(2,1)} %refs_2_.1, bf16[1024,512]{1,0:T(8,128)(2,1)} %refs_3_.3), custom_call_target="tpu_custom_call" | custom-call | flops 2000000000 | bytes 6297600 | tf_op jit(solution)/shard_map/grid_own/pallas_call | solution.py:210
  37.2 0.0 collective-permute-done.2.refs_3_
  37.2 0.0 copy-start.1
  37.2 0.0 collective-permute-done.3.refs_4_
  37.2 0.6 %copy-done.1 = bf16[96,512]{1,0:T(8,128)(2,1)} copy-done((bf16[96,512]{1,0:T(8,128)(2,1)}, bf16[96,512]{1,0:T(8,128)(2,1)S(1)}, u32[]{:S(2)}) %copy-start.1) | copy-done | bytes 98328
  37.8 0.0 copy-start.3
  37.8 0.6 %copy-done.3 = bf16[96,512]{1,0:T(8,128)(2,1)} copy-done((bf16[96,512]{1,0:T(8,128)(2,1)}, bf16[96,512]{1,0:T(8,128)(2,1)S(1)}, u32[]{:S(2)}) %copy-start.3) | copy-done | bytes 98328
  38.4 7.3 %grid.1 = (f32[87,512]{1,0:T(8,128)}, bf16[87,512]{1,0:T(8,128)(2,1)}) custom-call(s32[1]{0:T(128)} %bitcast.2.odd_ref.refs_0_, s32[1,1536]{1,0:T(1,128)} %broadcast_in_dim.24.refs_0_.refs_1_, f32[1536,512]{1,0:T(8,128)} %grid_own.1.refs_2_, bf16[96,512]{1,0:T(8,128)(2,1)} %copy-done.1, bf16[96,512]{1,0:T(8,128)(2,1)} %copy-done.3, ...), custom_call_target="tpu_custom_call" | custom-call | flops 2000000000 | bytes 5109760 | tf_op jit(solution)/shard_map/grid/pallas_call | solution.py:210
  45.8 9.3 %all-gather.1.everyone_ref = bf16[4,87,512]{2,1,0:T(8,128)(2,1)} all-gather(bf16[1,87,512]{2,1,0:T(8,128)(2,1)} %bitcast.12), channel_id=2, replica_groups=mesh['mem'=4,'patch'=8] {'mem'}, dimensions={0}, use_global_device_ids=true | all-gather | bytes 445440 | tf_op jit(solution)/shard_map/all_gather | solution.py:327
  55.1 2.1 %score.1 = f32[87,1,512]{2,1,0:T(1,128)} custom-call(f32[1,87]{1,0:T(1,128)} %bitcast.16, f32[1,512]{1,0:T(1,128)} %bitcast.13, f32[87,512]{1,0:T(8,128)} %get-tuple-element.17.difference_ref, bf16[4,87,512]{2,1,0:T(8,128)(2,1)} %all-gather.1.everyone_ref), custom_call_target="tpu_custom_call" | custom-call | flops 10000000 | bytes 715100 | tf_op jit(solution)/shard_map/score/pallas_call | solution.py:210
Async XLA Ops:
  2.2 15.7 %collective-permute-start = (bf16[96,512]{1,0:T(8,128)(2,1)}, bf16[96,512]{1,0:T(8,128)(2,1)S(1)}, u32[]{:S(2)}, u32[]{:S(2)}) collective-permute-start(bf16[96,512]{1,0:T(8,128)(2,1)} %get-tuple-element.12), channel_id=1, source_target_pairs={{0,1},{1,0},{2,3},{3,2},{4,5},{5,4},{6,7},{7,6},{8,9},{9,8},{10,11... | collective-permute-start | bytes 294920 | tf_op jit(solution)/shard_map/ppermute | solution.py:226
  2.4 15.5 %collective-permute-start.1 = (bf16[96,512]{1,0:T(8,128)(2,1)}, bf16[96,512]{1,0:T(8,128)(2,1)S(1)}, u32[]{:S(2)}, u32[]{:S(2)}) collective-permute-start(bf16[96,512]{1,0:T(8,128)(2,1)} %get-tuple-element.13), channel_id=1, source_target_pairs={{1,2},{2,1},{3,4},{4,3},{5,6},{6,5},{9,10},{10,9},{11,12},{12,11},... | collective-permute-start | bytes 294920 | tf_op jit(solution)/shard_map/ppermute | solution.py:226
  17.9 0.6 %copy-start = (bf16[96,512]{1,0:T(8,128)(2,1)}, bf16[96,512]{1,0:T(8,128)(2,1)S(1)}, u32[]{:S(2)}) copy-start(bf16[96,512]{1,0:T(8,128)(2,1)S(1)} %collective-permute-done.refs_6_) | copy-start | bytes 294916
  18.6 0.6 %copy-start.2 = (bf16[96,512]{1,0:T(8,128)(2,1)}, bf16[96,512]{1,0:T(8,128)(2,1)S(1)}, u32[]{:S(2)}) copy-start(bf16[96,512]{1,0:T(8,128)(2,1)S(1)} %collective-permute-done.1.refs_7_) | copy-start | bytes 294916
  27.1 10.1 %collective-permute-start.2 = (bf16[96,512]{1,0:T(8,128)(2,1)}, bf16[96,512]{1,0:T(8,128)(2,1)S(1)}, u32[]{:S(2)}, u32[]{:S(2)}) collective-permute-start(bf16[96,512]{1,0:T(8,128)(2,1)} %get-tuple-element.15), channel_id=1, source_target_pairs={{0,1},{1,0},{2,3},{3,2},{4,5},{5,4},{6,7},{7,6},{8,9},{9,8},{10,11... | collective-permute-start | bytes 294920 | tf_op jit(solution)/shard_map/ppermute | solution.py:226
  27.1 10.1 %collective-permute-start.3 = (bf16[96,512]{1,0:T(8,128)(2,1)}, bf16[96,512]{1,0:T(8,128)(2,1)S(1)}, u32[]{:S(2)}, u32[]{:S(2)}) collective-permute-start(bf16[96,512]{1,0:T(8,128)(2,1)} %get-tuple-element.16), channel_id=1, source_target_pairs={{1,2},{2,1},{3,4},{4,3},{5,6},{6,5},{9,10},{10,9},{11,12},{12,11},... | collective-permute-start | bytes 294920 | tf_op jit(solution)/shard_map/ppermute | solution.py:226
  37.2 0.6 %copy-start.1 = (bf16[96,512]{1,0:T(8,128)(2,1)}, bf16[96,512]{1,0:T(8,128)(2,1)S(1)}, u32[]{:S(2)}) copy-start(bf16[96,512]{1,0:T(8,128)(2,1)S(1)} %collective-permute-done.2.refs_3_) | copy-start | bytes 294916
  37.8 0.6 %copy-start.3 = (bf16[96,512]{1,0:T(8,128)(2,1)}, bf16[96,512]{1,0:T(8,128)(2,1)S(1)}, u32[]{:S(2)}) copy-start(bf16[96,512]{1,0:T(8,128)(2,1)S(1)} %collective-permute-done.3.refs_4_) | copy-start | bytes 294916

commit v2 on v1

v2 whole, which is shorter than its diff:
```python
import jax
import jax.numpy as jnp
from jax import lax
from jax.experimental import pallas as pl
from jax.experimental.pallas import tpu as pltpu
from jax.sharding import PartitionSpec as P

epsilon = 1e-05
smooth = 0.25
LANES = 128
VMEM = pltpu.VMEM
f32 = jnp.float32
bf16 = jnp.bfloat16


def dot(a, b):
    return jnp.dot(a, b, preferred_element_type=f32)


def silu_of_twice(half):
    return (half + half * jnp.tanh(half)).astype(bf16)


def normalised(centred):
    spread = jnp.mean(centred * centred, -1, keepdims=True)
    return centred * lax.rsqrt(spread + epsilon)


def centred_weight(ref):
    weight = ref[...].astype(f32)
    return (weight - jnp.mean(weight, -1, keepdims=True)).astype(bf16)


def column(row):
    return jnp.transpose(jnp.broadcast_to(row, (8, row.shape[1])))[:, :1]


def columns(ref, first, count):
    parts = [
        column(ref[first + at : first + at + LANES][None]) for at in range(0, count, LANES)
    ]
    return parts[0] if len(parts) == 1 else jnp.concatenate(parts, 0)


def chosen(index, width):
    lanes = lax.broadcasted_iota(jnp.int32, (index.shape[0], width), 1)
    return jnp.where(index == lanes, 1.0, 0.0).astype(bf16)


def placed(index, height):
    rows = lax.broadcasted_iota(jnp.int32, (height, index.shape[1]), 0)
    return jnp.where(index == rows, 1.0, 0.0).astype(bf16)


def halo_slots(index, nodes, halo, odd):
    at = index - nodes
    turned = jnp.where(at < halo, at + halo, at - halo)
    return jnp.where(at < 0, -1, jnp.where(odd, at, turned))


def pick_sends(sends_ref, odd, table, pair_ref, cross_ref):
    halo = sends_ref.shape[1]
    onward, back = sends_ref[0:1, :], sends_ref[1:2, :]
    pair = jnp.where(odd, back, onward)
    cross = jnp.where(odd, onward, back)
    index = jnp.concatenate([column(pair), column(cross)], 0)
    rows = dot(chosen(index, table.shape[0]), table).astype(bf16)
    pair_ref[...] = rows[:halo]
    cross_ref[...] = rows[halo:]


def halo_projection(pair_ref, cross_ref, weight_ref):
    rows = jnp.concatenate([pair_ref[...], cross_ref[...]], 0)
    return (0.5 * dot(rows, weight_ref[0 : rows.shape[1], :])).astype(bf16)


def select_kernel(odd_ref, sends_hbm, table_hbm, pair_ref, cross_ref, sends_ref, table_ref, semaphores):
    copies = [
        pltpu.make_async_copy(sends_hbm, sends_ref, semaphores.at[0]),
        pltpu.make_async_copy(table_hbm, table_ref, semaphores.at[1]),
    ]
    for copy in copies:
        copy.start()
    for copy in copies:
        copy.wait()
    pick_sends(sends_ref, odd_ref[0] == 1, table_ref[...], pair_ref, cross_ref)


def edge_own_kernel(
    block,
    senders_ref,
    receivers_ref,
    table_ref,
    edge_ref,
    inner_ref,
    outer_ref,
    node_inner_ref,
    node_outer_ref,
    pre_ref,
    node_pre_ref,
    outer_out_ref,
    node_outer_out_ref,
    sent_ref,
    got_ref,
):
    nodes, width = table_ref.shape
    sent_ref[...] = dot(table_ref[...], inner_ref[0:width, :]).astype(bf16)
    got_ref[...] = dot(table_ref[...], inner_ref[width : 2 * width, :]).astype(bf16)
    for at in range(0, edge_ref.shape[0], block):
        rows = slice(at, at + block)
        total = dot(edge_ref[rows, :], inner_ref[2 * width :, :])
        total += dot(chosen(columns(senders_ref, at, block), nodes), sent_ref[...])
        total += dot(chosen(columns(receivers_ref, at, block), nodes), got_ref[...])
        pre_ref[rows, :] = 0.5 * total
    node_pre_ref[...] = 0.5 * dot(table_ref[...], node_inner_ref[0:width, :])
    outer_out_ref[...] = centred_weight(outer_ref)
    node_outer_out_ref[...] = centred_weight(node_outer_ref)


def node_kernel(
    block,
    odd_ref,
    count_ref,
    sends_ref,
    senders_ref,
    receivers_ref,
    pre_ref,
    pair_in_ref,
    cross_in_ref,
    table_ref,
    inner_ref,
    outer_ref,
    node_pre_ref,
    node_inner_ref,
    node_outer_ref,
    updated_ref,
    pair_ref,
    cross_ref,
    halo_ref,
):
    odd = odd_ref[0] == 1
    nodes, width = table_ref.shape
    halo = pair_in_ref.shape[0]
    halo_ref[...] = halo_projection(pair_in_ref, cross_in_ref, inner_ref)
    summed = None
    for at in range(0, pre_ref.shape[0], block):
        rows = slice(at, at + block)
        slots = halo_slots(columns(senders_ref, at, block), nodes, halo, odd)
        total = pre_ref[rows, :] + dot(chosen(slots, 2 * halo), halo_ref[...])
        message = normalised(dot(silu_of_twice(total), outer_ref[...])).astype(bf16)
        position = at + lax.broadcasted_iota(jnp.int32, (1, block), 1)
        target = jnp.where(position < count_ref[0], receivers_ref[rows][None], -1)
        part = dot(placed(target, nodes), message)
        summed = part if summed is None else summed + part
    pre = node_pre_ref[...] + dot((0.5 * summed).astype(bf16), node_inner_ref[width:, :])
    change = normalised(dot(silu_of_twice(pre), node_outer_ref[...]))
    updated = (table_ref[...].astype(f32) + change).astype(bf16)
    updated_ref[...] = updated
    pick_sends(sends_ref, odd, updated, pair_ref, cross_ref)


def grid_own_kernel(block, senders_ref, table_ref, edge_ref, inner_ref, outer_ref, pre_ref, outer_out_ref, sent_ref):
    nodes, width = table_ref.shape
    sent_ref[...] = dot(table_ref[...], inner_ref[0:width, :]).astype(bf16)
    for at in range(0, edge_ref.shape[0], block):
        rows = slice(at, at + block)
        total = dot(edge_ref[rows, :], inner_ref[width:, :])
        total += dot(chosen(columns(senders_ref, at, block), nodes), sent_ref[...])
        pre_ref[rows, :] = 0.5 * total
    outer_out_ref[...] = centred_weight(outer_ref)


def grid_kernel(
    block,
    nodes,
    odd_ref,
    senders_ref,
    pre_ref,
    pair_in_ref,
    cross_in_ref,
    inner_ref,
    outer_ref,
    out_weight_ref,
    prior_ref,
    target_ref,
    difference_ref,
    rounded_ref,
    halo_ref,
    message_ref,
):
    odd = odd_ref[0] == 1
    halo = pair_in_ref.shape[0]
    halo_ref[...] = halo_projection(pair_in_ref, cross_in_ref, inner_ref)
    points = block // 3
    for at in range(0, pre_ref.shape[0], block):
        rows = slice(at, at + block)
        slots = halo_slots(columns(senders_ref, at, block), nodes, halo, odd)
        total = pre_ref[rows, :] + dot(chosen(slots, 2 * halo), halo_ref[...])
        message = normalised(dot(silu_of_twice(total), outer_ref[...]))
        tiles = []
        for t in range(message_ref.shape[0]):
            message_ref[t, rows, :] = message[:, t * LANES : (t + 1) * LANES]
            triple = [message_ref[t, pl.ds(at + k, points, 3), :] for k in range(3)]
            tiles.append((triple[0] + triple[1] + triple[2]).astype(bf16))
        grid_sum = jnp.concatenate(tiles, 1)
        output = lax.dot_general(
            out_weight_ref[...], grid_sum, (((1,), (1,)), ((), ())), preferred_element_type=f32
        )
        spots = slice(at // 3, at // 3 + points)
        difference = prior_ref[:, spots] + output - target_ref[:, spots]
        difference_ref[:, spots] = difference
        rounded_ref[:, spots] = difference.astype(bf16)


def smooth_slope(values):
    return values * lax.rsqrt(values * values + smooth * smooth)


def score_kernel(channel_ref, area_ref, difference_ref, everyone_ref, out_ref):
    difference = difference_ref[...]
    members = everyone_ref.shape[0]
    pairwise = smooth_slope(difference - everyone_ref[0].astype(f32))
    for n in range(1, members):
        pairwise += smooth_slope(difference - everyone_ref[n].astype(f32))
    result = smooth_slope(difference) - pairwise / (members - 1)
    weight = jnp.transpose(jnp.broadcast_to(channel_ref[...], (8, channel_ref.shape[1])))[:, :1]
    out_ref[:, 0, :] = result * weight * area_ref[...]


def spec():
    return pl.BlockSpec(memory_space=VMEM)


def far():
    return pl.BlockSpec(memory_space=pltpu.HBM)


def scalar():
    return pl.BlockSpec(memory_space=pltpu.SMEM)


def shape(*dims, dtype=bf16):
    return jax.ShapeDtypeStruct(dims, dtype)


def call(kernel, name, scalars, operands, outs, scratch, flops, from_hbm=False):
    moved = sum(o.size * o.dtype.itemsize for o in (*operands, *outs))
    return pl.pallas_call(
        kernel,
        name=name,
        out_shape=outs,
        in_specs=[scalar()] * len(scalars) + [far() if from_hbm else spec()] * len(operands),
        out_specs=tuple(spec() for _ in outs),
        scratch_shapes=scratch,
        compiler_params=pltpu.CompilerParams(vmem_limit_bytes=24 * 2**20),
        cost_estimate=pl.CostEstimate(flops=flops, bytes_accessed=moved, transcendentals=0),
    )(*scalars, *operands)


def exchange(pair_rows, cross_rows):
    members, bands = lax.axis_size("mem"), lax.axis_size("patch")
    pair = [(i, i ^ 1) for i in range(bands)]
    cross = []
    for m in range(members):
        for i in range(bands):
            j = ((i + 1) ^ 1) - 1
            other = (m, j) if 0 <= j < bands else (m ^ 1, i)
            cross.append((m * bands + i, other[0] * bands + other[1]))
    crossed = lax.ppermute(cross_rows, ("mem", "patch"), cross)
    return lax.ppermute(pair_rows, "patch", pair), crossed


def per_device(
    mesh_latent,
    edge_latent,
    grid_edge_latent,
    edge_inner,
    edge_outer,
    node_inner,
    node_outer,
    grid_inner,
    grid_outer,
    out_weight,
    prior_state,
    target,
    channel_weight,
    area_weight,
    send_rows,
    edge_senders,
    edge_receivers,
    edge_count,
    grid_senders,
):
    latent = mesh_latent[0]
    sends = send_rows[0]
    halo = sends.shape[1]
    nodes, width = latent.shape
    edges = edge_senders.shape[0]
    grid_edges = grid_senders.shape[0]
    channels, points = prior_state.shape
    odd = (lax.axis_index("patch") % 2).astype(jnp.int32)[None]
    senders = edge_senders
    receivers = edge_receivers
    grid_rows = grid_senders
    block = 512
    grid_block = 768

    pair, cross = call(
        select_kernel,
        "select",
        (odd,),
        tuple(pltpu.with_memory_space_constraint(x, pltpu.HBM) for x in (sends, latent)),
        (shape(halo, width), shape(halo, width)),
        (VMEM((2, halo), jnp.int32), VMEM((nodes, width), bf16), pltpu.SemaphoreType.DMA((2,))),
        10**10,
        from_hbm=True,
    )
    pair_in, cross_in = exchange(pair, cross)
    pre, node_pre, outer, second = call(
        lambda *refs: edge_own_kernel(block, *refs),
        "edge_own",
        (),
        (senders, receivers, latent, edge_latent, edge_inner, edge_outer, node_inner, node_outer),
        (
            shape(edges, width, dtype=f32),
            shape(nodes, width, dtype=f32),
            shape(width, width),
            shape(width, width),
        ),
        (VMEM((nodes, width), bf16), VMEM((nodes, width), bf16)),
        10**10,
    )
    updated, pair, cross = call(
        lambda *refs: node_kernel(block, *refs),
        "node",
        (odd, edge_count),
        (
            sends,
            senders,
            receivers,
            pre,
            pair_in,
            cross_in,
            latent,
            edge_inner,
            outer,
            node_pre,
            node_inner,
            second,
        ),
        (shape(nodes, width), shape(halo, width), shape(halo, width)),
        (VMEM((2 * halo, width), bf16),),
        10**10,
    )
    pair_in, cross_in = exchange(pair, cross)
    pre, outer = call(
        lambda *refs: grid_own_kernel(grid_block, *refs),
        "grid_own",
        (),
        (grid_rows, updated, grid_edge_latent, grid_inner, grid_outer),
        (shape(grid_edges, width, dtype=f32), shape(width, width)),
        (VMEM((nodes, width), bf16),),
        10**10,
    )
    difference, rounded = call(
        lambda *refs: grid_kernel(grid_block, nodes, *refs),
        "grid",
        (odd,),
        (grid_rows, pre, pair_in, cross_in, grid_inner, outer, out_weight, prior_state, target),
        (shape(channels, points, dtype=f32), shape(channels, points)),
        (VMEM((2 * halo, width), bf16), VMEM((width // LANES, grid_edges, LANES), f32)),
        10**10,
    )
    everyone = lax.all_gather(rounded[None], "mem", axis=0, tiled=True)
    (gradient,) = call(
        score_kernel,
        "score",
        (),
        (channel_weight[None], area_weight[None], difference, everyone),
        (shape(channels, 1, points, dtype=f32),),
        (),
        10**7,
    )
    return jnp.transpose(gradient, (1, 0, 2))


def solution(mesh):
    in_specs = (
        P("mem", "patch", None),
        P("patch", None),
        P("patch", None),
        P(),
        P(),
        P(),
        P(),
        P(),
        P(),
        P(),
        P(None, "patch"),
        P(None, "patch"),
        P(),
        P("patch"),
        P("patch", None, None),
        P("patch"),
        P("patch"),
        P("patch"),
        P("patch"),
    )
    out_specs = P("mem", None, "patch")
    return jax.shard_map(
        per_device, mesh=mesh, in_specs=in_specs, out_specs=out_specs, check_vma=False
    )
```

time: 57.5 us -> 29.3 us (0.51)
  the two profiles are of different devices: /device:TPU:11 before, /device:TPU:17 now
where the time goes in v2:
time: 29.3 us; the launch traced here: 29.1 us
  Pallas kernels  13.2 us (45%)
  blocking collectives  8.92 us (30%)
  starting transfers between devices  3.03 us (10%)
  waiting for transfers between devices  3 us (10%)
  between operations  0.87 us (3%)
    pallas_call x6, Pallas kernels, call(): pl.pallas_call(kernel, name=name, out_shape=outs, in_specs=[scalar()] * l...  13.2 us
    all_gather x1, blocking collectives, per_device(): everyone = lax.all_gather(rounded[None], 'mem', axis=0, tiled=True)  8.92 us
    ppermute x2, waiting for transfers between devices, exchange(): crossed = lax.ppermute(cross_rows, ('mem', 'patch'), cross)  2.99 us
    ppermute x2, starting transfers between devices, exchange(): return (lax.ppermute(pair_rows, 'patch', pair), crossed)  2.89 us
  transfers between devices with their start and end apart: 4, of which 2 were waited for; matrix products, arithmetic and copies ran while one was open for 0% of the time, Pallas kernels for 17%

profile of v2, /device:TPU:17, one launch (start us, length us, event | category | flops | bytes accessed | tf_op | source)
XLA Modules:
  0.0 29.1 jit_solution(13918608599832126432)
XLA Ops:
  0.0 0.0 copy-start.7
  0.0 0.0 copy-start.8
  0.0 0.0 copy-start.9
  0.0 0.0 copy-start.15
  0.0 0.0 copy-start.16
  0.1 1.7 %select.3 = (bf16[96,512]{1,0:T(8,128)(2,1)S(1)}, bf16[96,512]{1,0:T(8,128)(2,1)S(1)}) custom-call(s32[1]{0:T(128)} %bitcast.2.odd_ref.refs_0_, s32[2,96]{1,0:T(2,128)} %bitcast.13, bf16[512,512]{1,0:T(8,128)(2,1)} %bitcast.10), custom_call_target="tpu_custom_call" | custom-call | flops 10000000000 | bytes 721664 | tf_op jit(solution)/shard_map/select/pallas_call | solution.py:248
  1.7 1.3 %collective-permute-start = (bf16[96,512]{1,0:T(8,128)(2,1)S(1)}, bf16[96,512]{1,0:T(8,128)(2,1)S(1)}, u32[]{:S(2)}, u32[]{:S(2)}) collective-permute-start(bf16[96,512]{1,0:T(8,128)(2,1)S(1)} %get-tuple-element.19), channel_id=1, source_target_pairs={{0,1},{1,0},{2,3},{3,2},{4,5},{5,4},{6,7},{7,6},{8,9},{9,8},{10,11... | collective-permute-start | bytes 294920 | tf_op jit(solution)/shard_map/ppermute | solution.py:270
  3.0 0.1 collective-permute-start.1
  3.2 0.0 copy-done.4
  3.2 0.0 copy-done.7
  3.2 2.7 %edge_own.1 = (f32[1024,512]{1,0:T(8,128)S(1)}, f32[512,512]{1,0:T(8,128)S(1)}, bf16[512,512]{1,0:T(8,128)(2,1)S(1)}, bf16[512,512]{1,0:T(8,128)(2,1)S(1)}) custom-call(s32[1024]{0:T(1024)S(1)} %copy-done.15, s32[1024]{0:T(1024)S(1)} %copy-done.16, bf16[512,512]{1,0:T(8,128)(2,1)S(1)} %bitcast.11, bf16[1024,512]{1,0:T(8,128)(2,1)S(1)} %copy-done.4, ...), custom_call_target="tpu_custom_call" | custom-call | flops 10000000000 | bytes 9445376 | tf_op jit(solution)/shard_map/edge_own/pallas_call | solution.py:248
  6.6 0.0 collective-permute-done.refs_6_
  6.6 0.8 %collective-permute-done.1.refs_7_ = bf16[96,512]{1,0:T(8,128)(2,1)S(1)} collective-permute-done((bf16[96,512]{1,0:T(8,128)(2,1)S(1)}, bf16[96,512]{1,0:T(8,128)(2,1)S(1)}, u32[]{:S(2)}, u32[]{:S(2)}) %collective-permute-start.1) | collective-permute-done | bytes 98336 | tf_op jit(solution)/shard_map/ppermute | solution.py:269
  7.5 0.0 copy-done.17
  7.5 0.0 copy-start.14
  7.5 3.0 %node.1 = (bf16[512,512]{1,0:T(8,128)(2,1)S(1)}, bf16[96,512]{1,0:T(8,128)(2,1)S(1)}, bf16[96,512]{1,0:T(8,128)(2,1)S(1)}) custom-call(s32[1]{0:T(128)} %bitcast.2.odd_ref.refs_0_, s32[1]{0:T(128)S(6)} %copy.20.refs_1_, s32[2,96]{1,0:T(2,128)S(1)} %bitcast.14, s32[1024]{0:T(1024)S(1)} %copy-done.15, s32[1024]{0:T(1024)S(1)} %copy-done.16, ...), custom_call_target="tpu_custom_call" | custom-call | flops 10000000000 | bytes 8266496 | tf_op jit(solution)/shard_map/node/pallas_call | solution.py:248
  10.5 1.6 %collective-permute-start.2 = (bf16[96,512]{1,0:T(8,128)(2,1)S(1)}, bf16[96,512]{1,0:T(8,128)(2,1)S(1)}, u32[]{:S(2)}, u32[]{:S(2)}) collective-permute-start(bf16[96,512]{1,0:T(8,128)(2,1)S(1)} %get-tuple-element.26), channel_id=1, source_target_pairs={{0,1},{1,0},{2,3},{3,2},{4,5},{5,4},{6,7},{7,6},{8,9},{9,8},{10,11... | collective-permute-start | bytes 294920 | tf_op jit(solution)/shard_map/ppermute | solution.py:270
  12.1 0.0 collective-permute-start.3
  12.1 0.0 copy-done.6
  12.1 0.0 copy-done.10
  12.1 0.0 copy-done.14
  12.1 0.0 copy-start.11
  12.2 0.0 copy-start.12
  12.2 0.0 copy-start.13
  12.2 2.2 %grid_own.1 = (f32[1536,512]{1,0:T(8,128)S(1)}, bf16[512,512]{1,0:T(8,128)(2,1)S(1)}) custom-call(s32[1536]{0:T(1024)S(1)} %copy-done.14, bf16[512,512]{1,0:T(8,128)(2,1)S(1)} %get-tuple-element.24.refs_1_, bf16[1536,512]{1,0:T(8,128)(2,1)S(1)} %copy-done.3, bf16[1024,512]{1,0:T(8,128)(2,1)S(1)} %copy-done.6, bf16[512,512]{1,0:T(8,128)(2,1)S(1)} %copy-done.10), custom_call_target="tpu_custom_call" | custom-call | flops 10000000000 | bytes 7346176 | tf_op jit(solution)/shard_map/grid_own/pallas_call | solution.py:248
  14.4 0.0 collective-permute-done.2.refs_3_
  14.4 2.1 %collective-permute-done.3.refs_4_ = bf16[96,512]{1,0:T(8,128)(2,1)S(1)} collective-permute-done((bf16[96,512]{1,0:T(8,128)(2,1)S(1)}, bf16[96,512]{1,0:T(8,128)(2,1)S(1)}, u32[]{:S(2)}, u32[]{:S(2)}) %collective-permute-start.3) | collective-permute-done | bytes 98336 | tf_op jit(solution)/shard_map/ppermute | solution.py:269
  16.6 0.0 copy-start
  16.6 0.0 copy-start.1
  16.6 2.6 %grid.1 = (f32[87,512]{1,0:T(8,128)S(1)}, bf16[87,512]{1,0:T(8,128)(2,1)S(1)}) custom-call(s32[1]{0:T(128)} %bitcast.2.odd_ref.refs_0_, s32[1536]{0:T(1024)S(1)} %copy-done.14, f32[1536,512]{1,0:T(8,128)S(1)} %get-tuple-element.25.refs_2_, bf16[96,512]{1,0:T(8,128)(2,1)S(1)} %collective-permute-done.2.refs_3_, ...), custom_call_target="tpu_custom_call" | custom-call | flops 10000000000 | bytes 5634048 | tf_op jit(solution)/shard_map/grid/pallas_call | solution.py:248
  19.2 8.9 %all-gather.1.everyone_ref = bf16[4,87,512]{2,1,0:T(8,128)(2,1)S(1)} all-gather(bf16[1,87,512]{2,1,0:T(8,128)(2,1)S(1)} %bitcast.7), channel_id=2, replica_groups=mesh['mem'=4,'patch'=8] {'mem'}, dimensions={0}, use_global_device_ids=true | all-gather | bytes 445440 | tf_op jit(solution)/shard_map/all_gather | solution.py:374
  28.1 1.0 %score.1 = f32[87,1,512]{2,1,0:T(1,128)} custom-call(f32[1,87]{1,0:T(1,128)S(1)} %bitcast.9, f32[1,512]{1,0:T(1,128)S(1)} %bitcast.8, f32[87,512]{1,0:T(8,128)S(1)} %get-tuple-element.29.difference_ref, bf16[4,87,512]{2,1,0:T(8,128)(2,1)S(1)} %all-gather.1.everyone_ref), custom_call_target="tpu_custom_call" | custom-call | flops 10000000 | bytes 715100 | tf_op jit(solution)/shard_map/score/pallas_call | solution.py:248
  (19 shorter events, 0.0 us)
Async XLA Ops:
  0.0 3.2 %copy-start.2 = (bf16[1536,512]{1,0:T(8,128)(2,1)S(1)}, bf16[1536,512]{1,0:T(8,128)(2,1)}, u32[]{:S(2)}) copy-start(bf16[1536,512]{1,0:T(8,128)(2,1)} %refs_9_.2) | copy-start | bytes 4718596
  0.0 3.2 %copy-start.4 = (bf16[1024,512]{1,0:T(8,128)(2,1)S(1)}, bf16[1024,512]{1,0:T(8,128)(2,1)}, u32[]{:S(2)}) copy-start(bf16[1024,512]{1,0:T(8,128)(2,1)} %refs_3_.3) | copy-start | bytes 3145732
  0.0 3.2 %copy-start.5 = (bf16[1024,512]{1,0:T(8,128)(2,1)S(1)}, bf16[1024,512]{1,0:T(8,128)(2,1)}, u32[]{:S(2)}) copy-start(bf16[1024,512]{1,0:T(8,128)(2,1)} %refs_12_.1) | copy-start | bytes 3145732
  0.0 3.2 %copy-start.7 = (bf16[512,512]{1,0:T(8,128)(2,1)S(1)}, bf16[512,512]{1,0:T(8,128)(2,1)}, u32[]{:S(2)}) copy-start(bf16[512,512]{1,0:T(8,128)(2,1)} %refs_5_.2) | copy-start | bytes 1572868
  0.0 3.2 %copy-start.8 = (bf16[512,512]{1,0:T(8,128)(2,1)S(1)}, bf16[512,512]{1,0:T(8,128)(2,1)}, u32[]{:S(2)}) copy-start(bf16[512,512]{1,0:T(8,128)(2,1)} %refs_7_.2) | copy-start | bytes 1572868
  0.0 3.2 %copy-start.9 = (bf16[1,512,512]{2,1,0:T(8,128)(2,1)S(1)}, bf16[1,512,512]{2,1,0:T(8,128)(2,1)}, u32[]{:S(2)}) copy-start(bf16[1,512,512]{2,1,0:T(8,128)(2,1)} %param.19) | copy-start | bytes 1572868
  0.0 3.2 %copy-start.15 = (s32[1024]{0:T(1024)S(1)}, s32[1024]{0:T(1024)}, u32[]{:S(2)}) copy-start(s32[1024]{0:T(1024)} %refs_3_.4) | copy-start | bytes 12292
  0.0 3.2 %copy-start.16 = (s32[1024]{0:T(1024)S(1)}, s32[1024]{0:T(1024)}, u32[]{:S(2)}) copy-start(s32[1024]{0:T(1024)} %refs_4_.4) | copy-start | bytes 12292
  1.7 4.9 %collective-permute-start = (bf16[96,512]{1,0:T(8,128)(2,1)S(1)}, bf16[96,512]{1,0:T(8,128)(2,1)S(1)}, u32[]{:S(2)}, u32[]{:S(2)}) collective-permute-start(bf16[96,512]{1,0:T(8,128)(2,1)S(1)} %get-tuple-element.19), channel_id=1, source_target_pairs={{0,1},{1,0},{2,3},{3,2},{4,5},{5,4},{6,7},{7,6},{8,9},{9,8},{10,11... | collective-permute-start | bytes 294920 | tf_op jit(solution)/shard_map/ppermute | solution.py:270
  3.0 4.4 %copy-start.17 = (s32[1,2,96]{2,1,0:T(2,128)S(1)}, s32[1,2,96]{2,1,0:T(2,128)}, u32[]{:S(2)}) copy-start(s32[1,2,96]{2,1,0:T(2,128)} %param.33) | copy-start | bytes 2308
  3.0 4.4 %collective-permute-start.1 = (bf16[96,512]{1,0:T(8,128)(2,1)S(1)}, bf16[96,512]{1,0:T(8,128)(2,1)S(1)}, u32[]{:S(2)}, u32[]{:S(2)}) collective-permute-start(bf16[96,512]{1,0:T(8,128)(2,1)S(1)} %get-tuple-element.20), channel_id=1, source_target_pairs={{0,8},{1,2},{2,1},{3,4},{4,3},{5,6},{6,5},{7,15},{8,0},{9,10},{10,... | collective-permute-start | bytes 294920 | tf_op jit(solution)/shard_map/ppermute | solution.py:269
  7.5 4.7 %copy-start.3 = (bf16[1536,512]{1,0:T(8,128)(2,1)S(1)}, bf16[1536,512]{1,0:T(8,128)(2,1)}, u32[]{:S(2)}) copy-start(bf16[1536,512]{1,0:T(8,128)(2,1)} %refs_2_.1) | copy-start | bytes 4718596
  7.5 4.7 %copy-start.6 = (bf16[1024,512]{1,0:T(8,128)(2,1)S(1)}, bf16[1024,512]{1,0:T(8,128)(2,1)}, u32[]{:S(2)}) copy-start(bf16[1024,512]{1,0:T(8,128)(2,1)} %refs_5_.3) | copy-start | bytes 3145732
  7.5 4.7 %copy-start.10 = (bf16[512,512]{1,0:T(8,128)(2,1)S(1)}, bf16[512,512]{1,0:T(8,128)(2,1)}, u32[]{:S(2)}) copy-start(bf16[512,512]{1,0:T(8,128)(2,1)} %refs_4_.5) | copy-start | bytes 1572868
  7.5 4.7 %copy-start.14 = (s32[1536]{0:T(1024)S(1)}, s32[1536]{0:T(1024)}, u32[]{:S(2)}) copy-start(s32[1536]{0:T(1024)} %refs_1_.4) | copy-start | bytes 18436
  10.5 3.9 %collective-permute-start.2 = (bf16[96,512]{1,0:T(8,128)(2,1)S(1)}, bf16[96,512]{1,0:T(8,128)(2,1)S(1)}, u32[]{:S(2)}, u32[]{:S(2)}) collective-permute-start(bf16[96,512]{1,0:T(8,128)(2,1)S(1)} %get-tuple-element.26), channel_id=1, source_target_pairs={{0,1},{1,0},{2,3},{3,2},{4,5},{5,4},{6,7},{7,6},{8,9},{9,8},{10,11... | collective-permute-start | bytes 294920 | tf_op jit(solution)/shard_map/ppermute | solution.py:270
  12.1 4.5 %collective-permute-start.3 = (bf16[96,512]{1,0:T(8,128)(2,1)S(1)}, bf16[96,512]{1,0:T(8,128)(2,1)S(1)}, u32[]{:S(2)}, u32[]{:S(2)}) collective-permute-start(bf16[96,512]{1,0:T(8,128)(2,1)S(1)} %get-tuple-element.27), channel_id=1, source_target_pairs={{0,8},{1,2},{2,1},{3,4},{4,3},{5,6},{6,5},{7,15},{8,0},{9,10},{10,... | collective-permute-start | bytes 294920 | tf_op jit(solution)/shard_map/ppermute | solution.py:269
  12.1 4.4 %copy-start.11 = (f32[87,512]{1,0:T(8,128)S(1)}, f32[87,512]{1,0:T(8,128)}, u32[]{:S(2)}) copy-start(f32[87,512]{1,0:T(8,128)} %refs_8_.1) | copy-start | bytes 534532
  12.2 4.4 %copy-start.12 = (f32[87,512]{1,0:T(8,128)S(1)}, f32[87,512]{1,0:T(8,128)}, u32[]{:S(2)}) copy-start(f32[87,512]{1,0:T(8,128)} %refs_9_.3) | copy-start | bytes 534532
  12.2 4.4 %copy-start.13 = (bf16[87,512]{1,0:T(8,128)(2,1)S(1)}, bf16[87,512]{1,0:T(8,128)(2,1)}, u32[]{:S(2)}) copy-start(bf16[87,512]{1,0:T(8,128)(2,1)} %refs_7_.3) | copy-start | bytes 267268
  16.6 11.6 %copy-start = (f32[512]{0:T(512)S(1)}, f32[512]{0:T(512)}, u32[]{:S(2)}) copy-start(f32[512]{0:T(512)} %param.32) | copy-start | bytes 6148
  16.6 11.5 %copy-start.1 = (f32[87]{0:T(128)S(1)}, f32[87]{0:T(128)}, u32[]{:S(2)}) copy-start(f32[87]{0:T(128)} %param.31) | copy-start | bytes 1048

commit v3 on v2

--- a/solution.py
+++ b/solution.py
@@ -58,15 +58,15 @@
     return jnp.where(at < 0, -1, jnp.where(odd, at, turned))
 
 
-def pick_sends(sends_ref, odd, table, pair_ref, cross_ref):
-    halo = sends_ref.shape[1]
+def halo_choice(senders_ref, nodes, halo, odd, choice_ref):
+    for at in range(0, senders_ref.shape[0], LANES):
+        slots = halo_slots(senders_ref[at : at + LANES][None], nodes, halo, odd)
+        choice_ref[at : at + LANES, :] = chosen(column(slots), choice_ref.shape[1])
+
+
+def send_index(sends_ref, odd):
     onward, back = sends_ref[0:1, :], sends_ref[1:2, :]
-    pair = jnp.where(odd, back, onward)
-    cross = jnp.where(odd, onward, back)
-    index = jnp.concatenate([column(pair), column(cross)], 0)
-    rows = dot(chosen(index, table.shape[0]), table).astype(bf16)
-    pair_ref[...] = rows[:halo]
-    cross_ref[...] = rows[halo:]
+    return jnp.where(odd, back, onward), jnp.where(odd, onward, back)
 
 
 def halo_projection(pair_ref, cross_ref, weight_ref):
@@ -75,21 +75,40 @@
 
 
 def select_kernel(odd_ref, sends_hbm, table_hbm, pair_ref, cross_ref, sends_ref, table_ref, semaphores):
-    copies = [
-        pltpu.make_async_copy(sends_hbm, sends_ref, semaphores.at[0]),
-        pltpu.make_async_copy(table_hbm, table_ref, semaphores.at[1]),
-    ]
-    for copy in copies:
-        copy.start()
-    for copy in copies:
+    pieces = semaphores.shape[0] - 1
+    step = table_ref.shape[0] // pieces
+    first = pltpu.make_async_copy(sends_hbm, sends_ref, semaphores.at[pieces])
+    first.start()
+    copies = []
+    for at in range(pieces):
+        rows = pl.ds(at * step, step)
+        copies.append(
+            pltpu.make_async_copy(table_hbm.at[rows, :], table_ref.at[rows, :], semaphores.at[at])
+        )
+        copies[-1].start()
+    first.wait()
+    pair, cross = send_index(sends_ref, odd_ref[0] == 1)
+    index = jnp.concatenate([column(pair), column(cross)], 0)
+    picked = None
+    for at, copy in enumerate(copies):
         copy.wait()
-    pick_sends(sends_ref, odd_ref[0] == 1, table_ref[...], pair_ref, cross_ref)
+        part = dot(chosen(index - at * step, step), table_ref[at * step : (at + 1) * step, :])
+        picked = part if picked is None else picked + part
+    halo = pair_ref.shape[0]
+    rows = picked.astype(bf16)
+    pair_ref[...] = rows[:halo]
+    cross_ref[...] = rows[halo:]
 
 
 def edge_own_kernel(
     block,
+    odd_ref,
+    count_ref,
+    sends_ref,
     senders_ref,
     receivers_ref,
+    pair_ref,
+    cross_ref,
     table_ref,
     edge_ref,
     inner_ref,
@@ -97,84 +116,116 @@
     node_inner_ref,
     node_outer_ref,
     pre_ref,
-    node_pre_ref,
+    sent_pre_ref,
     outer_out_ref,
     node_outer_out_ref,
+    choice_ref,
+    placing_ref,
+    sent_placing_ref,
     sent_ref,
     got_ref,
 ):
     nodes, width = table_ref.shape
+    edges = edge_ref.shape[0]
+    halo = pair_ref.shape[0]
+    odd = odd_ref[0] == 1
     sent_ref[...] = dot(table_ref[...], inner_ref[0:width, :]).astype(bf16)
     got_ref[...] = dot(table_ref[...], inner_ref[width : 2 * width, :]).astype(bf16)
-    for at in range(0, edge_ref.shape[0], block):
+    for at in range(0, edges, block):
         rows = slice(at, at + block)
         total = dot(edge_ref[rows, :], inner_ref[2 * width :, :])
         total += dot(chosen(columns(senders_ref, at, block), nodes), sent_ref[...])
         total += dot(chosen(columns(receivers_ref, at, block), nodes), got_ref[...])
         pre_ref[rows, :] = 0.5 * total
-    node_pre_ref[...] = 0.5 * dot(table_ref[...], node_inner_ref[0:width, :])
     outer_out_ref[...] = centred_weight(outer_ref)
     node_outer_out_ref[...] = centred_weight(node_outer_ref)
-
-
-def node_kernel(
+    halo_choice(senders_ref, nodes, halo, odd, choice_ref)
+    position = lax.broadcasted_iota(jnp.int32, (1, edges), 1)
+    target = jnp.where(position < count_ref[...][None], receivers_ref[...][None], -1)
+    placing_ref[...] = placed(target, nodes)
+    pair, cross = send_index(sends_ref, odd)
+    index = jnp.concatenate([column(pair), column(cross)], 0)
+    sent_placing_ref[...] = jnp.where(index == target, 1.0, 0.0).astype(bf16)
+    rows = jnp.concatenate([pair_ref[...], cross_ref[...]], 0)
+    sent_pre_ref[...] = 0.5 * dot(rows, node_inner_ref[0:width, :])
+
+
+def node_update(placing_ref, message, table, pre, node_inner_ref, node_outer_ref):
+    width = table.shape[1]
+    summed = dot(placing_ref[...], message)
+    pre = pre + dot((0.5 * summed).astype(bf16), node_inner_ref[width:, :])
+    change = normalised(dot(silu_of_twice(pre), node_outer_ref[...]))
+    return (table.astype(f32) + change).astype(bf16)
+
+
+def message_kernel(
     block,
-    odd_ref,
-    count_ref,
-    sends_ref,
-    senders_ref,
-    receivers_ref,
+    choice_ref,
+    sent_placing_ref,
     pre_ref,
     pair_in_ref,
     cross_in_ref,
-    table_ref,
+    pair_ref,
+    cross_ref,
     inner_ref,
     outer_ref,
-    node_pre_ref,
+    sent_pre_ref,
     node_inner_ref,
     node_outer_ref,
-    updated_ref,
-    pair_ref,
-    cross_ref,
+    message_ref,
+    pair_out_ref,
+    cross_out_ref,
     halo_ref,
 ):
-    odd = odd_ref[0] == 1
-    nodes, width = table_ref.shape
-    halo = pair_in_ref.shape[0]
+    halo = pair_ref.shape[0]
     halo_ref[...] = halo_projection(pair_in_ref, cross_in_ref, inner_ref)
-    summed = None
     for at in range(0, pre_ref.shape[0], block):
         rows = slice(at, at + block)
-        slots = halo_slots(columns(senders_ref, at, block), nodes, halo, odd)
-        total = pre_ref[rows, :] + dot(chosen(slots, 2 * halo), halo_ref[...])
-        message = normalised(dot(silu_of_twice(total), outer_ref[...])).astype(bf16)
-        position = at + lax.broadcasted_iota(jnp.int32, (1, block), 1)
-        target = jnp.where(position < count_ref[0], receivers_ref[rows][None], -1)
-        part = dot(placed(target, nodes), message)
-        summed = part if summed is None else summed + part
-    pre = node_pre_ref[...] + dot((0.5 * summed).astype(bf16), node_inner_ref[width:, :])
-    change = normalised(dot(silu_of_twice(pre), node_outer_ref[...]))
-    updated = (table_ref[...].astype(f32) + change).astype(bf16)
-    updated_ref[...] = updated
-    pick_sends(sends_ref, odd, updated, pair_ref, cross_ref)
-
-
-def grid_own_kernel(block, senders_ref, table_ref, edge_ref, inner_ref, outer_ref, pre_ref, outer_out_ref, sent_ref):
+        total = pre_ref[rows, :] + dot(choice_ref[rows, :], halo_ref[...])
+        message_ref[rows, :] = normalised(dot(silu_of_twice(total), outer_ref[...])).astype(bf16)
+    table = jnp.concatenate([pair_ref[...], cross_ref[...]], 0)
+    updated = node_update(
+        sent_placing_ref, message_ref[...], table, sent_pre_ref[...], node_inner_ref, node_outer_ref
+    )
+    pair_out_ref[...] = updated[:halo]
+    cross_out_ref[...] = updated[halo:]
+
+
+def grid_own_kernel(
+    block,
+    halo,
+    odd_ref,
+    senders_ref,
+    placing_ref,
+    message_ref,
+    table_ref,
+    node_inner_ref,
+    node_outer_ref,
+    edge_ref,
+    inner_ref,
+    outer_ref,
+    pre_ref,
+    outer_out_ref,
+    choice_ref,
+    sent_ref,
+):
     nodes, width = table_ref.shape
-    sent_ref[...] = dot(table_ref[...], inner_ref[0:width, :]).astype(bf16)
+    table = table_ref[...]
+    pre = 0.5 * dot(table, node_inner_ref[0:width, :])
+    updated = node_update(placing_ref, message_ref[...], table, pre, node_inner_ref, node_outer_ref)
+    sent_ref[...] = dot(updated, inner_ref[0:width, :]).astype(bf16)
     for at in range(0, edge_ref.shape[0], block):
         rows = slice(at, at + block)
         total = dot(edge_ref[rows, :], inner_ref[width:, :])
         total += dot(chosen(columns(senders_ref, at, block), nodes), sent_ref[...])
         pre_ref[rows, :] = 0.5 * total
     outer_out_ref[...] = centred_weight(outer_ref)
+    halo_choice(senders_ref, nodes, halo, odd_ref[0] == 1, choice_ref)
 
 
 def grid_kernel(
     block,
-    nodes,
-    odd_ref,
-    senders_ref,
+    choice_ref,
     pre_ref,
     pair_in_ref,
     cross_in_ref,
@@ -188,14 +239,11 @@
     halo_ref,
     message_ref,
 ):
-    odd = odd_ref[0] == 1
-    halo = pair_in_ref.shape[0]
     halo_ref[...] = halo_projection(pair_in_ref, cross_in_ref, inner_ref)
     points = block // 3
     for at in range(0, pre_ref.shape[0], block):
         rows = slice(at, at + block)
-        slots = halo_slots(columns(senders_ref, at, block), nodes, halo, odd)
-        total = pre_ref[rows, :] + dot(chosen(slots, 2 * halo), halo_ref[...])
+        total = pre_ref[rows, :] + dot(choice_ref[rows, :], halo_ref[...])
         message = normalised(dot(silu_of_twice(total), outer_ref[...]))
         tiles = []
         for t in range(message_ref.shape[0]):
@@ -216,15 +264,27 @@
     return values * lax.rsqrt(values * values + smooth * smooth)
 
 
-def score_kernel(channel_ref, area_ref, difference_ref, everyone_ref, out_ref):
+def score_kernel(channel_ref, area_ref, difference_ref, *refs):
+    *others, partial_ref, weight_ref = refs
     difference = difference_ref[...]
-    members = everyone_ref.shape[0]
-    pairwise = smooth_slope(difference - everyone_ref[0].astype(f32))
-    for n in range(1, members):
-        pairwise += smooth_slope(difference - everyone_ref[n].astype(f32))
-    result = smooth_slope(difference) - pairwise / (members - 1)
-    weight = jnp.transpose(jnp.broadcast_to(channel_ref[...], (8, channel_ref.shape[1])))[:, :1]
-    out_ref[:, 0, :] = result * weight * area_ref[...]
+    members = 2 * len(others)
+    pairwise = smooth_slope(difference - difference)
+    for other_ref in others:
+        pairwise += smooth_slope(difference - other_ref[...].astype(f32))
+    channel = jnp.broadcast_to(channel_ref[...], (8, channel_ref.shape[1]))
+    weight = jnp.transpose(channel)[:, :1] * area_ref[...]
+    partial_ref[...] = (smooth_slope(difference) - pairwise / (members - 1)) * weight
+    weight_ref[...] = weight / (members - 1)
+
+
+def finish_kernel(difference_ref, partial_ref, weight_ref, *refs):
+    *others, out_ref = refs
+    difference = difference_ref[...]
+    pairwise = None
+    for other_ref in others:
+        part = smooth_slope(difference - other_ref[...].astype(f32))
+        pairwise = part if pairwise is None else pairwise + part
+    out_ref[:, 0, :] = partial_ref[...] - pairwise * weight_ref[...]
 
 
 def spec():
@@ -268,6 +328,20 @@
             cross.append((m * bands + i, other[0] * bands + other[1]))
     crossed = lax.ppermute(cross_rows, ("mem", "patch"), cross)
     return lax.ppermute(pair_rows, "patch", pair), crossed
+
+
+def mate(rows):
+    members = lax.axis_size("mem")
+    return lax.ppermute(rows, "mem", [(m, m ^ 1) for m in range(members)])
+
+
+def chip_mates(rows):
+    members = lax.axis_size("mem")
+    far_own = [
+        lax.ppermute(rows, "mem", [(m, (m + shift) % members) for m in range(members)])
+        for shift in range(2, members, 2)
+    ]
+    return mate(rows), far_own
 
 
 def per_device(
@@ -302,8 +376,6 @@
     senders = edge_senders
     receivers = edge_receivers
     grid_rows = grid_senders
-    block = 512
-    grid_block = 768
 
     pair, cross = call(
         select_kernel,
@@ -311,72 +383,107 @@
         (odd,),
         tuple(pltpu.with_memory_space_constraint(x, pltpu.HBM) for x in (sends, latent)),
         (shape(halo, width), shape(halo, width)),
-        (VMEM((2, halo), jnp.int32), VMEM((nodes, width), bf16), pltpu.SemaphoreType.DMA((2,))),
+        (VMEM((2, halo), jnp.int32), VMEM((nodes, width), bf16), pltpu.SemaphoreType.DMA((3,))),
         10**10,
         from_hbm=True,
     )
     pair_in, cross_in = exchange(pair, cross)
-    pre, node_pre, outer, second = call(
-        lambda *refs: edge_own_kernel(block, *refs),
+    pre, sent_pre, outer, second, choice, placing, sent_placing = call(
+        lambda *refs: edge_own_kernel(edges // 2, *refs),
         "edge_own",
-        (),
-        (senders, receivers, latent, edge_latent, edge_inner, edge_outer, node_inner, node_outer),
+        (odd,),
+        (
+            edge_count,
+            sends,
+            senders,
+            receivers,
+            pair,
+            cross,
+            latent,
+            edge_latent,
+            edge_inner,
+            edge_outer,
+            node_inner,
+            node_outer,
+        ),
         (
             shape(edges, width, dtype=f32),
-            shape(nodes, width, dtype=f32),
+            shape(2 * halo, width, dtype=f32),
             shape(width, width),
             shape(width, width),
+            shape(edges, 2 * halo),
+            shape(nodes, edges),
+            shape(2 * halo, edges),
         ),
         (VMEM((nodes, width), bf16), VMEM((nodes, width), bf16)),
         10**10,
     )
-    updated, pair, cross = call(
-        lambda *refs: node_kernel(block, *refs),
-        "node",
-        (odd, edge_count),
+    message, pair, cross = call(
+        lambda *refs: message_kernel(edges, *refs),
+        "message",
+        (),
         (
-            sends,
-            senders,
-            receivers,
+            choice,
+            sent_placing,
             pre,
             pair_in,
             cross_in,
-            latent,
+            pair,
+            cross,
             edge_inner,
             outer,
-            node_pre,
+            sent_pre,
             node_inner,
             second,
         ),
-        (shape(nodes, width), shape(halo, width), shape(halo, width)),
+        (shape(edges, width), shape(halo, width), shape(halo, width)),
         (VMEM((2 * halo, width), bf16),),
         10**10,
     )
     pair_in, cross_in = exchange(pair, cross)
-    pre, outer = call(
-        lambda *refs: grid_own_kernel(grid_block, *refs),
+    pre, outer, choice = call(
+        lambda *refs: grid_own_kernel(grid_edges // 2, halo, *refs),
         "grid_own",
-        (),
-        (grid_rows, updated, grid_edge_latent, grid_inner, grid_outer),
-        (shape(grid_edges, width, dtype=f32), shape(width, width)),
+        (odd,),
+        (
+            grid_rows,
+            placing,
+            message,
+            latent,
+            node_inner,
+            second,
+            grid_edge_latent,
+            grid_inner,
+            grid_outer,
+        ),
+        (shape(grid_edges, width, dtype=f32), shape(width, width), shape(grid_edges, 2 * halo)),
         (VMEM((nodes, width), bf16),),
         10**10,
     )
     difference, rounded = call(
-        lambda *refs: grid_kernel(grid_block, nodes, *refs),
+        lambda *refs: grid_kernel(grid_edges, *refs),
         "grid",
-        (odd,),
-        (grid_rows, pre, pair_in, cross_in, grid_inner, outer, out_weight, prior_state, target),
+        (),
+        (choice, pre, pair_in, cross_in, grid_inner, outer, out_weight, prior_state, target),
         (shape(channels, points, dtype=f32), shape(channels, points)),
         (VMEM((2 * halo, width), bf16), VMEM((width // LANES, grid_edges, LANES), f32)),
         10**10,
     )
-    everyone = lax.all_gather(rounded[None], "mem", axis=0, tiled=True)
-    (gradient,) = call(
+    near, far_own = chip_mates(rounded)
+    partial, weight = call(
         score_kernel,
         "score",
         (),
-        (channel_weight[None], area_weight[None], difference, everyone),
+        (channel_weight[None], area_weight[None], difference, near, *far_own),
+        (shape(channels, points, dtype=f32), shape(channels, points, dtype=f32)),
+        (),
+        10**8,
+    )
+    (gradient,) = call(
+        finish_kernel,
+        "finish",
+        (),
+        (difference, partial, weight, *(mate(rows) for rows in far_own)),
         (shape(channels, 1, points, dtype=f32),),
         (),
         10**7,

time: 29.3 us -> 27.2 us (0.928)
  blocking collectives: 8.92 us -> 0 us
  starting transfers between devices: 3.03 us -> 10.6 us
  waiting for transfers between devices: 3 us -> 1.75 us
  Pallas kernels: 13.2 us -> 13.7 us
    all_gather x1 -> x0, blocking collectives: 8.92 us -> none  [per_device(): everyone = lax.all_gather(rounded[None], 'mem', axis=0, tiled=True)]
    ppermute x0 -> x3, starting transfers between devices: none -> 7.15 us  [the longest x2 5.85 us: mate(): return lax.ppermute(rows, 'mem', [(m, m ^ 1) for m in range(members)])]
    ppermute x2, waiting for transfers between devices: 2.99 us -> 1.04 us  [exchange(): crossed = lax.ppermute(cross_rows, ('mem', 'patch'), cross)]
    ppermute x0 -> x3, waiting for transfers between devices: none -> 0.71 us  [the longest x2 0.71 us: mate(): return lax.ppermute(rows, 'mem', [(m, m ^ 1) for m in range(members)])]
    pallas_call x6 -> x7, Pallas kernels: 13.2 us -> 13.7 us  [call(): pl.pallas_call(kernel, name=name, out_shape=outs, in_specs=[scalar()] * l...]
    ppermute x2, starting transfers between devices: 2.89 us -> 3.26 us  [exchange(): return (lax.ppermute(pair_rows, 'patch', pair), crossed)]
  transfers between devices with their start and end apart: 4 -> 7, of which waited for: 2 -> 3; matrix products, arithmetic and copies ran while one was open for 0% -> 0% of each run, Pallas kernels for 17% -> 26%
where the time goes in v3:
time: 27.2 us; the launch traced here: 26.9 us
  Pallas kernels  13.7 us (50%)
  starting transfers between devices  10.6 us (39%)
  waiting for transfers between devices  1.75 us (6%)
  between operations  0.91 us (3%)
    pallas_call x7, Pallas kernels, call(): pl.pallas_call(kernel, name=name, out_shape=outs, in_specs=[scalar()] * l...  13.7 us
    ppermute x2, starting transfers between devices, mate(): return lax.ppermute(rows, 'mem', [(m, m ^ 1) for m in range(members)])  5.85 us
    ppermute x2, starting transfers between devices, exchange(): return (lax.ppermute(pair_rows, 'patch', pair), crossed)  3.26 us
    ppermute x1, starting transfers between devices, chip_mates(): lax.ppermute(rows, 'mem', [(m, (m + shift) % members) for m in range(memb...  1.3 us
    ppermute x2, waiting for transfers between devices, exchange(): crossed = lax.ppermute(cross_rows, ('mem', 'patch'), cross)  1.04 us
    ppermute x2, waiting for transfers between devices, mate(): return lax.ppermute(rows, 'mem', [(m, m ^ 1) for m in range(members)])  0.71 us
  transfers between devices with their start and end apart: 7, of which 3 were waited for; matrix products, arithmetic and copies ran while one was open for 0% of the time, Pallas kernels for 26%

profile of v3, /device:TPU:17, one launch (start us, length us, event | category | flops | bytes accessed | tf_op | source)
XLA Modules:
  0.0 26.9 jit_solution(11406483767471948960)
XLA Ops:
  0.0 0.0 copy-start.5
  0.0 0.0 copy-start.6
  0.0 0.0 copy-start.7
  0.0 0.0 copy-start.13
  0.0 0.0 copy-start.14
  0.1 1.5 %select.3 = (bf16[96,512]{1,0:T(8,128)(2,1)S(1)}, bf16[96,512]{1,0:T(8,128)(2,1)S(1)}) custom-call(s32[1]{0:T(128)} %bitcast.odd_ref.refs_0_, s32[2,96]{1,0:T(2,128)} %bitcast.10, bf16[512,512]{1,0:T(8,128)(2,1)} %bitcast.6), custom_call_target="tpu_custom_call" | custom-call | flops 10000000000 | bytes 721664 | tf_op jit(solution)/shard_map/select/pallas_call | solution.py:308
  1.6 1.3 %collective-permute-start = (bf16[96,512]{1,0:T(8,128)(2,1)S(1)}, bf16[96,512]{1,0:T(8,128)(2,1)S(1)}, u32[]{:S(2)}, u32[]{:S(2)}) collective-permute-start(bf16[96,512]{1,0:T(8,128)(2,1)S(1)} %get-tuple-element.24.refs_5_), channel_id=1, source_target_pairs={{0,1},{1,0},{2,3},{3,2},{4,5},{5,4},{6,7},{7,6},{8,9},{9,8},{10,11... | collective-permute-start | bytes 294920 | tf_op jit(solution)/shard_map/ppermute | solution.py:330
  2.9 0.1 collective-permute-start.1
  3.8 3.1 %edge_own.1 = (f32[1024,512]{1,0:T(8,128)S(1)}, f32[192,512]{1,0:T(8,128)S(1)}, bf16[512,512]{1,0:T(8,128)(2,1)S(1)}, bf16[512,512]{1,0:T(8,128)(2,1)S(1)}, bf16...) custom-call(s32[1]{0:T(128)} %bitcast.odd_ref.refs_0_, ...), custom_call_target="tpu_custom_call" | custom-call | flops 10000000000 | bytes 10822404 | tf_op jit(solution)/shard_map/edge_own/pallas_call | solution.py:308
  6.9 0.0 collective-permute-done.refs_3_
  6.9 0.5 %collective-permute-done.1.refs_4_ = bf16[96,512]{1,0:T(8,128)(2,1)S(1)} collective-permute-done((bf16[96,512]{1,0:T(8,128)(2,1)S(1)}, bf16[96,512]{1,0:T(8,128)(2,1)S(1)}, u32[]{:S(2)}, u32[]{:S(2)}) %collective-permute-start.1) | collective-permute-done | bytes 98336 | tf_op jit(solution)/shard_map/ppermute | solution.py:329
  7.3 2.0 %message.1 = (bf16[1024,512]{1,0:T(8,128)(2,1)S(1)}, bf16[96,512]{1,0:T(8,128)(2,1)S(1)}, bf16[96,512]{1,0:T(8,128)(2,1)S(1)}) custom-call(bf16[1024,192]{1,0:T(8,128)(2,1)S(1)} %get-tuple-element.27.refs_0_, bf16[192,1024]{1,0:T(8,128)(2,1)S(1)} %get-tuple-element.28.refs_1_, f32[1024,512]{1,0:T(8,128)S(1)} %get-tuple-element.29.refs_2_, ...), custom_call_target="tpu_custom_call" | custom-call | flops 10000000000 | bytes 8585216 | tf_op jit(solution)/shard_map/message/pallas_call | solution.py:308
  9.4 2.0 %collective-permute-start.2 = (bf16[96,512]{1,0:T(8,128)(2,1)S(1)}, bf16[96,512]{1,0:T(8,128)(2,1)S(1)}, u32[]{:S(2)}, u32[]{:S(2)}) collective-permute-start(bf16[96,512]{1,0:T(8,128)(2,1)S(1)} %get-tuple-element.36), channel_id=1, source_target_pairs={{0,1},{1,0},{2,3},{3,2},{4,5},{5,4},{6,7},{7,6},{8,9},{9,8},{10,11... | collective-permute-start | bytes 294920 | tf_op jit(solution)/shard_map/ppermute | solution.py:330
  11.4 0.0 collective-permute-start.3
  11.4 0.0 copy-start.9
  11.4 0.0 copy-start.10
  11.4 0.0 copy-start.11
  11.4 3.8 %grid_own.1 = (f32[1536,512]{1,0:T(8,128)S(1)}, bf16[512,512]{1,0:T(8,128)(2,1)S(1)}, bf16[1536,192]{1,0:T(8,128)(2,1)S(1)}) custom-call(s32[1]{0:T(128)} %bitcast.odd_ref.refs_0_, s32[1536]{0:T(1024)S(1)} %copy-done.12, bf16[512,1024]{1,0:T(8,128)(2,1)S(1)} %get-tuple-element.26.refs_2_, bf16[1024,512]{1,0:T(8,128)(2,1)S(1)} %get-tuple-element.33.refs_3_, ...), custom_call_target="tpu_custom_call" | custom-call | flops 10000000000 | bytes 11606016 | tf_op jit(solution)/shard_map/grid_own/pallas_call | solution.py:308
  15.3 0.0 collective-permute-done.2.refs_2_
  15.3 0.6 %collective-permute-done.3.refs_3_ = bf16[96,512]{1,0:T(8,128)(2,1)S(1)} collective-permute-done((bf16[96,512]{1,0:T(8,128)(2,1)S(1)}, bf16[96,512]{1,0:T(8,128)(2,1)S(1)}, u32[]{:S(2)}, u32[]{:S(2)}) %collective-permute-start.3) | collective-permute-done | bytes 98336 | tf_op jit(solution)/shard_map/ppermute | solution.py:329
  15.8 0.0 copy-done.10
  15.9 0.0 copy-start.15
  15.9 0.0 copy-start.17
  15.9 2.2 %grid.1 = (f32[87,512]{1,0:T(8,128)S(1)}, bf16[87,512]{1,0:T(8,128)(2,1)S(1)}) custom-call(bf16[1536,192]{1,0:T(8,128)(2,1)S(1)} %get-tuple-element.34.refs_0_, f32[1536,512]{1,0:T(8,128)S(1)} %get-tuple-element.35.refs_1_, bf16[96,512]{1,0:T(8,128)(2,1)S(1)} %collective-permute-done.2.refs_2_, bf16[96,512]{1,0:T(8,128)(2,1)S(1)} %collective-permute-done.3.refs_3_, ...), custom_call_target="tpu_custom_call" | custom-call | flops 10000000000 | bytes 6217728 | tf_op jit(solution)/shard_map/grid/pallas_call | solution.py:308
  18.1 1.3 %collective-permute-start.5 = (bf16[87,512]{1,0:T(8,128)(2,1)S(1)}, bf16[87,512]{1,0:T(8,128)(2,1)S(1)}, u32[]{:S(2)}, u32[]{:S(2)}) collective-permute-start(bf16[87,512]{1,0:T(8,128)(2,1)S(1)} %get-tuple-element.40), channel_id=1, source_target_pairs={{0,16},{8,24},{16,0},{24,8},{1,17},{9,25},{17,1},{25,9},{2,18},{10... | collective-permute-start | bytes 267272 | tf_op jit(solution)/shard_map/ppermute | solution.py:341
  19.4 2.8 %collective-permute-start.4 = (bf16[87,512]{1,0:T(8,128)(2,1)S(1)}, bf16[87,512]{1,0:T(8,128)(2,1)S(1)}, u32[]{:S(2)}, u32[]{:S(2)}) collective-permute-start(bf16[87,512]{1,0:T(8,128)(2,1)S(1)} %get-tuple-element.40), channel_id=1, source_target_pairs={{0,8},{8,0},{16,24},{24,16},{1,9},{9,1},{17,25},{25,17},{2,10},{10... | collective-permute-start | bytes 267272 | tf_op jit(solution)/shard_map/ppermute | solution.py:335
  22.2 0.0 collective-permute-done.5.refs_1_
  22.2 3.0 %collective-permute-start.6 = (bf16[87,512]{1,0:T(8,128)(2,1)S(1)}, bf16[87,512]{1,0:T(8,128)(2,1)S(1)}, u32[]{:S(2)}, u32[]{:S(2)}) collective-permute-start(bf16[87,512]{1,0:T(8,128)(2,1)S(1)} %collective-permute-done.5.refs_1_), channel_id=1, source_target_pairs={{0,8},{8,0},{16,24},{24,16},{1,9},{9,1},{17,25},{25,17},{2,10},{10... | collective-permute-start | bytes 267272 | tf_op jit(solution)/shard_map/ppermute | solution.py:335
  25.3 0.0 collective-permute-done.4.refs_0_
  25.3 0.2 score.1
  25.5 0.7 %collective-permute-done.6.refs_0_ = bf16[87,512]{1,0:T(8,128)(2,1)S(1)} collective-permute-done((bf16[87,512]{1,0:T(8,128)(2,1)S(1)}, bf16[87,512]{1,0:T(8,128)(2,1)S(1)}, u32[]{:S(2)}, u32[]{:S(2)}) %collective-permute-start.6) | collective-permute-done | bytes 89120 | tf_op jit(solution)/shard_map/ppermute | solution.py:335
  26.2 0.8 %finish.1 = f32[87,1,512]{2,1,0:T(1,128)} custom-call(f32[87,512]{1,0:T(8,128)S(1)} %get-tuple-element.39.difference_ref, f32[87,512]{1,0:T(8,128)S(1)} %get-tuple-element.41.partial_ref, f32[87,512]{1,0:T(8,128)S(1)} %get-tuple-element.42.weight_ref, bf16[87,512]{1,0:T(8,128)(2,1)S(1)} %collective-permute-done.6.refs_0_), custom_call_target="tpu_custom_call" | custom-call | flops 10000000 | bytes 801792 | tf_op jit(solution)/shard_map/finish/pallas_call | solution.py:308
  (25 shorter events, 0.0 us)
Async XLA Ops:
  0.0 3.7 %copy-start = (bf16[1536,512]{1,0:T(8,128)(2,1)S(1)}, bf16[1536,512]{1,0:T(8,128)(2,1)}, u32[]{:S(2)}) copy-start(bf16[1536,512]{1,0:T(8,128)(2,1)} %refs_7_.3) | copy-start | bytes 4718596
  0.0 3.7 %copy-start.2 = (bf16[1024,512]{1,0:T(8,128)(2,1)S(1)}, bf16[1024,512]{1,0:T(8,128)(2,1)}, u32[]{:S(2)}) copy-start(bf16[1024,512]{1,0:T(8,128)(2,1)} %refs_8_.3) | copy-start | bytes 3145732
  0.0 3.7 %copy-start.3 = (bf16[1024,512]{1,0:T(8,128)(2,1)S(1)}, bf16[1024,512]{1,0:T(8,128)(2,1)}, u32[]{:S(2)}) copy-start(bf16[1024,512]{1,0:T(8,128)(2,1)} %refs_5_.1) | copy-start | bytes 3145732
  0.0 3.7 %copy-start.5 = (bf16[512,512]{1,0:T(8,128)(2,1)S(1)}, bf16[512,512]{1,0:T(8,128)(2,1)}, u32[]{:S(2)}) copy-start(bf16[512,512]{1,0:T(8,128)(2,1)} %refs_10_.2) | copy-start | bytes 1572868
  0.0 3.7 %copy-start.6 = (bf16[512,512]{1,0:T(8,128)(2,1)S(1)}, bf16[512,512]{1,0:T(8,128)(2,1)}, u32[]{:S(2)}) copy-start(bf16[512,512]{1,0:T(8,128)(2,1)} %refs_12_.1) | copy-start | bytes 1572868
  0.0 3.7 %copy-start.7 = (bf16[1,512,512]{2,1,0:T(8,128)(2,1)S(1)}, bf16[1,512,512]{2,1,0:T(8,128)(2,1)}, u32[]{:S(2)}) copy-start(bf16[1,512,512]{2,1,0:T(8,128)(2,1)} %param.19) | copy-start | bytes 1572868
  0.0 3.7 %copy-start.13 = (s32[1024]{0:T(1024)S(1)}, s32[1024]{0:T(1024)}, u32[]{:S(2)}) copy-start(s32[1024]{0:T(1024)} %refs_3_.1) | copy-start | bytes 12292
  0.0 3.7 %copy-start.14 = (s32[1024]{0:T(1024)S(1)}, s32[1024]{0:T(1024)}, u32[]{:S(2)}) copy-start(s32[1024]{0:T(1024)} %refs_4_.2) | copy-start | bytes 12292
  0.1 3.7 %copy-start.16 = (s32[1,2,96]{2,1,0:T(2,128)S(1)}, s32[1,2,96]{2,1,0:T(2,128)}, u32[]{:S(2)}) copy-start(s32[1,2,96]{2,1,0:T(2,128)} %param.33) | copy-start | bytes 2308
  1.6 5.2 %collective-permute-start = (bf16[96,512]{1,0:T(8,128)(2,1)S(1)}, bf16[96,512]{1,0:T(8,128)(2,1)S(1)}, u32[]{:S(2)}, u32[]{:S(2)}) collective-permute-start(bf16[96,512]{1,0:T(8,128)(2,1)S(1)} %get-tuple-element.24.refs_5_), channel_id=1, source_target_pairs={{0,1},{1,0},{2,3},{3,2},{4,5},{5,4},{6,7},{7,6},{8,9},{9,8},{10,11... | collective-permute-start | bytes 294920 | tf_op jit(solution)/shard_map/ppermute | solution.py:330
  2.9 4.4 %collective-permute-start.1 = (bf16[96,512]{1,0:T(8,128)(2,1)S(1)}, bf16[96,512]{1,0:T(8,128)(2,1)S(1)}, u32[]{:S(2)}, u32[]{:S(2)}) collective-permute-start(bf16[96,512]{1,0:T(8,128)(2,1)S(1)} %get-tuple-element.25.refs_6_), channel_id=1, source_target_pairs={{0,8},{1,2},{2,1},{3,4},{4,3},{5,6},{6,5},{7,15},{8,0},{9,10},{10,... | collective-permute-start | bytes 294920 | tf_op jit(solution)/shard_map/ppermute | solution.py:329
  7.3 4.1 %copy-start.1 = (bf16[1536,512]{1,0:T(8,128)(2,1)S(1)}, bf16[1536,512]{1,0:T(8,128)(2,1)}, u32[]{:S(2)}) copy-start(bf16[1536,512]{1,0:T(8,128)(2,1)} %refs_7_.4) | copy-start | bytes 4718596
  7.3 4.1 %copy-start.4 = (bf16[1024,512]{1,0:T(8,128)(2,1)S(1)}, bf16[1024,512]{1,0:T(8,128)(2,1)}, u32[]{:S(2)}) copy-start(bf16[1024,512]{1,0:T(8,128)(2,1)} %refs_4_.3) | copy-start | bytes 3145732
  7.3 4.1 %copy-start.8 = (bf16[512,512]{1,0:T(8,128)(2,1)S(1)}, bf16[512,512]{1,0:T(8,128)(2,1)}, u32[]{:S(2)}) copy-start(bf16[512,512]{1,0:T(8,128)(2,1)} %refs_9_.3) | copy-start | bytes 1572868
  7.3 4.1 %copy-start.12 = (s32[1536]{0:T(1024)S(1)}, s32[1536]{0:T(1024)}, u32[]{:S(2)}) copy-start(s32[1536]{0:T(1024)} %refs_1_.2) | copy-start | bytes 18436
  9.4 5.9 %collective-permute-start.2 = (bf16[96,512]{1,0:T(8,128)(2,1)S(1)}, bf16[96,512]{1,0:T(8,128)(2,1)S(1)}, u32[]{:S(2)}, u32[]{:S(2)}) collective-permute-start(bf16[96,512]{1,0:T(8,128)(2,1)S(1)} %get-tuple-element.36), channel_id=1, source_target_pairs={{0,1},{1,0},{2,3},{3,2},{4,5},{5,4},{6,7},{7,6},{8,9},{9,8},{10,11... | collective-permute-start | bytes 294920 | tf_op jit(solution)/shard_map/ppermute | solution.py:330
  11.4 4.5 %collective-permute-start.3 = (bf16[96,512]{1,0:T(8,128)(2,1)S(1)}, bf16[96,512]{1,0:T(8,128)(2,1)S(1)}, u32[]{:S(2)}, u32[]{:S(2)}) collective-permute-start(bf16[96,512]{1,0:T(8,128)(2,1)S(1)} %get-tuple-element.37), channel_id=1, source_target_pairs={{0,8},{1,2},{2,1},{3,4},{4,3},{5,6},{6,5},{7,15},{8,0},{9,10},{10,... | collective-permute-start | bytes 294920 | tf_op jit(solution)/shard_map/ppermute | solution.py:329
  11.4 4.4 %copy-start.9 = (f32[87,512]{1,0:T(8,128)S(1)}, f32[87,512]{1,0:T(8,128)}, u32[]{:S(2)}) copy-start(f32[87,512]{1,0:T(8,128)} %refs_7_.5) | copy-start | bytes 534532
  11.4 4.4 %copy-start.10 = (f32[87,512]{1,0:T(8,128)S(1)}, f32[87,512]{1,0:T(8,128)}, u32[]{:S(2)}) copy-start(f32[87,512]{1,0:T(8,128)} %refs_8_.5) | copy-start | bytes 534532
  11.4 4.4 %copy-start.11 = (bf16[87,512]{1,0:T(8,128)(2,1)S(1)}, bf16[87,512]{1,0:T(8,128)(2,1)}, u32[]{:S(2)}) copy-start(bf16[87,512]{1,0:T(8,128)(2,1)} %refs_6_.1) | copy-start | bytes 267268
  15.9 9.4 %copy-start.15 = (f32[512]{0:T(512)S(1)}, f32[512]{0:T(512)}, u32[]{:S(2)}) copy-start(f32[512]{0:T(512)} %param.32) | copy-start | bytes 6148
  15.9 9.4 %copy-start.17 = (f32[87]{0:T(128)S(1)}, f32[87]{0:T(128)}, u32[]{:S(2)}) copy-start(f32[87]{0:T(128)} %param.31) | copy-start | bytes 1048
  18.1 4.1 %collective-permute-start.5 = (bf16[87,512]{1,0:T(8,128)(2,1)S(1)}, bf16[87,512]{1,0:T(8,128)(2,1)S(1)}, u32[]{:S(2)}, u32[]{:S(2)}) collective-permute-start(bf16[87,512]{1,0:T(8,128)(2,1)S(1)} %get-tuple-element.40), channel_id=1, source_target_pairs={{0,16},{8,24},{16,0},{24,8},{1,17},{9,25},{17,1},{25,9},{2,18},{10... | collective-permute-start | bytes 267272 | tf_op jit(solution)/shard_map/ppermute | solution.py:341
  19.4 5.9 %collective-permute-start.4 = (bf16[87,512]{1,0:T(8,128)(2,1)S(1)}, bf16[87,512]{1,0:T(8,128)(2,1)S(1)}, u32[]{:S(2)}, u32[]{:S(2)}) collective-permute-start(bf16[87,512]{1,0:T(8,128)(2,1)S(1)} %get-tuple-element.40), channel_id=1, source_target_pairs={{0,8},{8,0},{16,24},{24,16},{1,9},{9,1},{17,25},{25,17},{2,10},{10... | collective-permute-start | bytes 267272 | tf_op jit(solution)/shard_map/ppermute | solution.py:335
  22.2 3.9 %collective-permute-start.6 = (bf16[87,512]{1,0:T(8,128)(2,1)S(1)}, bf16[87,512]{1,0:T(8,128)(2,1)S(1)}, u32[]{:S(2)}, u32[]{:S(2)}) collective-permute-start(bf16[87,512]{1,0:T(8,128)(2,1)S(1)} %collective-permute-done.5.refs_1_), channel_id=1, source_target_pairs={{0,8},{8,0},{16,24},{24,16},{1,9},{9,1},{17,25},{25,17},{2,10},{10... | collective-permute-start | bytes 267272 | tf_op jit(solution)/shard_map/ppermute | solution.py:335

commit v4 on v3

--- a/solution.py
+++ b/solution.py
@@ -120,7 +120,7 @@
     outer_out_ref,
     node_outer_out_ref,
     choice_ref,
-    placing_ref,
+    live_ref,
     sent_placing_ref,
     sent_ref,
     got_ref,
@@ -129,6 +129,15 @@
     edges = edge_ref.shape[0]
     halo = pair_ref.shape[0]
     odd = odd_ref[0] == 1
+    outer_out_ref[...] = centred_weight(outer_ref)
+    node_outer_out_ref[...] = centred_weight(node_outer_ref)
+    halo_choice(senders_ref, nodes, halo, odd, choice_ref)
+    position = lax.broadcasted_iota(jnp.int32, (1, edges), 1)
+    target = jnp.where(position < count_ref[...][None], receivers_ref[...][None], -1)
+    live_ref[...] = target
+    pair, cross = send_index(sends_ref, odd)
+    index = jnp.concatenate([column(pair), column(cross)], 0)
+    sent_placing_ref[...] = jnp.where(index == target, 1.0, 0.0).astype(bf16)
     sent_ref[...] = dot(table_ref[...], inner_ref[0:width, :]).astype(bf16)
     got_ref[...] = dot(table_ref[...], inner_ref[width : 2 * width, :]).astype(bf16)
     for at in range(0, edges, block):
@@ -137,22 +146,13 @@
         total += dot(chosen(columns(senders_ref, at, block), nodes), sent_ref[...])
         total += dot(chosen(columns(receivers_ref, at, block), nodes), got_ref[...])
         pre_ref[rows, :] = 0.5 * total
-    outer_out_ref[...] = centred_weight(outer_ref)
-    node_outer_out_ref[...] = centred_weight(node_outer_ref)
-    halo_choice(senders_ref, nodes, halo, odd, choice_ref)
-    position = lax.broadcasted_iota(jnp.int32, (1, edges), 1)
-    target = jnp.where(position < count_ref[...][None], receivers_ref[...][None], -1)
-    placing_ref[...] = placed(target, nodes)
-    pair, cross = send_index(sends_ref, odd)
-    index = jnp.concatenate([column(pair), column(cross)], 0)
-    sent_placing_ref[...] = jnp.where(index == target, 1.0, 0.0).astype(bf16)
     rows = jnp.concatenate([pair_ref[...], cross_ref[...]], 0)
     sent_pre_ref[...] = 0.5 * dot(rows, node_inner_ref[0:width, :])
 
 
-def node_update(placing_ref, message, table, pre, node_inner_ref, node_outer_ref):
+def node_update(placing, message, table, pre, node_inner_ref, node_outer_ref):
     width = table.shape[1]
-    summed = dot(placing_ref[...], message)
+    summed = dot(placing, message)
     pre = pre + dot((0.5 * summed).astype(bf16), node_inner_ref[width:, :])
     change = normalised(dot(silu_of_twice(pre), node_outer_ref[...]))
     return (table.astype(f32) + change).astype(bf16)
@@ -185,7 +185,7 @@
         message_ref[rows, :] = normalised(dot(silu_of_twice(total), outer_ref[...])).astype(bf16)
     table = jnp.concatenate([pair_ref[...], cross_ref[...]], 0)
     updated = node_update(
-        sent_placing_ref, message_ref[...], table, sent_pre_ref[...], node_inner_ref, node_outer_ref
+        sent_placing_ref[...], message_ref[...], table, sent_pre_ref[...], node_inner_ref, node_outer_ref
     )
     pair_out_ref[...] = updated[:halo]
     cross_out_ref[...] = updated[halo:]
@@ -196,7 +196,7 @@
     halo,
     odd_ref,
     senders_ref,
-    placing_ref,
+    live_ref,
     message_ref,
     table_ref,
     node_inner_ref,
@@ -212,7 +212,7 @@
     nodes, width = table_ref.shape
     table = table_ref[...]
     pre = 0.5 * dot(table, node_inner_ref[0:width, :])
-    updated = node_update(placing_ref, message_ref[...], table, pre, node_inner_ref, node_outer_ref)
+    updated = node_update(placed(live_ref[...], nodes), message_ref[...], table, pre, node_inner_ref, node_outer_ref)
     sent_ref[...] = dot(updated, inner_ref[0:width, :]).astype(bf16)
     for at in range(0, edge_ref.shape[0], block):
         rows = slice(at, at + block)
@@ -388,8 +388,8 @@
         from_hbm=True,
     )
     pair_in, cross_in = exchange(pair, cross)
-    pre, sent_pre, outer, second, choice, placing, sent_placing = call(
-        lambda *refs: edge_own_kernel(edges // 2, *refs),
+    pre, sent_pre, outer, second, choice, live, sent_placing = call(
+        lambda *refs: edge_own_kernel(edges, *refs),
         "edge_own",
         (odd,),
         (
@@ -412,7 +412,7 @@
             shape(width, width),
             shape(width, width),
             shape(edges, 2 * halo),
-            shape(nodes, edges),
+            shape(1, edges, dtype=jnp.int32),
             shape(2 * halo, edges),
         ),
         (VMEM((nodes, width), bf16), VMEM((nodes, width), bf16)),
@@ -447,7 +447,7 @@
         (odd,),
         (
             grid_rows,
-            placing,
+            live,
             message,
             latent,
             node_inner,

time: 27.2 us -> 27 us (level)
  Pallas kernels: 13.7 us -> 13.3 us
  waiting for transfers between devices: 1.75 us -> 2.1 us
    ppermute x2, starting transfers between devices: 3.26 us -> 2.85 us  [exchange(): return (lax.ppermute(pair_rows, 'patch', pair), crossed)]
    ppermute x2, waiting for transfers between devices: 1.04 us -> 1.38 us  [exchange(): crossed = lax.ppermute(cross_rows, ('mem', 'patch'), cross)]
    pallas_call x7, Pallas kernels: 13.7 us -> 13.3 us  [call(): pl.pallas_call(kernel, name=name, out_shape=outs, in_specs=[scalar()] * l...]
  transfers between devices with their start and end apart: 7 -> 7, of which waited for: 3 -> 3; matrix products, arithmetic and copies ran while one was open for 0% -> 0% of each run, Pallas kernels for 26% -> 25%
where the time goes in v4:
time: 27 us; the launch traced here: 26.8 us
  Pallas kernels  13.3 us (49%)
  starting transfers between devices  10.4 us (39%)
  waiting for transfers between devices  2.1 us (8%)
  between operations  0.91 us (3%)
    pallas_call x7, Pallas kernels, call(): pl.pallas_call(kernel, name=name, out_shape=outs, in_specs=[scalar()] * l...  13.3 us
    ppermute x2, starting transfers between devices, mate(): return lax.ppermute(rows, 'mem', [(m, m ^ 1) for m in range(members)])  6.08 us
    ppermute x2, starting transfers between devices, exchange(): return (lax.ppermute(pair_rows, 'patch', pair), crossed)  2.85 us
    ppermute x2, waiting for transfers between devices, exchange(): crossed = lax.ppermute(cross_rows, ('mem', 'patch'), cross)  1.38 us
    ppermute x1, starting transfers between devices, chip_mates(): lax.ppermute(rows, 'mem', [(m, (m + shift) % members) for m in range(memb...  1.31 us
    ppermute x2, waiting for transfers between devices, mate(): return lax.ppermute(rows, 'mem', [(m, m ^ 1) for m in range(members)])  0.71 us
  transfers between devices with their start and end apart: 7, of which 3 were waited for; matrix products, arithmetic and copies ran while one was open for 0% of the time, Pallas kernels for 25%

profile of v4, /device:TPU:17, one launch (start us, length us, event | category | flops | bytes accessed | tf_op | source)
XLA Modules:
  0.0 26.8 jit_solution(15254445340961089005)
XLA Ops:
  0.1 1.5 %select.3 = (bf16[96,512]{1,0:T(8,128)(2,1)S(1)}, bf16[96,512]{1,0:T(8,128)(2,1)S(1)}) custom-call(s32[1]{0:T(128)} %bitcast.odd_ref.refs_0_, s32[2,96]{1,0:T(2,128)} %bitcast.10, bf16[512,512]{1,0:T(8,128)(2,1)} %bitcast.6), custom_call_target="tpu_custom_call" | custom-call | flops 10000000000 | bytes 721664 | tf_op jit(solution)/shard_map/select/pallas_call | solution.py:308
  1.6 1.3 %collective-permute-start = (bf16[96,512]{1,0:T(8,128)(2,1)S(1)}, bf16[96,512]{1,0:T(8,128)(2,1)S(1)}, u32[]{:S(2)}, u32[]{:S(2)}) collective-permute-start(bf16[96,512]{1,0:T(8,128)(2,1)S(1)} %get-tuple-element.24.refs_5_), channel_id=1, source_target_pairs={{0,1},{1,0},{2,3},{3,2},{4,5},{5,4},{6,7},{7,6},{8,9},{9,8},{10,11... | collective-permute-start | bytes 294920 | tf_op jit(solution)/shard_map/ppermute | solution.py:330
  2.9 0.1 collective-permute-start.1
  3.7 0.0 copy-done
  3.7 0.0 copy-done.2
  3.7 0.0 copy-done.3
  3.7 0.0 copy-done.5
  3.7 0.0 copy-done.6
  3.7 0.0 copy-done.7
  3.8 2.7 %edge_own.1 = (f32[1024,512]{1,0:T(8,128)S(1)}, f32[192,512]{1,0:T(8,128)S(1)}, bf16[512,512]{1,0:T(8,128)(2,1)S(1)}, bf16[512,512]{1,0:T(8,128)(2,1)S(1)}, bf16...) custom-call(s32[1]{0:T(128)} %bitcast.odd_ref.refs_0_, s32[1]{0:T(128)S(6)} %copy.20.refs_1_, ...), custom_call_target="tpu_custom_call" | custom-call | flops 10000000000 | bytes 9777924 | tf_op jit(solution)/shard_map/edge_own/pallas_call | solution.py:308
  6.4 0.0 collective-permute-done.refs_3_
  6.5 0.9 %collective-permute-done.1.refs_4_ = bf16[96,512]{1,0:T(8,128)(2,1)S(1)} collective-permute-done((bf16[96,512]{1,0:T(8,128)(2,1)S(1)}, bf16[96,512]{1,0:T(8,128)(2,1)S(1)}, u32[]{:S(2)}, u32[]{:S(2)}) %collective-permute-start.1) | collective-permute-done | bytes 98336 | tf_op jit(solution)/shard_map/ppermute | solution.py:329
  7.3 2.1 %message.1 = (bf16[1024,512]{1,0:T(8,128)(2,1)S(1)}, bf16[96,512]{1,0:T(8,128)(2,1)S(1)}, bf16[96,512]{1,0:T(8,128)(2,1)S(1)}) custom-call(bf16[1024,192]{1,0:T(8,128)(2,1)S(1)} %get-tuple-element.27.refs_0_, bf16[192,1024]{1,0:T(8,128)(2,1)S(1)} %get-tuple-element.28.refs_1_, f32[1024,512]{1,0:T(8,128)S(1)} %get-tuple-element.29.refs_2_, ...), custom_call_target="tpu_custom_call" | custom-call | flops 10000000000 | bytes 8585216 | tf_op jit(solution)/shard_map/message/pallas_call | solution.py:308
  9.4 1.6 %collective-permute-start.2 = (bf16[96,512]{1,0:T(8,128)(2,1)S(1)}, bf16[96,512]{1,0:T(8,128)(2,1)S(1)}, u32[]{:S(2)}, u32[]{:S(2)}) collective-permute-start(bf16[96,512]{1,0:T(8,128)(2,1)S(1)} %get-tuple-element.36), channel_id=1, source_target_pairs={{0,1},{1,0},{2,3},{3,2},{4,5},{5,4},{6,7},{7,6},{8,9},{9,8},{10,11... | collective-permute-start | bytes 294920 | tf_op jit(solution)/shard_map/ppermute | solution.py:330
  11.0 0.0 collective-permute-start.3
  11.0 0.0 copy-start.9
  11.0 0.0 copy-start.10
  11.0 0.0 copy-start.11
  11.0 3.9 %grid_own.1 = (f32[1536,512]{1,0:T(8,128)S(1)}, bf16[512,512]{1,0:T(8,128)(2,1)S(1)}, bf16[1536,192]{1,0:T(8,128)(2,1)S(1)}) custom-call(s32[1]{0:T(128)} %bitcast.odd_ref.refs_0_, s32[1536]{0:T(1024)S(1)} %copy-done.12, s32[1,1024]{1,0:T(1,128)S(1)} %get-tuple-element.26.refs_2_, bf16[1024,512]{1,0:T(8,128)(2,1)S(1)} %get-tuple-element.33.refs_3_, ...), custom_call_target="tpu_custom_call" | custom-call | flops 10000000000 | bytes 10561536 | tf_op jit(solution)/shard_map/grid_own/pallas_call | solution.py:308
  14.9 0.0 collective-permute-done.2.refs_2_
  14.9 0.5 %collective-permute-done.3.refs_3_ = bf16[96,512]{1,0:T(8,128)(2,1)S(1)} collective-permute-done((bf16[96,512]{1,0:T(8,128)(2,1)S(1)}, bf16[96,512]{1,0:T(8,128)(2,1)S(1)}, u32[]{:S(2)}, u32[]{:S(2)}) %collective-permute-start.3) | collective-permute-done | bytes 98336 | tf_op jit(solution)/shard_map/ppermute | solution.py:329
  15.5 0.0 copy-start.15
  15.5 0.0 copy-start.17
  15.5 2.2 %grid.1 = (f32[87,512]{1,0:T(8,128)S(1)}, bf16[87,512]{1,0:T(8,128)(2,1)S(1)}) custom-call(bf16[1536,192]{1,0:T(8,128)(2,1)S(1)} %get-tuple-element.34.refs_0_, f32[1536,512]{1,0:T(8,128)S(1)} %get-tuple-element.35.refs_1_, bf16[96,512]{1,0:T(8,128)(2,1)S(1)} %collective-permute-done.2.refs_2_, bf16[96,512]{1,0:T(8,128)(2,1)S(1)} %collective-permute-done.3.refs_3_, ...), custom_call_target="tpu_custom_call" | custom-call | flops 10000000000 | bytes 6217728 | tf_op jit(solution)/shard_map/grid/pallas_call | solution.py:308
  17.7 1.3 %collective-permute-start.5 = (bf16[87,512]{1,0:T(8,128)(2,1)S(1)}, bf16[87,512]{1,0:T(8,128)(2,1)S(1)}, u32[]{:S(2)}, u32[]{:S(2)}) collective-permute-start(bf16[87,512]{1,0:T(8,128)(2,1)S(1)} %get-tuple-element.40), channel_id=1, source_target_pairs={{0,16},{8,24},{16,0},{24,8},{1,17},{9,25},{17,1},{25,9},{2,18},{10... | collective-permute-start | bytes 267272 | tf_op jit(solution)/shard_map/ppermute | solution.py:341
  19.0 3.1 %collective-permute-start.4 = (bf16[87,512]{1,0:T(8,128)(2,1)S(1)}, bf16[87,512]{1,0:T(8,128)(2,1)S(1)}, u32[]{:S(2)}, u32[]{:S(2)}) collective-permute-start(bf16[87,512]{1,0:T(8,128)(2,1)S(1)} %get-tuple-element.40), channel_id=1, source_target_pairs={{0,8},{8,0},{16,24},{24,16},{1,9},{9,1},{17,25},{25,17},{2,10},{10... | collective-permute-start | bytes 267272 | tf_op jit(solution)/shard_map/ppermute | solution.py:335
  22.1 0.0 collective-permute-done.5.refs_1_
  22.1 3.0 %collective-permute-start.6 = (bf16[87,512]{1,0:T(8,128)(2,1)S(1)}, bf16[87,512]{1,0:T(8,128)(2,1)S(1)}, u32[]{:S(2)}, u32[]{:S(2)}) collective-permute-start(bf16[87,512]{1,0:T(8,128)(2,1)S(1)} %collective-permute-done.5.refs_1_), channel_id=1, source_target_pairs={{0,8},{8,0},{16,24},{24,16},{1,9},{9,1},{17,25},{25,17},{2,10},{10... | collective-permute-start | bytes 267272 | tf_op jit(solution)/shard_map/ppermute | solution.py:335
  25.1 0.0 collective-permute-done.4.refs_0_
  25.1 0.2 score.1
  25.3 0.7 %collective-permute-done.6.refs_0_ = bf16[87,512]{1,0:T(8,128)(2,1)S(1)} collective-permute-done((bf16[87,512]{1,0:T(8,128)(2,1)S(1)}, bf16[87,512]{1,0:T(8,128)(2,1)S(1)}, u32[]{:S(2)}, u32[]{:S(2)}) %collective-permute-start.6) | collective-permute-done | bytes 89120 | tf_op jit(solution)/shard_map/ppermute | solution.py:335
  26.0 0.8 %finish.1 = f32[87,1,512]{2,1,0:T(1,128)} custom-call(f32[87,512]{1,0:T(8,128)S(1)} %get-tuple-element.39.difference_ref, f32[87,512]{1,0:T(8,128)S(1)} %get-tuple-element.41.partial_ref, f32[87,512]{1,0:T(8,128)S(1)} %get-tuple-element.42.weight_ref, bf16[87,512]{1,0:T(8,128)(2,1)S(1)} %collective-permute-done.6.refs_0_), custom_call_target="tpu_custom_call" | custom-call | flops 10000000 | bytes 801792 | tf_op jit(solution)/shard_map/finish/pallas_call | solution.py:308
  (25 shorter events, 0.0 us)
Async XLA Ops:
  0.0 3.7 %copy-start = (bf16[1536,512]{1,0:T(8,128)(2,1)S(1)}, bf16[1536,512]{1,0:T(8,128)(2,1)}, u32[]{:S(2)}) copy-start(bf16[1536,512]{1,0:T(8,128)(2,1)} %refs_7_.3) | copy-start | bytes 4718596
  0.0 3.7 %copy-start.2 = (bf16[1024,512]{1,0:T(8,128)(2,1)S(1)}, bf16[1024,512]{1,0:T(8,128)(2,1)}, u32[]{:S(2)}) copy-start(bf16[1024,512]{1,0:T(8,128)(2,1)} %refs_8_.3) | copy-start | bytes 3145732
  0.0 3.7 %copy-start.3 = (bf16[1024,512]{1,0:T(8,128)(2,1)S(1)}, bf16[1024,512]{1,0:T(8,128)(2,1)}, u32[]{:S(2)}) copy-start(bf16[1024,512]{1,0:T(8,128)(2,1)} %refs_5_.1) | copy-start | bytes 3145732
  0.0 3.7 %copy-start.5 = (bf16[512,512]{1,0:T(8,128)(2,1)S(1)}, bf16[512,512]{1,0:T(8,128)(2,1)}, u32[]{:S(2)}) copy-start(bf16[512,512]{1,0:T(8,128)(2,1)} %refs_10_.2) | copy-start | bytes 1572868
  0.0 3.7 %copy-start.6 = (bf16[512,512]{1,0:T(8,128)(2,1)S(1)}, bf16[512,512]{1,0:T(8,128)(2,1)}, u32[]{:S(2)}) copy-start(bf16[512,512]{1,0:T(8,128)(2,1)} %refs_12_.1) | copy-start | bytes 1572868
  0.0 3.7 %copy-start.7 = (bf16[1,512,512]{2,1,0:T(8,128)(2,1)S(1)}, bf16[1,512,512]{2,1,0:T(8,128)(2,1)}, u32[]{:S(2)}) copy-start(bf16[1,512,512]{2,1,0:T(8,128)(2,1)} %param.19) | copy-start | bytes 1572868
  0.0 3.7 %copy-start.13 = (s32[1024]{0:T(1024)S(1)}, s32[1024]{0:T(1024)}, u32[]{:S(2)}) copy-start(s32[1024]{0:T(1024)} %refs_3_.1) | copy-start | bytes 12292
  0.0 3.7 %copy-start.14 = (s32[1024]{0:T(1024)S(1)}, s32[1024]{0:T(1024)}, u32[]{:S(2)}) copy-start(s32[1024]{0:T(1024)} %refs_4_.2) | copy-start | bytes 12292
  0.1 3.7 %copy-start.16 = (s32[1,2,96]{2,1,0:T(2,128)S(1)}, s32[1,2,96]{2,1,0:T(2,128)}, u32[]{:S(2)}) copy-start(s32[1,2,96]{2,1,0:T(2,128)} %param.33) | copy-start | bytes 2308
  1.6 4.8 %collective-permute-start = (bf16[96,512]{1,0:T(8,128)(2,1)S(1)}, bf16[96,512]{1,0:T(8,128)(2,1)S(1)}, u32[]{:S(2)}, u32[]{:S(2)}) collective-permute-start(bf16[96,512]{1,0:T(8,128)(2,1)S(1)} %get-tuple-element.24.refs_5_), channel_id=1, source_target_pairs={{0,1},{1,0},{2,3},{3,2},{4,5},{5,4},{6,7},{7,6},{8,9},{9,8},{10,11... | collective-permute-start | bytes 294920 | tf_op jit(solution)/shard_map/ppermute | solution.py:330
  2.9 4.4 %collective-permute-start.1 = (bf16[96,512]{1,0:T(8,128)(2,1)S(1)}, bf16[96,512]{1,0:T(8,128)(2,1)S(1)}, u32[]{:S(2)}, u32[]{:S(2)}) collective-permute-start(bf16[96,512]{1,0:T(8,128)(2,1)S(1)} %get-tuple-element.25.refs_6_), channel_id=1, source_target_pairs={{0,8},{1,2},{2,1},{3,4},{4,3},{5,6},{6,5},{7,15},{8,0},{9,10},{10,... | collective-permute-start | bytes 294920 | tf_op jit(solution)/shard_map/ppermute | solution.py:329
  7.3 3.7 %copy-start.1 = (bf16[1536,512]{1,0:T(8,128)(2,1)S(1)}, bf16[1536,512]{1,0:T(8,128)(2,1)}, u32[]{:S(2)}) copy-start(bf16[1536,512]{1,0:T(8,128)(2,1)} %refs_7_.4) | copy-start | bytes 4718596
  7.3 3.7 %copy-start.4 = (bf16[1024,512]{1,0:T(8,128)(2,1)S(1)}, bf16[1024,512]{1,0:T(8,128)(2,1)}, u32[]{:S(2)}) copy-start(bf16[1024,512]{1,0:T(8,128)(2,1)} %refs_4_.3) | copy-start | bytes 3145732
  7.3 3.7 %copy-start.8 = (bf16[512,512]{1,0:T(8,128)(2,1)S(1)}, bf16[512,512]{1,0:T(8,128)(2,1)}, u32[]{:S(2)}) copy-start(bf16[512,512]{1,0:T(8,128)(2,1)} %refs_9_.3) | copy-start | bytes 1572868
  7.3 3.7 %copy-start.12 = (s32[1536]{0:T(1024)S(1)}, s32[1536]{0:T(1024)}, u32[]{:S(2)}) copy-start(s32[1536]{0:T(1024)} %refs_1_.2) | copy-start | bytes 18436
  9.4 5.5 %collective-permute-start.2 = (bf16[96,512]{1,0:T(8,128)(2,1)S(1)}, bf16[96,512]{1,0:T(8,128)(2,1)S(1)}, u32[]{:S(2)}, u32[]{:S(2)}) collective-permute-start(bf16[96,512]{1,0:T(8,128)(2,1)S(1)} %get-tuple-element.36), channel_id=1, source_target_pairs={{0,1},{1,0},{2,3},{3,2},{4,5},{5,4},{6,7},{7,6},{8,9},{9,8},{10,11... | collective-permute-start | bytes 294920 | tf_op jit(solution)/shard_map/ppermute | solution.py:330
  11.0 4.5 %collective-permute-start.3 = (bf16[96,512]{1,0:T(8,128)(2,1)S(1)}, bf16[96,512]{1,0:T(8,128)(2,1)S(1)}, u32[]{:S(2)}, u32[]{:S(2)}) collective-permute-start(bf16[96,512]{1,0:T(8,128)(2,1)S(1)} %get-tuple-element.37), channel_id=1, source_target_pairs={{0,8},{1,2},{2,1},{3,4},{4,3},{5,6},{6,5},{7,15},{8,0},{9,10},{10,... | collective-permute-start | bytes 294920 | tf_op jit(solution)/shard_map/ppermute | solution.py:329
  11.0 4.4 %copy-start.9 = (f32[87,512]{1,0:T(8,128)S(1)}, f32[87,512]{1,0:T(8,128)}, u32[]{:S(2)}) copy-start(f32[87,512]{1,0:T(8,128)} %refs_7_.5) | copy-start | bytes 534532
  11.0 4.4 %copy-start.10 = (f32[87,512]{1,0:T(8,128)S(1)}, f32[87,512]{1,0:T(8,128)}, u32[]{:S(2)}) copy-start(f32[87,512]{1,0:T(8,128)} %refs_8_.5) | copy-start | bytes 534532
  11.0 4.4 %copy-start.11 = (bf16[87,512]{1,0:T(8,128)(2,1)S(1)}, bf16[87,512]{1,0:T(8,128)(2,1)}, u32[]{:S(2)}) copy-start(bf16[87,512]{1,0:T(8,128)(2,1)} %refs_6_.1) | copy-start | bytes 267268
  15.5 9.7 %copy-start.15 = (f32[512]{0:T(512)S(1)}, f32[512]{0:T(512)}, u32[]{:S(2)}) copy-start(f32[512]{0:T(512)} %param.32) | copy-start | bytes 6148
  15.5 9.6 %copy-start.17 = (f32[87]{0:T(128)S(1)}, f32[87]{0:T(128)}, u32[]{:S(2)}) copy-start(f32[87]{0:T(128)} %param.31) | copy-start | bytes 1048
  17.7 4.4 %collective-permute-start.5 = (bf16[87,512]{1,0:T(8,128)(2,1)S(1)}, bf16[87,512]{1,0:T(8,128)(2,1)S(1)}, u32[]{:S(2)}, u32[]{:S(2)}) collective-permute-start(bf16[87,512]{1,0:T(8,128)(2,1)S(1)} %get-tuple-element.40), channel_id=1, source_target_pairs={{0,16},{8,24},{16,0},{24,8},{1,17},{9,25},{17,1},{25,9},{2,18},{10... | collective-permute-start | bytes 267272 | tf_op jit(solution)/shard_map/ppermute | solution.py:341
  19.0 6.1 %collective-permute-start.4 = (bf16[87,512]{1,0:T(8,128)(2,1)S(1)}, bf16[87,512]{1,0:T(8,128)(2,1)S(1)}, u32[]{:S(2)}, u32[]{:S(2)}) collective-permute-start(bf16[87,512]{1,0:T(8,128)(2,1)S(1)} %get-tuple-element.40), channel_id=1, source_target_pairs={{0,8},{8,0},{16,24},{24,16},{1,9},{9,1},{17,25},{25,17},{2,10},{10... | collective-permute-start | bytes 267272 | tf_op jit(solution)/shard_map/ppermute | solution.py:335
  22.1 4.0 %collective-permute-start.6 = (bf16[87,512]{1,0:T(8,128)(2,1)S(1)}, bf16[87,512]{1,0:T(8,128)(2,1)S(1)}, u32[]{:S(2)}, u32[]{:S(2)}) collective-permute-start(bf16[87,512]{1,0:T(8,128)(2,1)S(1)} %collective-permute-done.5.refs_1_), channel_id=1, source_target_pairs={{0,8},{8,0},{16,24},{24,16},{1,9},{9,1},{17,25},{25,17},{2,10},{10... | collective-permute-start | bytes 267272 | tf_op jit(solution)/shard_map/ppermute | solution.py:335

commit v5 on v4

--- a/solution.py
+++ b/solution.py
@@ -17,6 +17,10 @@
     return jnp.dot(a, b, preferred_element_type=f32)
 
 
+def odd_band():
+    return lax.rem(lax.axis_index("patch"), 2) == 1
+
+
 def silu_of_twice(half):
     return (half + half * jnp.tanh(half)).astype(bf16)
 
@@ -74,7 +78,7 @@
     return (0.5 * dot(rows, weight_ref[0 : rows.shape[1], :])).astype(bf16)
 
 
-def select_kernel(odd_ref, sends_hbm, table_hbm, pair_ref, cross_ref, sends_ref, table_ref, semaphores):
+def select_kernel(sends_hbm, table_hbm, pair_ref, cross_ref, sends_ref, table_ref, semaphores):
     pieces = semaphores.shape[0] - 1
     step = table_ref.shape[0] // pieces
     first = pltpu.make_async_copy(sends_hbm, sends_ref, semaphores.at[pieces])
@@ -87,7 +91,7 @@
         )
         copies[-1].start()
     first.wait()
-    pair, cross = send_index(sends_ref, odd_ref[0] == 1)
+    pair, cross = send_index(sends_ref, odd_band())
     index = jnp.concatenate([column(pair), column(cross)], 0)
     picked = None
     for at, copy in enumerate(copies):
@@ -102,7 +106,6 @@
 
 def edge_own_kernel(
     block,
-    odd_ref,
     count_ref,
     sends_ref,
     senders_ref,
@@ -128,7 +131,7 @@
     nodes, width = table_ref.shape
     edges = edge_ref.shape[0]
     halo = pair_ref.shape[0]
-    odd = odd_ref[0] == 1
+    odd = odd_band()
     outer_out_ref[...] = centred_weight(outer_ref)
     node_outer_out_ref[...] = centred_weight(node_outer_ref)
     halo_choice(senders_ref, nodes, halo, odd, choice_ref)
@@ -194,7 +197,6 @@
 def grid_own_kernel(
     block,
     halo,
-    odd_ref,
     senders_ref,
     live_ref,
     message_ref,
@@ -220,7 +222,7 @@
         total += dot(chosen(columns(senders_ref, at, block), nodes), sent_ref[...])
         pre_ref[rows, :] = 0.5 * total
     outer_out_ref[...] = centred_weight(outer_ref)
-    halo_choice(senders_ref, nodes, halo, odd_ref[0] == 1, choice_ref)
+    halo_choice(senders_ref, nodes, halo, odd_band(), choice_ref)
 
 
 def grid_kernel(
@@ -372,7 +374,6 @@
     edges = edge_senders.shape[0]
     grid_edges = grid_senders.shape[0]
     channels, points = prior_state.shape
-    odd = (lax.axis_index("patch") % 2).astype(jnp.int32)[None]
     senders = edge_senders
     receivers = edge_receivers
     grid_rows = grid_senders
@@ -380,7 +381,7 @@
     pair, cross = call(
         select_kernel,
         "select",
-        (odd,),
+        (),
         tuple(pltpu.with_memory_space_constraint(x, pltpu.HBM) for x in (sends, latent)),
         (shape(halo, width), shape(halo, width)),
         (VMEM((2, halo), jnp.int32), VMEM((nodes, width), bf16), pltpu.SemaphoreType.DMA((3,))),
@@ -391,7 +392,7 @@
     pre, sent_pre, outer, second, choice, live, sent_placing = call(
         lambda *refs: edge_own_kernel(edges, *refs),
         "edge_own",
-        (odd,),
+        (),
         (
             edge_count,
             sends,
@@ -444,7 +445,7 @@
     pre, outer, choice = call(
         lambda *refs: grid_own_kernel(grid_edges // 2, halo, *refs),
         "grid_own",
-        (odd,),
+        (),
         (
             grid_rows,
             live,

time: 27 us -> 26.9 us (level)
  no operation moved by 1% of the time
where the time goes in v5:
time: 26.9 us; the launch traced here: 26.8 us
  Pallas kernels  13.2 us (49%)
  starting transfers between devices  10.4 us (39%)
  waiting for transfers between devices  2.15 us (8%)
  between operations  0.91 us (3%)
    pallas_call x7, Pallas kernels, call(): pl.pallas_call(kernel, name=name, out_shape=outs, in_specs=[scalar()] * l...  13.2 us
    ppermute x2, starting transfers between devices, mate(): return lax.ppermute(rows, 'mem', [(m, m ^ 1) for m in range(members)])  6.09 us
    ppermute x2, starting transfers between devices, exchange(): return (lax.ppermute(pair_rows, 'patch', pair), crossed)  2.85 us
    ppermute x2, waiting for transfers between devices, exchange(): crossed = lax.ppermute(cross_rows, ('mem', 'patch'), cross)  1.43 us
    ppermute x1, starting transfers between devices, chip_mates(): lax.ppermute(rows, 'mem', [(m, (m + shift) % members) for m in range(memb...  1.3 us
    ppermute x2, waiting for transfers between devices, mate(): return lax.ppermute(rows, 'mem', [(m, m ^ 1) for m in range(members)])  0.71 us
  transfers between devices with their start and end apart: 7, of which 3 were waited for; matrix products, arithmetic and copies ran while one was open for 0% of the time, Pallas kernels for 25%

profile of v5, /device:TPU:17, one launch (start us, length us, event | category | flops | bytes accessed | tf_op | source)
XLA Modules:
  0.0 26.8 jit_solution(5137691679071140057)
XLA Ops:
  0.0 0.0 copy-start.5
  0.0 0.0 copy-start.6
  0.0 0.0 copy-start.7
  0.0 0.0 copy-start.13
  0.0 0.0 copy-start.14
  0.1 0.0 copy-start.16
  0.1 1.5 %select.1 = (bf16[96,512]{1,0:T(8,128)(2,1)S(1)}, bf16[96,512]{1,0:T(8,128)(2,1)S(1)}) custom-call(s32[2,96]{1,0:T(2,128)} %bitcast.9, bf16[512,512]{1,0:T(8,128)(2,1)} %bitcast.5), custom_call_target="tpu_custom_call" | custom-call | flops 10000000000 | bytes 721664 | tf_op jit(solution)/shard_map/select/pallas_call | solution.py:310
  1.6 1.3 %collective-permute-start = (bf16[96,512]{1,0:T(8,128)(2,1)S(1)}, bf16[96,512]{1,0:T(8,128)(2,1)S(1)}, u32[]{:S(2)}, u32[]{:S(2)}) collective-permute-start(bf16[96,512]{1,0:T(8,128)(2,1)S(1)} %get-tuple-element.24.refs_4_.refs_5_), channel_id=1, source_target_pairs={{0,1},{1,0},{2,3},{3,2},{4,5},{5,4},{6,7},{7,6},{8,9},{9,8},{10,11... | collective-permute-start | bytes 294920 | tf_op jit(solution)/shard_map/ppermute | solution.py:332
  2.9 0.1 collective-permute-start.1
  3.8 2.7 %edge_own.1 = (f32[1024,512]{1,0:T(8,128)S(1)}, f32[192,512]{1,0:T(8,128)S(1)}, bf16[512,512]{1,0:T(8,128)(2,1)S(1)}, bf16[512,512]{1,0:T(8,128)(2,1)S(1)}, bf16...) custom-call(s32[1]{0:T(128)S(6)} %copy.20.refs_0_, s32[2,96]{1,0:T(2,128)S(1)} %bitcast.10, ...), custom_call_target="tpu_custom_call" | custom-call | flops 10000000000 | bytes 9777924 | tf_op jit(solution)/shard_map/edge_own/pallas_call | solution.py:310
  6.4 0.0 collective-permute-done.refs_3_
  6.4 0.9 %collective-permute-done.1.refs_4_ = bf16[96,512]{1,0:T(8,128)(2,1)S(1)} collective-permute-done((bf16[96,512]{1,0:T(8,128)(2,1)S(1)}, bf16[96,512]{1,0:T(8,128)(2,1)S(1)}, u32[]{:S(2)}, u32[]{:S(2)}) %collective-permute-start.1) | collective-permute-done | bytes 98336 | tf_op jit(solution)/shard_map/ppermute | solution.py:331
  7.3 2.1 %message.1 = (bf16[1024,512]{1,0:T(8,128)(2,1)S(1)}, bf16[96,512]{1,0:T(8,128)(2,1)S(1)}, bf16[96,512]{1,0:T(8,128)(2,1)S(1)}) custom-call(bf16[1024,192]{1,0:T(8,128)(2,1)S(1)} %get-tuple-element.27.refs_0_, bf16[192,1024]{1,0:T(8,128)(2,1)S(1)} %get-tuple-element.28.refs_1_, f32[1024,512]{1,0:T(8,128)S(1)} %get-tuple-element.29.refs_2_, ...), custom_call_target="tpu_custom_call" | custom-call | flops 10000000000 | bytes 8585216 | tf_op jit(solution)/shard_map/message/pallas_call | solution.py:310
  9.4 1.6 %collective-permute-start.2 = (bf16[96,512]{1,0:T(8,128)(2,1)S(1)}, bf16[96,512]{1,0:T(8,128)(2,1)S(1)}, u32[]{:S(2)}, u32[]{:S(2)}) collective-permute-start(bf16[96,512]{1,0:T(8,128)(2,1)S(1)} %get-tuple-element.36), channel_id=1, source_target_pairs={{0,1},{1,0},{2,3},{3,2},{4,5},{5,4},{6,7},{7,6},{8,9},{9,8},{10,11... | collective-permute-start | bytes 294920 | tf_op jit(solution)/shard_map/ppermute | solution.py:332
  11.0 0.0 collective-permute-start.3
  11.0 0.0 copy-start.9
  11.0 0.0 copy-start.10
  11.0 0.0 copy-start.11
  11.0 3.8 %grid_own.1 = (f32[1536,512]{1,0:T(8,128)S(1)}, bf16[512,512]{1,0:T(8,128)(2,1)S(1)}, bf16[1536,192]{1,0:T(8,128)(2,1)S(1)}) custom-call(s32[1536]{0:T(1024)S(1)} %copy-done.12, s32[1,1024]{1,0:T(1,128)S(1)} %get-tuple-element.26.refs_1_, bf16[1024,512]{1,0:T(8,128)(2,1)S(1)} %get-tuple-element.33.refs_2_, bf16[512,512]{1,0:T(8,128)(2,1)S(1)} %bitcast.7, ...), custom_call_target="tpu_custom_call" | custom-call | flops 10000000000 | bytes 10561536 | tf_op jit(solution)/shard_map/grid_own/pallas_call | solution.py:310
  14.9 0.0 collective-permute-done.2.refs_2_
  14.9 0.5 %collective-permute-done.3.refs_3_ = bf16[96,512]{1,0:T(8,128)(2,1)S(1)} collective-permute-done((bf16[96,512]{1,0:T(8,128)(2,1)S(1)}, bf16[96,512]{1,0:T(8,128)(2,1)S(1)}, u32[]{:S(2)}, u32[]{:S(2)}) %collective-permute-start.3) | collective-permute-done | bytes 98336 | tf_op jit(solution)/shard_map/ppermute | solution.py:331
  15.5 0.0 copy-start.15
  15.5 0.0 copy-start.17
  15.5 2.2 %grid.1 = (f32[87,512]{1,0:T(8,128)S(1)}, bf16[87,512]{1,0:T(8,128)(2,1)S(1)}) custom-call(bf16[1536,192]{1,0:T(8,128)(2,1)S(1)} %get-tuple-element.34.refs_0_, f32[1536,512]{1,0:T(8,128)S(1)} %get-tuple-element.35.refs_1_, bf16[96,512]{1,0:T(8,128)(2,1)S(1)} %collective-permute-done.2.refs_2_, bf16[96,512]{1,0:T(8,128)(2,1)S(1)} %collective-permute-done.3.refs_3_, ...), custom_call_target="tpu_custom_call" | custom-call | flops 10000000000 | bytes 6217728 | tf_op jit(solution)/shard_map/grid/pallas_call | solution.py:310
  17.7 1.3 %collective-permute-start.5 = (bf16[87,512]{1,0:T(8,128)(2,1)S(1)}, bf16[87,512]{1,0:T(8,128)(2,1)S(1)}, u32[]{:S(2)}, u32[]{:S(2)}) collective-permute-start(bf16[87,512]{1,0:T(8,128)(2,1)S(1)} %get-tuple-element.40), channel_id=1, source_target_pairs={{0,16},{8,24},{16,0},{24,8},{1,17},{9,25},{17,1},{25,9},{2,18},{10... | collective-permute-start | bytes 267272 | tf_op jit(solution)/shard_map/ppermute | solution.py:343
  19.0 3.1 %collective-permute-start.4 = (bf16[87,512]{1,0:T(8,128)(2,1)S(1)}, bf16[87,512]{1,0:T(8,128)(2,1)S(1)}, u32[]{:S(2)}, u32[]{:S(2)}) collective-permute-start(bf16[87,512]{1,0:T(8,128)(2,1)S(1)} %get-tuple-element.40), channel_id=1, source_target_pairs={{0,8},{8,0},{16,24},{24,16},{1,9},{9,1},{17,25},{25,17},{2,10},{10... | collective-permute-start | bytes 267272 | tf_op jit(solution)/shard_map/ppermute | solution.py:337
  22.1 0.0 collective-permute-done.5.refs_1_
  22.1 3.0 %collective-permute-start.6 = (bf16[87,512]{1,0:T(8,128)(2,1)S(1)}, bf16[87,512]{1,0:T(8,128)(2,1)S(1)}, u32[]{:S(2)}, u32[]{:S(2)}) collective-permute-start(bf16[87,512]{1,0:T(8,128)(2,1)S(1)} %collective-permute-done.5.refs_1_), channel_id=1, source_target_pairs={{0,8},{8,0},{16,24},{24,16},{1,9},{9,1},{17,25},{25,17},{2,10},{10... | collective-permute-start | bytes 267272 | tf_op jit(solution)/shard_map/ppermute | solution.py:337
  25.1 0.0 collective-permute-done.4.refs_0_
  25.1 0.2 score.1
  25.3 0.7 %collective-permute-done.6.refs_0_ = bf16[87,512]{1,0:T(8,128)(2,1)S(1)} collective-permute-done((bf16[87,512]{1,0:T(8,128)(2,1)S(1)}, bf16[87,512]{1,0:T(8,128)(2,1)S(1)}, u32[]{:S(2)}, u32[]{:S(2)}) %collective-permute-start.6) | collective-permute-done | bytes 89120 | tf_op jit(solution)/shard_map/ppermute | solution.py:337
  26.0 0.8 %finish.1 = f32[87,1,512]{2,1,0:T(1,128)} custom-call(f32[87,512]{1,0:T(8,128)S(1)} %get-tuple-element.39.difference_ref, f32[87,512]{1,0:T(8,128)S(1)} %get-tuple-element.41.partial_ref, f32[87,512]{1,0:T(8,128)S(1)} %get-tuple-element.42.weight_ref, bf16[87,512]{1,0:T(8,128)(2,1)S(1)} %collective-permute-done.6.refs_0_), custom_call_target="tpu_custom_call" | custom-call | flops 10000000 | bytes 801792 | tf_op jit(solution)/shard_map/finish/pallas_call | solution.py:310
  (25 shorter events, 0.0 us)
Async XLA Ops:
  0.0 3.7 %copy-start = (bf16[1536,512]{1,0:T(8,128)(2,1)S(1)}, bf16[1536,512]{1,0:T(8,128)(2,1)}, u32[]{:S(2)}) copy-start(bf16[1536,512]{1,0:T(8,128)(2,1)} %refs_7_.5) | copy-start | bytes 4718596
  0.0 3.7 %copy-start.2 = (bf16[1024,512]{1,0:T(8,128)(2,1)S(1)}, bf16[1024,512]{1,0:T(8,128)(2,1)}, u32[]{:S(2)}) copy-start(bf16[1024,512]{1,0:T(8,128)(2,1)} %refs_7_.4) | copy-start | bytes 3145732
  0.0 3.7 %copy-start.3 = (bf16[1024,512]{1,0:T(8,128)(2,1)S(1)}, bf16[1024,512]{1,0:T(8,128)(2,1)}, u32[]{:S(2)}) copy-start(bf16[1024,512]{1,0:T(8,128)(2,1)} %refs_4_.2) | copy-start | bytes 3145732
  0.0 3.7 %copy-start.5 = (bf16[512,512]{1,0:T(8,128)(2,1)S(1)}, bf16[512,512]{1,0:T(8,128)(2,1)}, u32[]{:S(2)}) copy-start(bf16[512,512]{1,0:T(8,128)(2,1)} %refs_9_.1) | copy-start | bytes 1572868
  0.0 3.7 %copy-start.6 = (bf16[512,512]{1,0:T(8,128)(2,1)S(1)}, bf16[512,512]{1,0:T(8,128)(2,1)}, u32[]{:S(2)}) copy-start(bf16[512,512]{1,0:T(8,128)(2,1)} %refs_11_.1) | copy-start | bytes 1572868
  0.0 3.7 %copy-start.7 = (bf16[1,512,512]{2,1,0:T(8,128)(2,1)S(1)}, bf16[1,512,512]{2,1,0:T(8,128)(2,1)}, u32[]{:S(2)}) copy-start(bf16[1,512,512]{2,1,0:T(8,128)(2,1)} %param.19) | copy-start | bytes 1572868
  0.0 3.7 %copy-start.13 = (s32[1024]{0:T(1024)S(1)}, s32[1024]{0:T(1024)}, u32[]{:S(2)}) copy-start(s32[1024]{0:T(1024)} %refs_2_.1) | copy-start | bytes 12292
  0.0 3.7 %copy-start.14 = (s32[1024]{0:T(1024)S(1)}, s32[1024]{0:T(1024)}, u32[]{:S(2)}) copy-start(s32[1024]{0:T(1024)} %refs_3_.1) | copy-start | bytes 12292
  0.1 3.7 %copy-start.16 = (s32[1,2,96]{2,1,0:T(2,128)S(1)}, s32[1,2,96]{2,1,0:T(2,128)}, u32[]{:S(2)}) copy-start(s32[1,2,96]{2,1,0:T(2,128)} %param.33) | copy-start | bytes 2308
  1.6 4.8 %collective-permute-start = (bf16[96,512]{1,0:T(8,128)(2,1)S(1)}, bf16[96,512]{1,0:T(8,128)(2,1)S(1)}, u32[]{:S(2)}, u32[]{:S(2)}) collective-permute-start(bf16[96,512]{1,0:T(8,128)(2,1)S(1)} %get-tuple-element.24.refs_4_.refs_5_), channel_id=1, source_target_pairs={{0,1},{1,0},{2,3},{3,2},{4,5},{5,4},{6,7},{7,6},{8,9},{9,8},{10,11... | collective-permute-start | bytes 294920 | tf_op jit(solution)/shard_map/ppermute | solution.py:332
  2.9 4.4 %collective-permute-start.1 = (bf16[96,512]{1,0:T(8,128)(2,1)S(1)}, bf16[96,512]{1,0:T(8,128)(2,1)S(1)}, u32[]{:S(2)}, u32[]{:S(2)}) collective-permute-start(bf16[96,512]{1,0:T(8,128)(2,1)S(1)} %get-tuple-element.25.refs_5_.refs_6_), channel_id=1, source_target_pairs={{0,8},{1,2},{2,1},{3,4},{4,3},{5,6},{6,5},{7,15},{8,0},{9,10},{10,... | collective-permute-start | bytes 294920 | tf_op jit(solution)/shard_map/ppermute | solution.py:331
  7.3 3.7 %copy-start.1 = (bf16[1536,512]{1,0:T(8,128)(2,1)S(1)}, bf16[1536,512]{1,0:T(8,128)(2,1)}, u32[]{:S(2)}) copy-start(bf16[1536,512]{1,0:T(8,128)(2,1)} %refs_6_.2) | copy-start | bytes 4718596
  7.3 3.7 %copy-start.4 = (bf16[1024,512]{1,0:T(8,128)(2,1)S(1)}, bf16[1024,512]{1,0:T(8,128)(2,1)}, u32[]{:S(2)}) copy-start(bf16[1024,512]{1,0:T(8,128)(2,1)} %refs_4_.3) | copy-start | bytes 3145732
  7.3 3.7 %copy-start.8 = (bf16[512,512]{1,0:T(8,128)(2,1)S(1)}, bf16[512,512]{1,0:T(8,128)(2,1)}, u32[]{:S(2)}) copy-start(bf16[512,512]{1,0:T(8,128)(2,1)} %refs_8_.4) | copy-start | bytes 1572868
  7.3 3.7 %copy-start.12 = (s32[1536]{0:T(1024)S(1)}, s32[1536]{0:T(1024)}, u32[]{:S(2)}) copy-start(s32[1536]{0:T(1024)} %refs_0_.2) | copy-start | bytes 18436
  9.4 5.5 %collective-permute-start.2 = (bf16[96,512]{1,0:T(8,128)(2,1)S(1)}, bf16[96,512]{1,0:T(8,128)(2,1)S(1)}, u32[]{:S(2)}, u32[]{:S(2)}) collective-permute-start(bf16[96,512]{1,0:T(8,128)(2,1)S(1)} %get-tuple-element.36), channel_id=1, source_target_pairs={{0,1},{1,0},{2,3},{3,2},{4,5},{5,4},{6,7},{7,6},{8,9},{9,8},{10,11... | collective-permute-start | bytes 294920 | tf_op jit(solution)/shard_map/ppermute | solution.py:332
  11.0 4.5 %collective-permute-start.3 = (bf16[96,512]{1,0:T(8,128)(2,1)S(1)}, bf16[96,512]{1,0:T(8,128)(2,1)S(1)}, u32[]{:S(2)}, u32[]{:S(2)}) collective-permute-start(bf16[96,512]{1,0:T(8,128)(2,1)S(1)} %get-tuple-element.37), channel_id=1, source_target_pairs={{0,8},{1,2},{2,1},{3,4},{4,3},{5,6},{6,5},{7,15},{8,0},{9,10},{10,... | collective-permute-start | bytes 294920 | tf_op jit(solution)/shard_map/ppermute | solution.py:331
  11.0 4.4 %copy-start.9 = (f32[87,512]{1,0:T(8,128)S(1)}, f32[87,512]{1,0:T(8,128)}, u32[]{:S(2)}) copy-start(f32[87,512]{1,0:T(8,128)} %refs_7_.7) | copy-start | bytes 534532
  11.0 4.4 %copy-start.10 = (f32[87,512]{1,0:T(8,128)S(1)}, f32[87,512]{1,0:T(8,128)}, u32[]{:S(2)}) copy-start(f32[87,512]{1,0:T(8,128)} %refs_8_.5) | copy-start | bytes 534532
  11.0 4.4 %copy-start.11 = (bf16[87,512]{1,0:T(8,128)(2,1)S(1)}, bf16[87,512]{1,0:T(8,128)(2,1)}, u32[]{:S(2)}) copy-start(bf16[87,512]{1,0:T(8,128)(2,1)} %refs_6_.3) | copy-start | bytes 267268
  15.5 9.6 %copy-start.15 = (f32[512]{0:T(512)S(1)}, f32[512]{0:T(512)}, u32[]{:S(2)}) copy-start(f32[512]{0:T(512)} %param.32) | copy-start | bytes 6148
  15.5 9.6 %copy-start.17 = (f32[87]{0:T(128)S(1)}, f32[87]{0:T(128)}, u32[]{:S(2)}) copy-start(f32[87]{0:T(128)} %param.31) | copy-start | bytes 1048
  17.7 4.4 %collective-permute-start.5 = (bf16[87,512]{1,0:T(8,128)(2,1)S(1)}, bf16[87,512]{1,0:T(8,128)(2,1)S(1)}, u32[]{:S(2)}, u32[]{:S(2)}) collective-permute-start(bf16[87,512]{1,0:T(8,128)(2,1)S(1)} %get-tuple-element.40), channel_id=1, source_target_pairs={{0,16},{8,24},{16,0},{24,8},{1,17},{9,25},{17,1},{25,9},{2,18},{10... | collective-permute-start | bytes 267272 | tf_op jit(solution)/shard_map/ppermute | solution.py:343
  19.0 6.1 %collective-permute-start.4 = (bf16[87,512]{1,0:T(8,128)(2,1)S(1)}, bf16[87,512]{1,0:T(8,128)(2,1)S(1)}, u32[]{:S(2)}, u32[]{:S(2)}) collective-permute-start(bf16[87,512]{1,0:T(8,128)(2,1)S(1)} %get-tuple-element.40), channel_id=1, source_target_pairs={{0,8},{8,0},{16,24},{24,16},{1,9},{9,1},{17,25},{25,17},{2,10},{10... | collective-permute-start | bytes 267272 | tf_op jit(solution)/shard_map/ppermute | solution.py:337
  22.1 3.9 %collective-permute-start.6 = (bf16[87,512]{1,0:T(8,128)(2,1)S(1)}, bf16[87,512]{1,0:T(8,128)(2,1)S(1)}, u32[]{:S(2)}, u32[]{:S(2)}) collective-permute-start(bf16[87,512]{1,0:T(8,128)(2,1)S(1)} %collective-permute-done.5.refs_1_), channel_id=1, source_target_pairs={{0,8},{8,0},{16,24},{24,16},{1,9},{9,1},{17,25},{25,17},{2,10},{10... | collective-permute-start | bytes 267272 | tf_op jit(solution)/shard_map/ppermute | solution.py:337

commit v6 on v5

--- a/solution.py
+++ b/solution.py
@@ -175,9 +175,11 @@
     sent_pre_ref,
     node_inner_ref,
     node_outer_ref,
+    nodes_ref,
     message_ref,
     pair_out_ref,
     cross_out_ref,
+    node_pre_ref,
     halo_ref,
 ):
     halo = pair_ref.shape[0]
@@ -192,6 +194,8 @@
     )
     pair_out_ref[...] = updated[:halo]
     cross_out_ref[...] = updated[halo:]
+    width = nodes_ref.shape[1]
+    node_pre_ref[...] = 0.5 * dot(nodes_ref[...], node_inner_ref[0:width, :])
 
 
 def grid_own_kernel(
@@ -201,6 +205,7 @@
     live_ref,
     message_ref,
     table_ref,
+    node_pre_ref,
     node_inner_ref,
     node_outer_ref,
     edge_ref,
@@ -213,7 +218,7 @@
 ):
     nodes, width = table_ref.shape
     table = table_ref[...]
-    pre = 0.5 * dot(table, node_inner_ref[0:width, :])
+    pre = node_pre_ref[...]
     updated = node_update(placed(live_ref[...], nodes), message_ref[...], table, pre, node_inner_ref, node_outer_ref)
     sent_ref[...] = dot(updated, inner_ref[0:width, :]).astype(bf16)
     for at in range(0, edge_ref.shape[0], block):
@@ -419,7 +424,7 @@
         (VMEM((nodes, width), bf16), VMEM((nodes, width), bf16)),
         10**10,
     )
-    message, pair, cross = call(
+    message, pair, cross, node_pre = call(
         lambda *refs: message_kernel(edges, *refs),
         "message",
         (),
@@ -436,8 +441,14 @@
             sent_pre,
             node_inner,
             second,
+            latent,
         ),
-        (shape(edges, width), shape(halo, width), shape(halo, width)),
+        (
+            shape(edges, width),
+            shape(halo, width),
+            shape(halo, width),
+            shape(nodes, width, dtype=f32),
+        ),
         (VMEM((2 * halo, width), bf16),),
         10**10,
     )
@@ -451,6 +462,7 @@
             live,
             message,
             latent,
+            node_pre,
             node_inner,
             second,
             grid_edge_latent,

time: 26.9 us -> 27.1 us (level)
  waiting for transfers between devices: 2.15 us -> 2.48 us
    ppermute x2, waiting for transfers between devices: 1.43 us -> 1.77 us  [exchange(): crossed = lax.ppermute(cross_rows, ('mem', 'patch'), cross)]
  transfers between devices with their start and end apart: 7 -> 7, of which waited for: 3 -> 3; matrix products, arithmetic and copies ran while one was open for 0% -> 0% of each run, Pallas kernels for 25% -> 24%
where the time goes in v6:
time: 27.1 us; the launch traced here: 27 us
  Pallas kernels  13.1 us (48%)
  starting transfers between devices  10.4 us (38%)
  waiting for transfers between devices  2.48 us (9%)
  between operations  0.91 us (3%)
    pallas_call x7, Pallas kernels, call(): pl.pallas_call(kernel, name=name, out_shape=outs, in_specs=[scalar()] * l...  13.1 us
    ppermute x2, starting transfers between devices, mate(): return lax.ppermute(rows, 'mem', [(m, m ^ 1) for m in range(members)])  6.11 us
    ppermute x2, starting transfers between devices, exchange(): return (lax.ppermute(pair_rows, 'patch', pair), crossed)  2.84 us
    ppermute x2, waiting for transfers between devices, exchange(): crossed = lax.ppermute(cross_rows, ('mem', 'patch'), cross)  1.77 us
    ppermute x1, starting transfers between devices, chip_mates(): lax.ppermute(rows, 'mem', [(m, (m + shift) % members) for m in range(memb...  1.28 us
    ppermute x2, waiting for transfers between devices, mate(): return lax.ppermute(rows, 'mem', [(m, m ^ 1) for m in range(members)])  0.71 us
  transfers between devices with their start and end apart: 7, of which 3 were waited for; matrix products, arithmetic and copies ran while one was open for 0% of the time, Pallas kernels for 24%

profile of v6, /device:TPU:17, one launch (start us, length us, event | category | flops | bytes accessed | tf_op | source)
XLA Modules:
  0.0 27.0 jit_solution(14751090358252135940)
XLA Ops:
  0.0 0.0 copy-start.5
  0.0 0.0 copy-start.6
  0.0 0.0 copy-start.7
  0.0 0.0 copy-start.13
  0.0 0.0 copy-start.14
  0.1 0.0 copy-start.16
  0.1 1.5 %select.1 = (bf16[96,512]{1,0:T(8,128)(2,1)S(1)}, bf16[96,512]{1,0:T(8,128)(2,1)S(1)}) custom-call(s32[2,96]{1,0:T(2,128)} %bitcast.10, bf16[512,512]{1,0:T(8,128)(2,1)} %bitcast.5), custom_call_target="tpu_custom_call" | custom-call | flops 10000000000 | bytes 721664 | tf_op jit(solution)/shard_map/select/pallas_call | solution.py:315
  1.6 1.3 %collective-permute-start = (bf16[96,512]{1,0:T(8,128)(2,1)S(1)}, bf16[96,512]{1,0:T(8,128)(2,1)S(1)}, u32[]{:S(2)}, u32[]{:S(2)}) collective-permute-start(bf16[96,512]{1,0:T(8,128)(2,1)S(1)} %get-tuple-element.25.refs_4_.refs_5_), channel_id=1, source_target_pairs={{0,1},{1,0},{2,3},{3,2},{4,5},{5,4},{6,7},{7,6},{8,9},{9,8},{10,11... | collective-permute-start | bytes 294920 | tf_op jit(solution)/shard_map/ppermute | solution.py:337
  2.9 0.1 collective-permute-start.1
  3.8 2.7 %edge_own.1 = (f32[1024,512]{1,0:T(8,128)S(1)}, f32[192,512]{1,0:T(8,128)S(1)}, bf16[512,512]{1,0:T(8,128)(2,1)S(1)}, bf16[512,512]{1,0:T(8,128)(2,1)S(1)}, bf16...) custom-call(s32[1]{0:T(128)S(6)} %copy.20.refs_0_, s32[2,96]{1,0:T(2,128)S(1)} %bitcast.11, ...), custom_call_target="tpu_custom_call" | custom-call | flops 10000000000 | bytes 9777924 | tf_op jit(solution)/shard_map/edge_own/pallas_call | solution.py:315
  6.4 0.0 collective-permute-done.refs_3_
  6.4 0.9 %collective-permute-done.1.refs_4_ = bf16[96,512]{1,0:T(8,128)(2,1)S(1)} collective-permute-done((bf16[96,512]{1,0:T(8,128)(2,1)S(1)}, bf16[96,512]{1,0:T(8,128)(2,1)S(1)}, u32[]{:S(2)}, u32[]{:S(2)}) %collective-permute-start.1) | collective-permute-done | bytes 98336 | tf_op jit(solution)/shard_map/ppermute | solution.py:336
  7.3 2.3 %message.1 = (bf16[1024,512]{1,0:T(8,128)(2,1)S(1)}, bf16[96,512]{1,0:T(8,128)(2,1)S(1)}, bf16[96,512]{1,0:T(8,128)(2,1)S(1)}, f32[512,512]{1,0:T(8,128)S(1)}) custom-call(bf16[1024,192]{1,0:T(8,128)(2,1)S(1)} %get-tuple-element.28.refs_0_, bf16[192,1024]{1,0:T(8,128)(2,1)S(1)} %get-tuple-element.29.refs_1_, f32[1024,512]{1,0:T(8,128)S(1)} %get-tuple-element.30.refs_2_, ...), custom_call_target="tpu_custom_call" | custom-call | flops 10000000000 | bytes 10158080 | tf_op jit(solution)/shard_map/message/pallas_call | solution.py:315
  9.6 1.6 %collective-permute-start.2 = (bf16[96,512]{1,0:T(8,128)(2,1)S(1)}, bf16[96,512]{1,0:T(8,128)(2,1)S(1)}, u32[]{:S(2)}, u32[]{:S(2)}) collective-permute-start(bf16[96,512]{1,0:T(8,128)(2,1)S(1)} %get-tuple-element.38), channel_id=1, source_target_pairs={{0,1},{1,0},{2,3},{3,2},{4,5},{5,4},{6,7},{7,6},{8,9},{9,8},{10,11... | collective-permute-start | bytes 294920 | tf_op jit(solution)/shard_map/ppermute | solution.py:337
  11.2 0.0 collective-permute-start.3
  11.2 0.0 copy-start.9
  11.2 0.0 copy-start.10
  11.2 0.0 copy-start.11
  11.3 3.5 %grid_own.1 = (f32[1536,512]{1,0:T(8,128)S(1)}, bf16[512,512]{1,0:T(8,128)(2,1)S(1)}, bf16[1536,192]{1,0:T(8,128)(2,1)S(1)}) custom-call(s32[1536]{0:T(1024)S(1)} %copy-done.12, s32[1,1024]{1,0:T(1,128)S(1)} %get-tuple-element.27.refs_1_, bf16[1024,512]{1,0:T(8,128)(2,1)S(1)} %get-tuple-element.34.refs_2_, bf16[512,512]{1,0:T(8,128)(2,1)S(1)} %bitcast.8, ...), custom_call_target="tpu_custom_call" | custom-call | flops 10000000000 | bytes 11610112 | tf_op jit(solution)/shard_map/grid_own/pallas_call | solution.py:315
  14.8 0.0 collective-permute-done.2.refs_2_
  14.8 0.9 %collective-permute-done.3.refs_3_ = bf16[96,512]{1,0:T(8,128)(2,1)S(1)} collective-permute-done((bf16[96,512]{1,0:T(8,128)(2,1)S(1)}, bf16[96,512]{1,0:T(8,128)(2,1)S(1)}, u32[]{:S(2)}, u32[]{:S(2)}) %collective-permute-start.3) | collective-permute-done | bytes 98336 | tf_op jit(solution)/shard_map/ppermute | solution.py:336
  15.7 0.0 copy-start.15
  15.7 0.0 copy-start.17
  15.7 2.2 %grid.1 = (f32[87,512]{1,0:T(8,128)S(1)}, bf16[87,512]{1,0:T(8,128)(2,1)S(1)}) custom-call(bf16[1536,192]{1,0:T(8,128)(2,1)S(1)} %get-tuple-element.36.refs_0_, f32[1536,512]{1,0:T(8,128)S(1)} %get-tuple-element.37.refs_1_, bf16[96,512]{1,0:T(8,128)(2,1)S(1)} %collective-permute-done.2.refs_2_, bf16[96,512]{1,0:T(8,128)(2,1)S(1)} %collective-permute-done.3.refs_3_, ...), custom_call_target="tpu_custom_call" | custom-call | flops 10000000000 | bytes 6217728 | tf_op jit(solution)/shard_map/grid/pallas_call | solution.py:315
  17.9 1.3 %collective-permute-start.5 = (bf16[87,512]{1,0:T(8,128)(2,1)S(1)}, bf16[87,512]{1,0:T(8,128)(2,1)S(1)}, u32[]{:S(2)}, u32[]{:S(2)}) collective-permute-start(bf16[87,512]{1,0:T(8,128)(2,1)S(1)} %get-tuple-element.42), channel_id=1, source_target_pairs={{0,16},{8,24},{16,0},{24,8},{1,17},{9,25},{17,1},{25,9},{2,18},{10... | collective-permute-start | bytes 267272 | tf_op jit(solution)/shard_map/ppermute | solution.py:348
  19.2 3.1 %collective-permute-start.4 = (bf16[87,512]{1,0:T(8,128)(2,1)S(1)}, bf16[87,512]{1,0:T(8,128)(2,1)S(1)}, u32[]{:S(2)}, u32[]{:S(2)}) collective-permute-start(bf16[87,512]{1,0:T(8,128)(2,1)S(1)} %get-tuple-element.42), channel_id=1, source_target_pairs={{0,8},{8,0},{16,24},{24,16},{1,9},{9,1},{17,25},{25,17},{2,10},{10... | collective-permute-start | bytes 267272 | tf_op jit(solution)/shard_map/ppermute | solution.py:342
  22.3 0.0 collective-permute-done.5.refs_1_
  22.3 3.0 %collective-permute-start.6 = (bf16[87,512]{1,0:T(8,128)(2,1)S(1)}, bf16[87,512]{1,0:T(8,128)(2,1)S(1)}, u32[]{:S(2)}, u32[]{:S(2)}) collective-permute-start(bf16[87,512]{1,0:T(8,128)(2,1)S(1)} %collective-permute-done.5.refs_1_), channel_id=1, source_target_pairs={{0,8},{8,0},{16,24},{24,16},{1,9},{9,1},{17,25},{25,17},{2,10},{10... | collective-permute-start | bytes 267272 | tf_op jit(solution)/shard_map/ppermute | solution.py:342
  25.3 0.0 collective-permute-done.4.refs_0_
  25.3 0.2 score.1
  25.5 0.7 %collective-permute-done.6.refs_0_ = bf16[87,512]{1,0:T(8,128)(2,1)S(1)} collective-permute-done((bf16[87,512]{1,0:T(8,128)(2,1)S(1)}, bf16[87,512]{1,0:T(8,128)(2,1)S(1)}, u32[]{:S(2)}, u32[]{:S(2)}) %collective-permute-start.6) | collective-permute-done | bytes 89120 | tf_op jit(solution)/shard_map/ppermute | solution.py:342
  26.2 0.8 %finish.1 = f32[87,1,512]{2,1,0:T(1,128)} custom-call(f32[87,512]{1,0:T(8,128)S(1)} %get-tuple-element.41.difference_ref, f32[87,512]{1,0:T(8,128)S(1)} %get-tuple-element.43.partial_ref, f32[87,512]{1,0:T(8,128)S(1)} %get-tuple-element.44.weight_ref, bf16[87,512]{1,0:T(8,128)(2,1)S(1)} %collective-permute-done.6.refs_0_), custom_call_target="tpu_custom_call" | custom-call | flops 10000000 | bytes 801792 | tf_op jit(solution)/shard_map/finish/pallas_call | solution.py:315
  (25 shorter events, 0.0 us)
Async XLA Ops:
  0.0 3.7 %copy-start = (bf16[1536,512]{1,0:T(8,128)(2,1)S(1)}, bf16[1536,512]{1,0:T(8,128)(2,1)}, u32[]{:S(2)}) copy-start(bf16[1536,512]{1,0:T(8,128)(2,1)} %refs_7_.5) | copy-start | bytes 4718596
  0.0 3.7 %copy-start.2 = (bf16[1024,512]{1,0:T(8,128)(2,1)S(1)}, bf16[1024,512]{1,0:T(8,128)(2,1)}, u32[]{:S(2)}) copy-start(bf16[1024,512]{1,0:T(8,128)(2,1)} %refs_7_.4) | copy-start | bytes 3145732
  0.0 3.7 %copy-start.3 = (bf16[1024,512]{1,0:T(8,128)(2,1)S(1)}, bf16[1024,512]{1,0:T(8,128)(2,1)}, u32[]{:S(2)}) copy-start(bf16[1024,512]{1,0:T(8,128)(2,1)} %refs_5_.1) | copy-start | bytes 3145732
  0.0 3.7 %copy-start.5 = (bf16[512,512]{1,0:T(8,128)(2,1)S(1)}, bf16[512,512]{1,0:T(8,128)(2,1)}, u32[]{:S(2)}) copy-start(bf16[512,512]{1,0:T(8,128)(2,1)} %refs_9_.2) | copy-start | bytes 1572868
  0.0 3.7 %copy-start.6 = (bf16[512,512]{1,0:T(8,128)(2,1)S(1)}, bf16[512,512]{1,0:T(8,128)(2,1)}, u32[]{:S(2)}) copy-start(bf16[512,512]{1,0:T(8,128)(2,1)} %refs_11_.1) | copy-start | bytes 1572868
  0.0 3.7 %copy-start.7 = (bf16[1,512,512]{2,1,0:T(8,128)(2,1)S(1)}, bf16[1,512,512]{2,1,0:T(8,128)(2,1)}, u32[]{:S(2)}) copy-start(bf16[1,512,512]{2,1,0:T(8,128)(2,1)} %param.19) | copy-start | bytes 1572868
  0.0 3.7 %copy-start.13 = (s32[1024]{0:T(1024)S(1)}, s32[1024]{0:T(1024)}, u32[]{:S(2)}) copy-start(s32[1024]{0:T(1024)} %refs_2_.1) | copy-start | bytes 12292
  0.0 3.7 %copy-start.14 = (s32[1024]{0:T(1024)S(1)}, s32[1024]{0:T(1024)}, u32[]{:S(2)}) copy-start(s32[1024]{0:T(1024)} %refs_3_.1) | copy-start | bytes 12292
  0.1 3.7 %copy-start.16 = (s32[1,2,96]{2,1,0:T(2,128)S(1)}, s32[1,2,96]{2,1,0:T(2,128)}, u32[]{:S(2)}) copy-start(s32[1,2,96]{2,1,0:T(2,128)} %param.33) | copy-start | bytes 2308
  1.6 4.8 %collective-permute-start = (bf16[96,512]{1,0:T(8,128)(2,1)S(1)}, bf16[96,512]{1,0:T(8,128)(2,1)S(1)}, u32[]{:S(2)}, u32[]{:S(2)}) collective-permute-start(bf16[96,512]{1,0:T(8,128)(2,1)S(1)} %get-tuple-element.25.refs_4_.refs_5_), channel_id=1, source_target_pairs={{0,1},{1,0},{2,3},{3,2},{4,5},{5,4},{6,7},{7,6},{8,9},{9,8},{10,11... | collective-permute-start | bytes 294920 | tf_op jit(solution)/shard_map/ppermute | solution.py:337
  2.9 4.4 %collective-permute-start.1 = (bf16[96,512]{1,0:T(8,128)(2,1)S(1)}, bf16[96,512]{1,0:T(8,128)(2,1)S(1)}, u32[]{:S(2)}, u32[]{:S(2)}) collective-permute-start(bf16[96,512]{1,0:T(8,128)(2,1)S(1)} %get-tuple-element.26.refs_5_.refs_6_), channel_id=1, source_target_pairs={{0,8},{1,2},{2,1},{3,4},{4,3},{5,6},{6,5},{7,15},{8,0},{9,10},{10,... | collective-permute-start | bytes 294920 | tf_op jit(solution)/shard_map/ppermute | solution.py:336
  7.3 3.9 %copy-start.1 = (bf16[1536,512]{1,0:T(8,128)(2,1)S(1)}, bf16[1536,512]{1,0:T(8,128)(2,1)}, u32[]{:S(2)}) copy-start(bf16[1536,512]{1,0:T(8,128)(2,1)} %refs_7_.6) | copy-start | bytes 4718596
  7.3 3.9 %copy-start.4 = (bf16[1024,512]{1,0:T(8,128)(2,1)S(1)}, bf16[1024,512]{1,0:T(8,128)(2,1)}, u32[]{:S(2)}) copy-start(bf16[1024,512]{1,0:T(8,128)(2,1)} %refs_4_.1) | copy-start | bytes 3145732
  7.3 3.9 %copy-start.8 = (bf16[512,512]{1,0:T(8,128)(2,1)S(1)}, bf16[512,512]{1,0:T(8,128)(2,1)}, u32[]{:S(2)}) copy-start(bf16[512,512]{1,0:T(8,128)(2,1)} %refs_9_.3) | copy-start | bytes 1572868
  7.3 3.9 %copy-start.12 = (s32[1536]{0:T(1024)S(1)}, s32[1536]{0:T(1024)}, u32[]{:S(2)}) copy-start(s32[1536]{0:T(1024)} %refs_0_.2) | copy-start | bytes 18436
  9.6 5.1 %collective-permute-start.2 = (bf16[96,512]{1,0:T(8,128)(2,1)S(1)}, bf16[96,512]{1,0:T(8,128)(2,1)S(1)}, u32[]{:S(2)}, u32[]{:S(2)}) collective-permute-start(bf16[96,512]{1,0:T(8,128)(2,1)S(1)} %get-tuple-element.38), channel_id=1, source_target_pairs={{0,1},{1,0},{2,3},{3,2},{4,5},{5,4},{6,7},{7,6},{8,9},{9,8},{10,11... | collective-permute-start | bytes 294920 | tf_op jit(solution)/shard_map/ppermute | solution.py:337
  11.2 4.5 %collective-permute-start.3 = (bf16[96,512]{1,0:T(8,128)(2,1)S(1)}, bf16[96,512]{1,0:T(8,128)(2,1)S(1)}, u32[]{:S(2)}, u32[]{:S(2)}) collective-permute-start(bf16[96,512]{1,0:T(8,128)(2,1)S(1)} %get-tuple-element.39), channel_id=1, source_target_pairs={{0,8},{1,2},{2,1},{3,4},{4,3},{5,6},{6,5},{7,15},{8,0},{9,10},{10,... | collective-permute-start | bytes 294920 | tf_op jit(solution)/shard_map/ppermute | solution.py:336
  11.2 4.4 %copy-start.9 = (f32[87,512]{1,0:T(8,128)S(1)}, f32[87,512]{1,0:T(8,128)}, u32[]{:S(2)}) copy-start(f32[87,512]{1,0:T(8,128)} %refs_7_.7) | copy-start | bytes 534532
  11.2 4.4 %copy-start.10 = (f32[87,512]{1,0:T(8,128)S(1)}, f32[87,512]{1,0:T(8,128)}, u32[]{:S(2)}) copy-start(f32[87,512]{1,0:T(8,128)} %refs_8_.5) | copy-start | bytes 534532
  11.2 4.4 %copy-start.11 = (bf16[87,512]{1,0:T(8,128)(2,1)S(1)}, bf16[87,512]{1,0:T(8,128)(2,1)}, u32[]{:S(2)}) copy-start(bf16[87,512]{1,0:T(8,128)(2,1)} %refs_6_.1) | copy-start | bytes 267268
  15.7 9.6 %copy-start.15 = (f32[512]{0:T(512)S(1)}, f32[512]{0:T(512)}, u32[]{:S(2)}) copy-start(f32[512]{0:T(512)} %param.32) | copy-start | bytes 6148
  15.7 9.6 %copy-start.17 = (f32[87]{0:T(128)S(1)}, f32[87]{0:T(128)}, u32[]{:S(2)}) copy-start(f32[87]{0:T(128)} %param.31) | copy-start | bytes 1048
  17.9 4.4 %collective-permute-start.5 = (bf16[87,512]{1,0:T(8,128)(2,1)S(1)}, bf16[87,512]{1,0:T(8,128)(2,1)S(1)}, u32[]{:S(2)}, u32[]{:S(2)}) collective-permute-start(bf16[87,512]{1,0:T(8,128)(2,1)S(1)} %get-tuple-element.42), channel_id=1, source_target_pairs={{0,16},{8,24},{16,0},{24,8},{1,17},{9,25},{17,1},{25,9},{2,18},{10... | collective-permute-start | bytes 267272 | tf_op jit(solution)/shard_map/ppermute | solution.py:348
  19.2 6.1 %collective-permute-start.4 = (bf16[87,512]{1,0:T(8,128)(2,1)S(1)}, bf16[87,512]{1,0:T(8,128)(2,1)S(1)}, u32[]{:S(2)}, u32[]{:S(2)}) collective-permute-start(bf16[87,512]{1,0:T(8,128)(2,1)S(1)} %get-tuple-element.42), channel_id=1, source_target_pairs={{0,8},{8,0},{16,24},{24,16},{1,9},{9,1},{17,25},{25,17},{2,10},{10... | collective-permute-start | bytes 267272 | tf_op jit(solution)/shard_map/ppermute | solution.py:342
  22.3 3.9 %collective-permute-start.6 = (bf16[87,512]{1,0:T(8,128)(2,1)S(1)}, bf16[87,512]{1,0:T(8,128)(2,1)S(1)}, u32[]{:S(2)}, u32[]{:S(2)}) collective-permute-start(bf16[87,512]{1,0:T(8,128)(2,1)S(1)} %collective-permute-done.5.refs_1_), channel_id=1, source_target_pairs={{0,8},{8,0},{16,24},{24,16},{1,9},{9,1},{17,25},{25,17},{2,10},{10... | collective-permute-start | bytes 267272 | tf_op jit(solution)/shard_map/ppermute | solution.py:342
